TPU v7x, 512 devices: a whole 4x8x8 slice. The times are simulated.
512 devices in a mesh: dp: 4 (over y_lo, core), space: 128 (over z, x, y_hi).
Axes of the slice: x: 4, y: 8 (y_hi: 4, y_lo: 2; y = y_hi * 2 + y_lo), z: 8, core: 2. Of those that a mesh axis runs over, the one named last changes fastest.
Arguments:
- volume: bfloat16 [4, 256, 32, 48, 64], P('dp', 'space'), may hold values from -6 to 6
- cotangent: bfloat16 [4, 128, 16, 24, 256], P('dp', 'space'), may hold values from -6 to 6
- w_first: bfloat16 [3, 3, 3, 64, 128], replicated, may hold values from -0.15625 to 0.15625
- w_second: bfloat16 [3, 3, 3, 16, 256], replicated, may hold values from -0.3125 to 0.3125
Outputs:
- grad_input: bfloat16 [4, 256, 32, 48, 64], P('dp', 'space')
- grad_first: float32 [3, 3, 3, 64, 128], replicated
- grad_second: float32 [3, 3, 3, 16, 256], replicated
All inputs are finite; a program needn't handle non-finite values.
Results may differ from a plain program's by a relative error of at most 0.0057.
Values may be sent and summed in bfloat16 or wider, within the bound.
No kernel may reach another device: no remote copies, remote signals or barrier semaphores. Data moves between devices by JAX's collectives and lax.ppermute only.
A program may use at most 64 MiB of HBM per device.

v0:
```python
import jax
import jax.numpy as jnp
from jax import lax
from jax.sharding import PartitionSpec as P

GROUPS = 8


layout_names = ("NDHWC", "DHWIO", "NDHWC")


def shifted(array, axis, by):
    size = lax.axis_size(axis)
    pairs = [(i, i + by) for i in range(size) if 0 <= i + by < size]
    return lax.ppermute(array, axis, pairs)


def strided_conv(inputs, weights):
    return lax.conv_general_dilated(
        inputs,
        weights,
        (2, 2, 2),
        ((0, 0), (1, 0), (1, 0)),
        dimension_numbers=layout_names,
        preferred_element_type=jnp.float32,
    )


def flipped(weights, groups):
    in_width = weights.shape[3]
    out_width = weights.shape[4] // groups
    turned = weights[::-1, ::-1, ::-1].reshape(3, 3, 3, in_width, groups, out_width)
    return turned.transpose(0, 1, 2, 5, 4, 3).reshape(3, 3, 3, out_width, groups * in_width)


def back_conv(upstream, weights, dilation, pads, groups):
    return lax.conv_general_dilated(
        upstream,
        flipped(weights, groups),
        (1, 1, 1),
        pads,
        lhs_dilation=dilation,
        dimension_numbers=layout_names,
        feature_group_count=groups,
        preferred_element_type=jnp.float32,
    )


def tap_grad(inputs, upstream, stride, pads, groups):
    padded = jnp.pad(inputs, ((0, 0),) + pads + ((0, 0),))
    out_depth, out_rows, out_cols = (upstream.shape[1], upstream.shape[2], upstream.shape[3])
    in_lanes = inputs.shape[4] // groups
    out_lanes = upstream.shape[4] // groups
    shaped_up = upstream.reshape(upstream.shape[:4] + (groups, out_lanes))
    tap_list = []
    for depth_tap in range(3):
        for row_tap in range(3):
            for col_tap in range(3):
                starts = (0, depth_tap, row_tap, col_tap, 0)
                limits = (
                    padded.shape[0],
                    depth_tap + (out_depth - 1) * stride + 1,
                    row_tap + (out_rows - 1) * stride + 1,
                    col_tap + (out_cols - 1) * stride + 1,
                    padded.shape[4],
                )
                window = lax.slice(padded, starts, limits, (1, stride, stride, stride, 1))
                window = window.reshape(window.shape[:4] + (groups, in_lanes))
                term = jnp.einsum(
                    "ndhwgi,ndhwgo->igo", window, shaped_up, preferred_element_type=jnp.float32
                )
                tap_list.append(term.reshape(in_lanes, groups * out_lanes))
    return jnp.stack(tap_list).reshape(3, 3, 3, in_lanes, groups * out_lanes)


def to_groups(tensor, blocks, width):
    planes = tensor.shape[1]
    rows = tensor.shape[2] // blocks
    columns = tensor.shape[3]
    shaped = tensor.reshape(planes, blocks, rows, columns, GROUPS, width)
    return shaped.transpose(1, 4, 0, 2, 3, 5).reshape(blocks * GROUPS, planes, rows, columns, width)


def group_section(hidden, cotangent, w_second):
    devices = lax.axis_size("space")
    blocks = devices // GROUPS
    in_width = hidden.shape[4] // GROUPS
    out_width = cotangent.shape[4] // GROUPS
    planes = hidden.shape[1]
    rows = hidden.shape[2] // blocks
    columns = hidden.shape[3]
    grouped, grouped_cot = (
        lax.all_to_all(
            to_groups(hidden, blocks, in_width), "space", split_axis=0, concat_axis=1, tiled=True
        ),
        lax.all_to_all(
            to_groups(cotangent, blocks, out_width),
            "space",
            split_axis=0,
            concat_axis=1,
            tiled=True,
        ),
    )
    position = lax.axis_index("space")
    group = position % GROUPS
    below, below_cot = shifted(
        (grouped[:, :, rows - 1 :], grouped_cot[:, :, rows - 1 :]), "space", GROUPS
    )
    above, above_cot = shifted((grouped[:, :, :1], grouped_cot), "space", -GROUPS)
    rimmed = jnp.concatenate([below, grouped, above], axis=2)
    rimmed_cot = jnp.concatenate([below_cot, grouped_cot, above_cot], axis=2)
    own_weights = lax.dynamic_slice_in_dim(w_second, group * out_width, out_width, 4)
    part_grad = tap_grad(rimmed, grouped_cot, 1, ((1, 1), (0, 0), (1, 1)), 1)
    full_grad = lax.dynamic_update_slice_in_dim(
        jnp.zeros(w_second.shape, jnp.float32), part_grad, group * out_width, 4
    )
    backward = back_conv(rimmed_cot, own_weights, (1, 1, 1), ((1, 1), (2, 2), (1, 1)), 1)
    local_grad = backward[:, :, 2 : rows + 2].astype(jnp.bfloat16)
    returned = lax.all_to_all(
        local_grad.reshape(1, devices, planes, rows, columns, in_width),
        "space",
        split_axis=1,
        concat_axis=0,
        tiled=True,
    )
    regrouped = returned.reshape(blocks, GROUPS, planes, rows, columns, in_width).transpose(
        2, 0, 3, 4, 1, 5
    )
    return (regrouped.reshape(1, planes, blocks * rows, columns, GROUPS * in_width), full_grad)


def on_device(volume, cotangent, w_first, w_second):
    depth = volume.shape[1]
    lower = shifted(volume[:, depth - 1 :], "space", 1)
    padded = jnp.concatenate([lower, volume], axis=1)
    pre = strided_conv(padded, w_first)
    hidden = jax.nn.silu(pre).astype(jnp.bfloat16)
    grad_hidden, second_terms = group_section(hidden, cotangent, w_second)
    sigma = jax.nn.sigmoid(pre)
    grad_pre = (grad_hidden.astype(jnp.float32) * sigma * (1.0 + pre * (1.0 - sigma))).astype(
        jnp.bfloat16
    )
    upper = shifted(grad_pre[:, :1], "space", -1)
    first_terms = tap_grad(padded, grad_pre, 2, ((0, 0), (1, 0), (1, 0)), 1)
    extended = jnp.concatenate([grad_pre, upper], axis=1)
    backward = back_conv(extended, w_first, (2, 2, 2), ((2, 2), (1, 2), (1, 2)), 1)
    grad_input = backward[:, 1 : depth + 1].astype(jnp.bfloat16)
    sum_first, sum_second = lax.psum((first_terms, second_terms), ("dp", "space"))
    count = (
        volume.shape[0]
        * lax.axis_size("dp")
        * pre.shape[1]
        * lax.axis_size("space")
        * pre.shape[2]
        * pre.shape[3]
    )
    scale = float(count) ** (-0.5)
    return (grad_input, sum_first * scale, sum_second * scale)


def solution(mesh):
    placed = (P("dp", "space", None, None, None), P("dp", "space", None, None, None), P(), P())
    return jax.shard_map(
        on_device,
        mesh=mesh,
        in_specs=placed,
        out_specs=(P("dp", "space", None, None, None), P(), P()),
        check_vma=False,
    )
```

profile of v0, /device:TPU:1, one launch (start us, length us, event | category | flops | bytes accessed | tf_op | source)
XLA Modules:
  0.0 565.6 jit_solution(13641238648373466001)
XLA Ops:
  8.3 5.1 collective-permute-start.2
  13.4 8.0 %collective-permute-done.2 = bf16[1,1,32,48,64]{4,3,2,1,0:T(8,128)(2,1)S(1)} collective-permute-done((bf16[1,1,32,48,64]{4,3,2,1,0:T(8,128)(2,1)S(1)}, bf16[1,1,32,48,64]{4,3,2,1,0:T(8,128)(2,1)S(1)}, u32[]{:S(2)}, u32[]{:S(2)}) %collective-permute-start.2) | collective-permute-done | bytes 196640 | tf_op jit(solution)/shard_map/ppermute | solution.py:15
  23.1 1.6 multiply_convert_fusion
  25.8 1.2 reshape.680
  27.0 30.2 %all-to-all-start.2 = ((bf16[128,2,192]{2,1,0:T(2,128)(2,1)}), bf16[128,2,192]{2,1,0:T(2,128)(2,1)S(1)}, u32[]{:S(2)}, u32[]{:S(2)}) async-start(bf16[128,2,192]{2,1,0:T(2,128)(2,1)} %reshape.680), calls=%async_computation.2 | async-start | bytes 262144 | tf_op jit(solution)/shard_map/all_to_all | solution.py:93
  57.8 1.3 reshape.676
  59.1 11.9 %all-to-all-done.2 = bf16[128,2,192]{2,1,0:T(2,128)(2,1)S(1)} async-done(((bf16[128,2,192]{2,1,0:T(2,128)(2,1)}), bf16[128,2,192]{2,1,0:T(2,128)(2,1)S(1)}, u32[]{:S(2)}, u32[]{:S(2)}) %all-to-all-start.2) | async-done | bytes 98336 | tf_op jit(solution)/shard_map/all_to_all | solution.py:93
  70.9 6.2 %all-to-all-start = ((bf16[128,2,384]{2,1,0:T(2,128)(2,1)}), bf16[128,2,384]{2,1,0:T(2,128)(2,1)S(1)}, u32[]{:S(2)}, u32[]{:S(2)}) async-start(bf16[128,2,384]{2,1,0:T(2,128)(2,1)} %reshape.676), calls=%async_computation | async-start | bytes 393216 | tf_op jit(solution)/shard_map/all_to_all | solution.py:96
  78.0 4.6 collective-permute-start.4
  82.6 1.5 collective-permute-start.5
  85.4 4.9 slice.198
  90.3 4.9 slice.199
  95.2 4.9 slice.200
  100.1 4.9 slice.201
  105.0 4.9 slice.202
  109.9 4.9 slice.203
  114.9 5.0 slice.204
  119.8 4.9 slice.205
  124.8 5.0 slice.206
  129.8 4.9 slice.207
  134.6 4.9 slice.208
  139.6 4.9 slice.209
  144.5 4.9 slice.210
  149.4 4.9 slice.211
  154.3 4.9 slice.212
  159.2 4.9 slice.213
  164.2 5.0 slice.214
  169.1 5.0 slice.215
  174.1 4.9 slice.216
  179.0 4.9 slice.217
  183.9 4.9 slice.218
  188.8 4.9 slice.219
  193.8 4.9 slice.220
  202.8 5.5 collective-permute-start
  208.3 1.3 collective-permute-start.1
  209.6 1.3 select_maximum_fusion
  219.1 4.4 copy.82
  223.5 5.9 %fusion = bf16[128,1,8,4,16]{4,2,3,1,0:T(8,128)(2,1)S(1)} fusion(bf16[128,3,1,8,6,32]{5,3,4,1,0,2:T(8,128)(2,1)} %copy.82, bf16[3,3,3,16,32]{4,3,2,1,0:T(8,128)(2,1)S(1)} %copy-done.30), kind=kOutput, calls=%fused_computation | convolution fusion | flops 112656384 | bytes 1338368 | tf_op jit(solution)/shard_map/slice | solution.py:118
  231.1 1.2 reshape.678
  232.3 19.2 %all-to-all-start.1 = ((bf16[128,2,192]{2,1,0:T(2,128)(2,1)}), bf16[128,2,192]{2,1,0:T(2,128)(2,1)S(1)}, u32[]{:S(2)}, u32[]{:S(2)}) async-start(bf16[128,2,192]{2,1,0:T(2,128)(2,1)} %reshape.678), calls=%async_computation.1 | async-start | bytes 262144 | tf_op jit(solution)/shard_map/all_to_all | solution.py:119
  252.8 12.1 %all-to-all-done.1 = bf16[128,2,192]{2,1,0:T(2,128)(2,1)S(1)} async-done(((bf16[128,2,192]{2,1,0:T(2,128)(2,1)}), bf16[128,2,192]{2,1,0:T(2,128)(2,1)S(1)}, u32[]{:S(2)}, u32[]{:S(2)}) %all-to-all-start.1) | async-done | bytes 98336 | tf_op jit(solution)/shard_map/all_to_all | solution.py:119
  266.0 1.4 collective-permute-start.3
  267.6 1.1 fusion.43
  268.8 1.1 fusion.42
  269.9 1.1 fusion.41
  272.2 1.1 fusion.39
  281.8 273.9 %all-reduce.5.cloned.1.call-done = (f32[3,3,3,64,128]{4,3,2,1,0:T(8,128)}, f32[3,3,3,16,256]{4,3,2,1,0:T(8,128)}) async-done(((f32[3,3,3,64,128]{4,3,2,1,0:T(8,128)}, f32[3,3,3,16,256]{4,3,2,1,0:T(8,128)}), (f32[3,3,3,64,128]{4,3,2,1,0:T(8,128)}, f32[3,3,3,16,256]{4,3,2,1,0:T(8,128)})) %all-reduce.5.cloned.1.call-update) | async-done | bytes 1327120 | tf_op jit(solution)/shard_map/psum | solution.py:148
  555.7 2.3 broadcast_multiply_fusion
  (178 shorter events, 32.8 us)
Async XLA Ops:
  7.2 76.9 %copy-start = (bf16[3,3,3,16,256]{4,3,2,1,0:T(8,128)(2,1)S(1)}, bf16[3,3,3,16,256]{4,3,2,1,0:T(8,128)(2,1)}, u32[]{:S(2)}) copy-start(bf16[3,3,3,16,256]{4,3,2,1,0:T(8,128)(2,1)} %param.7) | copy-start | bytes 663556
  7.2 14.2 %copy-start.1 = (bf16[1,2,32,48,64]{4,3,2,1,0:T(8,128)(2,1)S(1)}, bf16[1,2,32,48,64]{4,3,2,1,0:T(8,128)(2,1)}, u32[]{:S(2)}) copy-start(bf16[1,2,32,48,64]{4,3,2,1,0:T(8,128)(2,1)} %param.4) | copy-start | bytes 1179652
  8.3 13.0 %collective-permute-start.2 = (bf16[1,1,32,48,64]{4,3,2,1,0:T(8,128)(2,1)S(1)}, bf16[1,1,32,48,64]{4,3,2,1,0:T(8,128)(2,1)S(1)}, u32[]{:S(2)}, u32[]{:S(2)}) collective-permute-start(bf16[1,1,32,48,64]{4,3,2,1,0:T(8,128)(2,1)S(1)} %slice.196), channel_id=1, source_target_pairs={{0,1},{1,2},{2,3},{3,4},{4,5},{5,6},{6,7},{7,8},{8,9},{9,10},{10,1... | collective-permute-start | bytes 589832 | tf_op jit(solution)/shard_map/ppermute | solution.py:15
  22.1 1.0 copy-start.4
  22.1 1.0 copy-start.33
  24.8 32.5 %copy-start.29 = (bf16[1,1,16,24,256]{4,3,2,1,0:T(8,128)(2,1)S(1)}, bf16[1,1,16,24,256]{4,3,2,1,0:T(8,128)(2,1)}, u32[]{:S(2)}) copy-start(bf16[1,1,16,24,256]{4,3,2,1,0:T(8,128)(2,1)} %param.5) | copy-start | bytes 589828
  27.0 43.9 %all-to-all-start.2 = ((bf16[128,2,192]{2,1,0:T(2,128)(2,1)}), bf16[128,2,192]{2,1,0:T(2,128)(2,1)S(1)}, u32[]{:S(2)}, u32[]{:S(2)}) async-start(bf16[128,2,192]{2,1,0:T(2,128)(2,1)} %reshape.680), calls=%async_computation.2 | async-start | bytes 262144 | tf_op jit(solution)/shard_map/all_to_all | solution.py:93
  70.9 131.0 %all-to-all-start = ((bf16[128,2,384]{2,1,0:T(2,128)(2,1)}), bf16[128,2,384]{2,1,0:T(2,128)(2,1)S(1)}, u32[]{:S(2)}, u32[]{:S(2)}) async-start(bf16[128,2,384]{2,1,0:T(2,128)(2,1)} %reshape.676), calls=%async_computation | async-start | bytes 393216 | tf_op jit(solution)/shard_map/all_to_all | solution.py:96
  78.0 131.6 %collective-permute-start.4 = (bf16[1,128,1,24,16]{1,4,3,2,0:T(8,128)(2,1)S(1)}, bf16[1,128,1,24,16]{1,4,3,2,0:T(8,128)(2,1)}, u32[]{:S(2)}, u32[]{:S(2)}) collective-permute-start(bf16[1,128,1,24,16]{1,4,3,2,0:T(8,128)(2,1)S(1)} %bitcast.945), channel_id=1, source_target_pairs={{0,8},{1,9},{2,10},{3,11},{4,12},{5,13},{6,14},{7,15},{8,16},{9,17... | collective-permute-start | bytes 294920 | tf_op jit(solution)/shard_map/ppermute | solution.py:15
  82.6 127.0 %collective-permute-start.5 = (bf16[1,128,1,24,16]{1,4,3,2,0:T(8,128)(2,1)S(1)}, bf16[1,128,1,24,16]{1,4,3,2,0:T(8,128)(2,1)}, u32[]{:S(2)}, u32[]{:S(2)}) collective-permute-start(bf16[1,128,1,24,16]{1,4,3,2,0:T(8,128)(2,1)S(1)} %bitcast.946), channel_id=1, source_target_pairs={{8,0},{9,1},{10,2},{11,3},{12,4},{13,5},{14,6},{15,7},{16,8},{17,9... | collective-permute-start | bytes 294920 | tf_op jit(solution)/shard_map/ppermute | solution.py:15
  139.6 62.0 %copy-start.26 = (f32[1,16,8,4,128]{4,2,3,1,0:T(8,128)S(1)}, f32[1,16,8,4,128]{4,2,3,1,0:T(8,128)}, u32[]{:S(2)}) copy-start(f32[1,16,8,4,128]{4,2,3,1,0:T(8,128)} %get-tuple-element.7) | copy-start | bytes 786436
  164.2 37.6 %copy-start.25 = (f32[1,16,8,4,128]{4,2,3,1,0:T(8,128)S(1)}, f32[1,16,8,4,128]{4,2,3,1,0:T(8,128)}, u32[]{:S(2)}) copy-start(f32[1,16,8,4,128]{4,2,3,1,0:T(8,128)} %get-tuple-element.6) | copy-start | bytes 786436
  202.8 15.4 %collective-permute-start = (bf16[1,128,1,24,32]{1,4,3,2,0:T(8,128)(2,1)S(1)}, bf16[1,128,1,24,32]{1,4,3,2,0:T(8,128)(2,1)S(1)}, u32[]{:S(2)}, u32[]{:S(2)}) collective-permute-start(bf16[1,128,1,24,32]{1,4,3,2,0:T(8,128)(2,1)S(1)} %bitcast.929), channel_id=1, source_target_pairs={{0,8},{1,9},{2,10},{3,11},{4,12},{5,13},{6,14},{7,15},{8,16},{9,17... | collective-permute-start | bytes 589832 | tf_op jit(solution)/shard_map/ppermute | solution.py:15
  208.3 9.9 %collective-permute-start.1 = (bf16[1,128,1,24,32]{1,4,3,2,0:T(8,128)(2,1)S(1)}, bf16[1,128,1,24,32]{1,4,3,2,0:T(8,128)(2,1)S(1)}, u32[]{:S(2)}, u32[]{:S(2)}) collective-permute-start(bf16[1,128,1,24,32]{1,4,3,2,0:T(8,128)(2,1)S(1)} %bitcast.930), channel_id=1, source_target_pairs={{8,0},{9,1},{10,2},{11,3},{12,4},{13,5},{14,6},{15,7},{16,8},{17,9... | collective-permute-start | bytes 589832 | tf_op jit(solution)/shard_map/ppermute | solution.py:15
  218.2 0.7 copy-start.27
  219.1 4.4 copy-start.30
  223.5 7.0 %copy-start.31 = (pred[8,4]{1,0:T(8,128)(4,1)S(1)}, pred[8,4]{1,0:T(8,128)(4,1)}, u32[]{:S(2)}) copy-start(pred[8,4]{1,0:T(8,128)(4,1)} %constant.52) | copy-start | bytes 100
  229.5 22.4 %copy-start.28 = (f32[27,16,32]{2,1,0:T(8,128)S(1)}, f32[27,16,32]{2,1,0:T(8,128)}, u32[]{:S(2)}) copy-start(f32[27,16,32]{2,1,0:T(8,128)} %copy-done.27) | copy-start | bytes 165892
  232.3 32.6 %all-to-all-start.1 = ((bf16[128,2,192]{2,1,0:T(2,128)(2,1)}), bf16[128,2,192]{2,1,0:T(2,128)(2,1)S(1)}, u32[]{:S(2)}, u32[]{:S(2)}) async-start(bf16[128,2,192]{2,1,0:T(2,128)(2,1)} %reshape.678), calls=%async_computation.1 | async-start | bytes 262144 | tf_op jit(solution)/shard_map/all_to_all | solution.py:119
  251.5 304.2 %all-reduce.5.cloned.1.call-start = ((), (), s32[]{:S(2)}) async-start(), calls=%async_computation.3 | async-start | bytes 2654208 | tf_op jit(solution)/shard_map/psum | solution.py:148
  252.7 13.0 %copy-start.2 = (f32[3,3,3,16,256]{4,3,2,1,0:T(8,128)}, f32[3,3,3,16,256]{4,3,2,1,0:T(8,128)S(1)}, u32[]{:S(2)}) copy-start(f32[3,3,3,16,256]{4,3,2,1,0:T(8,128)S(1)} %dynamic_update_slice.3) | copy-start | bytes 1327108
  265.4 2.0 copy-start.24
  265.4 7.9 %copy-start.23 = (bf16[1,1,16,24,64]{4,3,2,1,0:T(8,128)(2,1)S(1)}, bf16[1,1,16,24,64]{4,3,2,1,0:T(8,128)(2,1)}, u32[]{:S(2)}) copy-start(bf16[1,1,16,24,64]{4,3,2,1,0:T(8,128)(2,1)} %slice.204) | copy-start | bytes 147460
  265.4 8.1 %copy-start.22 = (bf16[1,1,16,24,64]{4,3,2,1,0:T(8,128)(2,1)S(1)}, bf16[1,1,16,24,64]{4,3,2,1,0:T(8,128)(2,1)}, u32[]{:S(2)}) copy-start(bf16[1,1,16,24,64]{4,3,2,1,0:T(8,128)(2,1)} %slice.205) | copy-start | bytes 147460
  265.8 8.0 %copy-start.21 = (bf16[1,1,16,24,64]{4,3,2,1,0:T(8,128)(2,1)S(1)}, bf16[1,1,16,24,64]{4,3,2,1,0:T(8,128)(2,1)}, u32[]{:S(2)}) copy-start(bf16[1,1,16,24,64]{4,3,2,1,0:T(8,128)(2,1)} %slice.206) | copy-start | bytes 147460
  265.8 8.2 %copy-start.20 = (bf16[1,1,16,24,64]{4,3,2,1,0:T(8,128)(2,1)S(1)}, bf16[1,1,16,24,64]{4,3,2,1,0:T(8,128)(2,1)}, u32[]{:S(2)}) copy-start(bf16[1,1,16,24,64]{4,3,2,1,0:T(8,128)(2,1)} %slice.207) | copy-start | bytes 147460
  265.8 8.4 %copy-start.19 = (bf16[1,1,16,24,64]{4,3,2,1,0:T(8,128)(2,1)S(1)}, bf16[1,1,16,24,64]{4,3,2,1,0:T(8,128)(2,1)}, u32[]{:S(2)}) copy-start(bf16[1,1,16,24,64]{4,3,2,1,0:T(8,128)(2,1)} %slice.208) | copy-start | bytes 147460
  265.8 8.6 %copy-start.18 = (bf16[1,1,16,24,64]{4,3,2,1,0:T(8,128)(2,1)S(1)}, bf16[1,1,16,24,64]{4,3,2,1,0:T(8,128)(2,1)}, u32[]{:S(2)}) copy-start(bf16[1,1,16,24,64]{4,3,2,1,0:T(8,128)(2,1)} %slice.209) | copy-start | bytes 147460
  265.8 8.8 %copy-start.17 = (bf16[1,1,16,24,64]{4,3,2,1,0:T(8,128)(2,1)S(1)}, bf16[1,1,16,24,64]{4,3,2,1,0:T(8,128)(2,1)}, u32[]{:S(2)}) copy-start(bf16[1,1,16,24,64]{4,3,2,1,0:T(8,128)(2,1)} %slice.210) | copy-start | bytes 147460
  265.9 8.9 %copy-start.16 = (bf16[1,1,16,24,64]{4,3,2,1,0:T(8,128)(2,1)S(1)}, bf16[1,1,16,24,64]{4,3,2,1,0:T(8,128)(2,1)}, u32[]{:S(2)}) copy-start(bf16[1,1,16,24,64]{4,3,2,1,0:T(8,128)(2,1)} %slice.211) | copy-start | bytes 147460
  265.9 9.1 %copy-start.15 = (bf16[1,1,16,24,64]{4,3,2,1,0:T(8,128)(2,1)S(1)}, bf16[1,1,16,24,64]{4,3,2,1,0:T(8,128)(2,1)}, u32[]{:S(2)}) copy-start(bf16[1,1,16,24,64]{4,3,2,1,0:T(8,128)(2,1)} %slice.212) | copy-start | bytes 147460
  266.0 12.9 %collective-permute-start.3 = (bf16[1,1,16,24,128]{4,3,2,1,0:T(8,128)(2,1)S(1)}, bf16[1,1,16,24,128]{4,3,2,1,0:T(8,128)(2,1)S(1)}, u32[]{:S(2)}, u32[]{:S(2)}) collective-permute-start(bf16[1,1,16,24,128]{4,3,2,1,0:T(8,128)(2,1)S(1)} %fusion.85), channel_id=1, source_target_pairs={{1,0},{2,1},{3,2},{4,3},{5,4},{6,5},{7,6},{8,7},{9,8},{10,9},{11,1... | collective-permute-start | bytes 294920 | tf_op jit(solution)/shard_map/ppermute | solution.py:15
  267.6 7.7 %copy-start.14 = (bf16[1,1,16,24,64]{4,3,2,1,0:T(8,128)(2,1)S(1)}, bf16[1,1,16,24,64]{4,3,2,1,0:T(8,128)(2,1)}, u32[]{:S(2)}) copy-start(bf16[1,1,16,24,64]{4,3,2,1,0:T(8,128)(2,1)} %slice.213) | copy-start | bytes 147460
  268.7 6.8 %copy-start.13 = (bf16[1,1,16,24,64]{4,3,2,1,0:T(8,128)(2,1)S(1)}, bf16[1,1,16,24,64]{4,3,2,1,0:T(8,128)(2,1)}, u32[]{:S(2)}) copy-start(bf16[1,1,16,24,64]{4,3,2,1,0:T(8,128)(2,1)} %slice.214) | copy-start | bytes 147460
  269.9 5.8 %copy-start.12 = (bf16[1,1,16,24,64]{4,3,2,1,0:T(8,128)(2,1)S(1)}, bf16[1,1,16,24,64]{4,3,2,1,0:T(8,128)(2,1)}, u32[]{:S(2)}) copy-start(bf16[1,1,16,24,64]{4,3,2,1,0:T(8,128)(2,1)} %slice.215) | copy-start | bytes 147460
  271.0 4.9 copy-start.11
  272.2 4.0 copy-start.10
  273.3 3.0 copy-start.9
  273.6 3.0 copy-start.8
  273.8 3.0 copy-start.7
  276.1 2.6 copy-start.5
  277.8 0.9 copy-start.3
  278.8 0.7 copy-start.32
  555.7 2.3 copy-start.6
Sparse Core Ops, SparseCore 0:
  278.9 276.7 all-reduce.4
where the time goes:
time: 567 us; the launch traced here: 566 us
  waiting for transfers between devices  306 us (54%)
  local copies, waits for them, and re-layouts  138 us (24%)
  starting transfers between devices  75.2 us (13%)
  matrix products  26.1 us (5%)
  between operations  15.2 us (3%)
    psum x1, waiting for transfers between devices, on_device(): lax.psum((first_terms, second_terms), ('dp', 'space'))  274 us
    slice x27, local copies, waits for them, and re-layouts, tap_grad(): window = lax.slice(padded, starts, limits, (1, stride, stride, stride, 1))  116 us
    all_to_all x1, starting transfers between devices, group_section(): lax.all_to_all(to_groups(hidden, blocks, in_width), 'space', split_axis=0...  30.2 us
    ppermute x6, starting transfers between devices, shifted(): return lax.ppermute(array, axis, pairs)  19.3 us
    all_to_all x1, starting transfers between devices, group_section(): lax.all_to_all(local_grad.reshape(1, devices, planes, rows, columns, in_w...  19.2 us
    dot_general x54, matrix products, tap_grad(): jnp.einsum('ndhwgi,ndhwgo->igo', window, shaped_up, preferred_element_typ...  17.4 us
    all_to_all x1, waiting for transfers between devices, group_section(): lax.all_to_all(local_grad.reshape(1, devices, planes, rows, columns, in_w...  12.1 us
    all_to_all x1, waiting for transfers between devices, group_section(): lax.all_to_all(to_groups(hidden, blocks, in_width), 'space', split_axis=0...  11.9 us
  transfers between devices with their start and end apart: 10, of which 4 were waited for; matrix products, arithmetic and copies ran while one was open for 25% of the time, Pallas kernels for 0%

commit v1 on v0

v1 whole, which is shorter than its diff:
```python
import jax
import jax.numpy as jnp
from jax import lax
from jax.experimental import pallas as pl
from jax.experimental.pallas import tpu as pltpu
from jax.sharding import PartitionSpec as P

GROUPS = 8
PAD = 32
F32 = jnp.float32
BF16 = jnp.bfloat16

NT = (((1,), (1,)), ((), ()))
NN = (((1,), (0,)), ((), ()))
TN = (((0,), (0,)), ((), ()))


def dot(a, b, dims):
    return lax.dot_general(a, b, dims, preferred_element_type=F32)


def vmem(n):
    return [pl.BlockSpec(memory_space=pltpu.VMEM)] * n


def shifted(array, by):
    size = lax.axis_size("space")
    pairs = [(i, i + by) for i in range(size) if 0 <= i + by < size]
    return lax.ppermute(array, "space", pairs)


def pair_kernel(vol, out, tmp):
    planes, rows, cols, chans = vol.shape
    step = tmp.shape[0]
    low = lax.broadcasted_iota(jnp.int32, (step, cols // 2, 2 * chans), 2) < chans

    def body(i, carry):
        p = i // (rows // step)
        r = (i % (rows // step)) * step
        tmp[:, :, 0:chans] = vol[p, pl.ds(r, step)].astype(F32)
        even = tmp[:, pl.ds(0, cols // 2, 2), :]
        odd = pltpu.roll(tmp[:, pl.ds(1, cols // 2, 2), :], chans, 2)
        out[p, pl.ds(r, step)] = jnp.where(low, even, odd).astype(BF16)
        return carry

    lax.fori_loop(0, planes * rows // step, body, 0)


def pair_columns(volume):
    planes, rows, cols, chans = volume.shape
    return pl.pallas_call(
        pair_kernel,
        out_shape=jax.ShapeDtypeStruct((planes, rows, cols // 2, 2 * chans), BF16),
        in_specs=vmem(1),
        out_specs=pl.BlockSpec(memory_space=pltpu.VMEM),
        scratch_shapes=[pltpu.VMEM((8, cols, 2 * chans), F32)],
        name="pair_columns",
        cost_estimate=pl.CostEstimate(flops=0, bytes_accessed=2 << 20, transcendentals=0),
    )(volume)


def clear(ref):
    ref[...] = jnp.zeros_like(ref)


def column_mask(shape):
    return (lax.broadcasted_iota(jnp.int32, shape, 0) & (PAD - 1)) < 24


def roll_rows(x, by):
    return pltpu.roll(x, by % x.shape[0], 0)


def group_kernel(cot_lo, cot, cot_hi, w2, gh, cpad, wd, acc):
    h2, w = cot.shape[0], cot.shape[1]
    clear(cpad)
    for p, src in enumerate((cot_lo, cot, cot_hi)):
        cpad[p, 1 : h2 + 1, 0:w] = src[...]
    lane_group = lax.broadcasted_iota(jnp.int32, (128, 256), 1) // 32
    row_group = lax.broadcasted_iota(jnp.int32, (128, 256), 0) // 16
    own = lane_group == row_group
    for tap in range(27):
        spread = jnp.concatenate([w2[tap]] * GROUPS, axis=0)
        wd[tap // 3, (tap % 3) * 128 : (tap % 3) * 128 + 128] = jnp.where(own, spread, 0.0).astype(BF16)
    for kd in range(3):
        for kr in range(3):
            x = cpad[2 - kd, 2 - kr : 2 - kr + h2].reshape(h2 * PAD, 256)
            term = dot(x, wd[kd * 3 + kr], NT)
            if kd + kr == 0:
                acc[...] = term
            else:
                acc[...] += term
    total = roll_rows(acc[:, 0:128], -1) + acc[:, 128:256] + roll_rows(acc[:, 256:384], 1)
    gh[...] = total.astype(BF16)


def group_backward(cot_lo, cot, cot_hi, w2):
    return pl.pallas_call(
        group_kernel,
        out_shape=(
            jax.ShapeDtypeStruct((16 * PAD, 128), BF16),
            jax.ShapeDtypeStruct((3, 18, PAD, 256), BF16),
        ),
        in_specs=vmem(4),
        out_specs=tuple(vmem(2)),
        scratch_shapes=[
            pltpu.VMEM((9, 384, 256), BF16),
            pltpu.VMEM((16 * PAD, 384), F32),
        ],
        name="group_backward",
        cost_estimate=pl.CostEstimate(flops=2 << 30, bytes_accessed=2 << 20, transcendentals=0),
    )(cot_lo, cot, cot_hi, w2)


def middle_kernel(lower, pairs, w1, gh, cpad, gp_out, first, second, even, odd, hid, ups):
    h2, w = 16, pairs.shape[2]
    cells = h2 * PAD
    clear(even)
    clear(odd)
    for p in range(3):
        src = lower if p == 0 else pairs.at[p - 1]
        for r in range(h2):
            even[p, r, 0:w] = src[2 * r]
            odd[p, r + 1, 0:w] = src[2 * r + 1]

    def window(kd, kr):
        if kr == 1:
            return even[kd].reshape(cells, 128)
        if kr == 0:
            return odd[kd, 0:h2].reshape(cells, 128)
        return odd[kd, 1 : h2 + 1].reshape(cells, 128)

    zeros = jnp.zeros((64, 128), BF16)
    total = None
    for kd in range(3):
        for kr in range(3):
            left = jnp.concatenate([w1[kd, kr, 1], w1[kd, kr, 2]], axis=0)
            right = jnp.concatenate([zeros, w1[kd, kr, 0]], axis=0)
            weights = jnp.concatenate([left, right], axis=1)
            term = dot(window(kd, kr), weights, NN)
            total = term if total is None else total + term
    keep = column_mask((cells, 128))
    pre = total[:, 0:128] + roll_rows(total[:, 128:256], 1)
    pre = jnp.where(keep, pre, 0.0)
    s = jax.nn.sigmoid(pre)
    hidden = (pre * s).astype(BF16).astype(F32)
    grad = gh[...].astype(F32) * s * (1.0 + pre * (1.0 - s))
    grad = jnp.where(keep, grad, 0.0).astype(BF16).astype(F32)
    ups[:, 0:128] = grad.astype(BF16)
    ups[:, 128:256] = roll_rows(grad, -1).astype(BF16)
    hid[:, 0:128] = roll_rows(hidden, 1).astype(BF16)
    hid[:, 128:256] = hidden.astype(BF16)
    hid[:, 256:384] = roll_rows(hidden, -1).astype(BF16)
    gp_out[...] = ups[:, 0:128].reshape(h2, PAD, 128)[:, 0:w]
    for kd in range(3):
        for kr in range(3):
            term = dot(window(kd, kr), ups[...], TN)
            first[kd, kr, 0] = term[64:128, 128:256]
            first[kd, kr, 1] = term[0:64, 0:128]
            first[kd, kr, 2] = term[64:128, 0:128]
    lane_group = lax.broadcasted_iota(jnp.int32, (GROUPS, 16, 256), 2) // 32
    own = lane_group == lax.broadcasted_iota(jnp.int32, (GROUPS, 16, 256), 0)
    for kd in range(3):
        for kr in range(3):
            x = cpad[2 - kd, 2 - kr : 2 - kr + h2].reshape(cells, 256)
            term = dot(hid[...], x, TN).reshape(3, GROUPS, 16, 256)
            for kc in range(3):
                second[kd, kr, kc] = jnp.sum(jnp.where(own, term[kc], 0.0), axis=0)


def middle(lower, pairs, w1, gh, cpad):
    return pl.pallas_call(
        middle_kernel,
        out_shape=(
            jax.ShapeDtypeStruct((16, 24, 128), BF16),
            jax.ShapeDtypeStruct((3, 3, 3, 64, 128), F32),
            jax.ShapeDtypeStruct((3, 3, 3, 16, 256), F32),
        ),
        in_specs=vmem(5),
        out_specs=tuple(vmem(3)),
        scratch_shapes=[
            pltpu.VMEM((3, 16, PAD, 128), BF16),
            pltpu.VMEM((3, 17, PAD, 128), BF16),
            pltpu.VMEM((16 * PAD, 384), BF16),
            pltpu.VMEM((16 * PAD, 256), BF16),
        ],
        name="middle",
        cost_estimate=pl.CostEstimate(flops=3 << 30, bytes_accessed=4 << 20, transcendentals=1 << 16),
    )(lower, pairs, w1, gh, cpad)


def input_kernel(gp, upper, w1, out, pad, tmp):
    h2, w = gp.shape[0], gp.shape[1]
    cells = h2 * PAD
    clear(pad)
    pad[0, 0:h2, 0:w] = gp[...]
    pad[1, 0:h2, 0:w] = upper[...]
    zeros = jnp.zeros((64, 128), BF16)
    low = lax.broadcasted_iota(jnp.int32, (cells, 128), 1) < 64
    for par in range(2):
        depth = ((0, 1),) if par == 0 else ((0, 2), (1, 0))
        for row_par in range(2):
            rows = ((0, 1),) if row_par == 0 else ((0, 2), (1, 0))
            total = None
            for plane, kd in depth:
                for start, kr in rows:
                    x = pad[plane, start : start + h2].reshape(cells, 128)
                    weights = jnp.concatenate(
                        [w1[kd, kr, 1], w1[kd, kr, 2], zeros, w1[kd, kr, 0]], axis=0
                    )
                    term = dot(x, weights, NT)
                    total = term if total is None else total + term
            both = total[:, 0:128] + roll_rows(total[:, 128:256], -1)
            turned = pltpu.roll(both, 64, 1)
            both = both.reshape(h2, PAD, 128)
            turned = turned.reshape(h2, PAD, 128)
            for r in range(h2):
                tmp[r % 2, pl.ds(0, w, 2), :] = both[r, 0:w]
                tmp[r % 2, pl.ds(1, w, 2), :] = turned[r, 0:w]
                out[par, 2 * r + row_par] = tmp[r % 2, :, 0:64].astype(BF16)


def input_backward(gp, upper, w1):
    return pl.pallas_call(
        input_kernel,
        out_shape=jax.ShapeDtypeStruct((2, 32, 48, 64), BF16),
        in_specs=vmem(3),
        out_specs=pl.BlockSpec(memory_space=pltpu.VMEM),
        scratch_shapes=[
            pltpu.VMEM((2, 17, PAD, 128), BF16),
            pltpu.VMEM((2, 48, 128), F32),
        ],
        name="input_backward",
        cost_estimate=pl.CostEstimate(flops=1 << 30, bytes_accessed=2 << 20, transcendentals=0),
    )(gp, upper, w1)


def on_device(volume, cotangent, w_first, w_second):
    cot = cotangent[0, 0]
    cot_lo = shifted(cot, 1)
    cot_hi = shifted(cot, -1)
    pairs = pair_columns(volume[0])
    lower = shifted(pairs[1], 1)
    gh, cpad = group_backward(cot_lo, cot, cot_hi, w_second.reshape(27, 16, 256))
    gp, first, second = middle(lower, pairs, w_first, gh, cpad)
    upper = shifted(gp, -1)
    grad_input = input_backward(gp, upper, w_first)
    sum_first, sum_second = lax.psum((first, second), ("dp", "space"))
    count = lax.axis_size("dp") * lax.axis_size("space") * 16 * 24
    scale = float(count) ** (-0.5)
    return (grad_input[None], sum_first * scale, sum_second * scale)


def solution(mesh):
    placed = (P("dp", "space", None, None, None), P("dp", "space", None, None, None), P(), P())
    return jax.shard_map(
        on_device,
        mesh=mesh,
        in_specs=placed,
        out_specs=(P("dp", "space", None, None, None), P(), P()),
        check_vma=False,
    )
```

time: 567 us -> 336 us (0.59)
  local copies, waits for them, and re-layouts: 138 us -> 3.85 us
  starting transfers between devices: 75.2 us -> 13.8 us
  matrix products: 26.1 us -> 0 us
  waiting for transfers between devices: 306 us -> 286 us
  Pallas kernels: 0 us -> 14.9 us
    slice x33 -> x0, local copies, waits for them, and re-layouts: 123 us -> none  [the longest x27 116 us: tap_grad(): window = lax.slice(padded, starts, limits, (1, stride, stride, stride, 1))]
    all_to_all x3 -> x0, starting transfers between devices: 55.6 us -> none  [the longest x1 30.2 us: group_section(): lax.all_to_all(to_groups(hidden, blocks, in_width), 'space', split_axis=0...]
    all_to_all x3 -> x0, waiting for transfers between devices: 24 us -> none  [the longest x1 12.1 us: group_section(): lax.all_to_all(local_grad.reshape(1, devices, planes, rows, columns, in_w...]
    dot_general x54 -> x0, matrix products: 17.4 us -> none  [tap_grad(): jnp.einsum('ndhwgi,ndhwgo->igo', window, shaped_up, preferred_element_typ...]
    pallas_call x0 -> x4, Pallas kernels: none -> 14.9 us  [the longest x1 5.86 us: middle(): pl.pallas_call(middle_kernel, out_shape=(jax.ShapeDtypeStruct((16, 24, 12...]
    slice x2 -> x0, matrix products: 7.01 us -> none  [the longest x1 5.94 us: group_section(): local_grad = backward[:, :, 2:rows + 2].astype(jnp.bfloat16)]
    ppermute x6 -> x4, starting transfers between devices: 19.3 us -> 13.7 us  [shifted(): return lax.ppermute(array, 'space', pairs)]
  transfers between devices with their start and end apart: 10 -> 5, of which waited for: 4 -> 3; matrix products, arithmetic and copies ran while one was open for 25% -> 0% of each run, Pallas kernels for 0% -> 3%
where the time goes in v1:
time: 336 us; the launch traced here: 335 us
  waiting for transfers between devices  286 us (85%)
  Pallas kernels  14.9 us (4%)
  between operations  14.1 us (4%)
  starting transfers between devices  13.8 us (4%)
  local copies, waits for them, and re-layouts  3.85 us (1%)
    psum x1, waiting for transfers between devices, on_device(): sum_first, sum_second = lax.psum((first, second), ('dp', 'space'))  275 us
    ppermute x4, starting transfers between devices, shifted(): return lax.ppermute(array, 'space', pairs)  13.7 us
    ppermute x4, waiting for transfers between devices, shifted(): return lax.ppermute(array, 'space', pairs)  10.2 us
  transfers between devices with their start and end apart: 5, of which 3 were waited for; matrix products, arithmetic and copies ran while one was open for 0% of the time, Pallas kernels for 3%

profile of v1, /device:TPU:1, one launch (start us, length us, event | category | flops | bytes accessed | tf_op | source)
XLA Modules:
  0.0 335.3 jit_solution(17459164677035669713)
XLA Ops:
  7.2 0.0 all-reduce.3.cloned.1.call-start
  7.2 1.3 collective-permute-start.2
  8.5 5.7 %collective-permute-start.1 = (bf16[16,24,256]{2,1,0:T(8,128)(2,1)}, bf16[16,24,256]{2,1,0:T(8,128)(2,1)S(1)}, u32[]{:S(2)}, u32[]{:S(2)}) collective-permute-start(bf16[16,24,256]{2,1,0:T(8,128)(2,1)} %bitcast.9), channel_id=1, source_target_pairs={{0,1},{1,2},{2,3},{3,4},{4,5},{5,6},{6,7},{7,8},{8,9},{9,10},{10,1... | collective-permute-start | bytes 589832 | tf_op jit(solution)/shard_map/ppermute | solution.py:29
  14.2 2.7 pair_columns.1.pairs
  16.9 0.9 slice_bitcast_fusion
  17.8 5.5 %collective-permute-start = (bf16[32,24,128]{2,1,0:T(8,128)(2,1)S(1)}, bf16[32,24,128]{2,1,0:T(8,128)(2,1)S(1)}, u32[]{:S(2)}, u32[]{:S(2)}) collective-permute-start(bf16[32,24,128]{2,1,0:T(8,128)(2,1)S(1)} %slice_bitcast_fusion), channel_id=1, source_target_pairs={{0,1},{1,2},{2,3},{3,4},{4,5},{5,6},{6,7},{7,8},{8,9},{9,10},{10,1... | collective-permute-start | bytes 589832 | tf_op jit(solution)/shard_map/ppermute | solution.py:29
  23.3 0.0 collective-permute-done.2.cot_hi
  23.3 0.0 copy-start.2
  23.3 0.0 collective-permute-done.1.cot_lo
  23.3 0.0 copy-start.3
  23.3 0.7 copy-done.2
  24.0 0.1 copy-done.3
  24.0 3.3 group_backward.1
  27.4 4.3 %collective-permute-done.lower = bf16[32,24,128]{2,1,0:T(8,128)(2,1)S(1)} collective-permute-done((bf16[32,24,128]{2,1,0:T(8,128)(2,1)S(1)}, bf16[32,24,128]{2,1,0:T(8,128)(2,1)S(1)}, u32[]{:S(2)}, u32[]{:S(2)}) %collective-permute-start) | collective-permute-done | bytes 196640 | tf_op jit(solution)/shard_map/ppermute | solution.py:29
  31.7 0.0 copy-start.1
  31.7 0.7 copy-done.1
  32.4 5.9 %middle.1 = (bf16[16,24,128]{2,1,0:T(8,128)(2,1)}, f32[3,3,3,64,128]{4,3,2,1,0:T(8,128)}, f32[3,3,3,16,256]{4,3,2,1,0:T(8,128)}) custom-call(bf16[32,24,128]{2,1,0:T(8,128)(2,1)} %copy-done.1, bf16[2,32,24,128]{3,2,1,0:T(8,128)(2,1)} %pair_columns.1.pairs, bf16[3,3,3,64,128]{4,3,2,1,0:T(8,128)(2,1)} %w1.3, bf16[512,128]{1,0:T(8,128)(2,1)} %get-tuple-element.8.gh, ...), custom_call_target="tpu_custom_call" | custom-call | flops 3221225472 | bytes 4194304 | tf_op jit(solution)/shard_map/middle/pallas_call | solution.py:172
  38.2 0.0 copy-start.4
  38.2 0.0 all-reduce.3.cloned.1.call-update
  38.3 0.9 copy-done.4
  39.1 1.3 collective-permute-start.3
  40.4 5.9 %collective-permute-done.3.upper = bf16[16,24,128]{2,1,0:T(8,128)(2,1)S(1)} collective-permute-done((bf16[16,24,128]{2,1,0:T(8,128)(2,1)S(1)}, bf16[16,24,128]{2,1,0:T(8,128)(2,1)S(1)}, u32[]{:S(2)}, u32[]{:S(2)}) %collective-permute-start.3) | collective-permute-done | bytes 98336 | tf_op jit(solution)/shard_map/ppermute | solution.py:29
  46.3 0.0 copy-start.5
  46.3 0.6 copy-done.5
  46.9 3.1 input_backward.1
  50.0 275.4 %all-reduce.3.cloned.1.call-done = (f32[3,3,3,64,128]{4,3,2,1,0:T(8,128)}, f32[3,3,3,16,256]{4,3,2,1,0:T(8,128)}) async-done(((f32[3,3,3,64,128]{4,3,2,1,0:T(8,128)}, f32[3,3,3,16,256]{4,3,2,1,0:T(8,128)}), (f32[3,3,3,64,128]{4,3,2,1,0:T(8,128)}, f32[3,3,3,16,256]{4,3,2,1,0:T(8,128)})) %all-reduce.3.cloned.1.call-update) | async-done | bytes 1327120 | tf_op jit(solution)/shard_map/psum | solution.py:248
  325.4 0.0 copy-start
  325.4 2.3 broadcast_multiply_fusion
  327.6 0.0 copy-done
  327.6 0.8 broadcast_multiply_fusion.1
Async XLA Ops:
  7.2 318.2 %all-reduce.3.cloned.1.call-start = ((), (), s32[]{:S(2)}) async-start(), calls=%async_computation | async-start | bytes 2654208 | tf_op jit(solution)/shard_map/psum | solution.py:248
  7.2 16.1 %collective-permute-start.2 = (bf16[16,24,256]{2,1,0:T(8,128)(2,1)}, bf16[16,24,256]{2,1,0:T(8,128)(2,1)S(1)}, u32[]{:S(2)}, u32[]{:S(2)}) collective-permute-start(bf16[16,24,256]{2,1,0:T(8,128)(2,1)} %bitcast.8), channel_id=1, source_target_pairs={{1,0},{2,1},{3,2},{4,3},{5,4},{6,5},{7,6},{8,7},{9,8},{10,9},{11,1... | collective-permute-start | bytes 589832 | tf_op jit(solution)/shard_map/ppermute | solution.py:29
  8.5 14.8 %collective-permute-start.1 = (bf16[16,24,256]{2,1,0:T(8,128)(2,1)}, bf16[16,24,256]{2,1,0:T(8,128)(2,1)S(1)}, u32[]{:S(2)}, u32[]{:S(2)}) collective-permute-start(bf16[16,24,256]{2,1,0:T(8,128)(2,1)} %bitcast.9), channel_id=1, source_target_pairs={{0,1},{1,2},{2,3},{3,4},{4,5},{5,6},{6,7},{7,8},{8,9},{9,10},{10,1... | collective-permute-start | bytes 589832 | tf_op jit(solution)/shard_map/ppermute | solution.py:29
  17.8 13.9 %collective-permute-start = (bf16[32,24,128]{2,1,0:T(8,128)(2,1)S(1)}, bf16[32,24,128]{2,1,0:T(8,128)(2,1)S(1)}, u32[]{:S(2)}, u32[]{:S(2)}) collective-permute-start(bf16[32,24,128]{2,1,0:T(8,128)(2,1)S(1)} %slice_bitcast_fusion), channel_id=1, source_target_pairs={{0,1},{1,2},{2,3},{3,4},{4,5},{5,6},{6,7},{7,8},{8,9},{9,10},{10,1... | collective-permute-start | bytes 589832 | tf_op jit(solution)/shard_map/ppermute | solution.py:29
  23.3 0.7 copy-start.2
  23.3 0.7 copy-start.3
  31.7 0.7 copy-start.1
  38.2 0.9 copy-start.4
  39.1 7.2 %collective-permute-start.3 = (bf16[16,24,128]{2,1,0:T(8,128)(2,1)S(1)}, bf16[16,24,128]{2,1,0:T(8,128)(2,1)S(1)}, u32[]{:S(2)}, u32[]{:S(2)}) collective-permute-start(bf16[16,24,128]{2,1,0:T(8,128)(2,1)S(1)} %copy-done.4), channel_id=1, source_target_pairs={{1,0},{2,1},{3,2},{4,3},{5,4},{6,5},{7,6},{8,7},{9,8},{10,9},{11,1... | collective-permute-start | bytes 294920 | tf_op jit(solution)/shard_map/ppermute | solution.py:29
  46.3 0.6 copy-start.5
  325.4 2.3 copy-start
Sparse Core Ops, SparseCore 0:
  38.4 286.9 all-reduce.2

commit v2 on v1

--- a/solution.py
+++ b/solution.py
@@ -3,9 +3,14 @@
 from jax import lax
 from jax.experimental import pallas as pl
 from jax.experimental.pallas import tpu as pltpu
+from jax.sharding import Mesh
 from jax.sharding import PartitionSpec as P
 
 GROUPS = 8
+SAMPLE_AXES = ("yl", "core")
+DEPTH_AXES = ("z", "x", "yh")
+HALF = 1296
+HALF_PADDED = 1536
 PAD = 32
 F32 = jnp.float32
 BF16 = jnp.bfloat16
@@ -24,9 +29,9 @@
 
 
 def shifted(array, by):
-    size = lax.axis_size("space")
+    size = lax.axis_size(DEPTH_AXES)
     pairs = [(i, i + by) for i in range(size) if 0 <= i + by < size]
-    return lax.ppermute(array, "space", pairs)
+    return lax.ppermute(array, DEPTH_AXES, pairs)
 
 
 def pair_kernel(vol, out, tmp):
@@ -112,7 +117,23 @@
     )(cot_lo, cot, cot_hi, w2)
 
 
-def middle_kernel(lower, pairs, w1, gh, cpad, gp_out, first, second, even, odd, hid, ups):
+def row_runs(start, count):
+    runs = []
+    done = 0
+    while done < count:
+        half, row = divmod(start + done, HALF)
+        size = min(count - done, HALF - row)
+        runs.append((half, row, done, size))
+        done += size
+    return runs
+
+
+def put_rows(terms, start, value):
+    for half, row, done, size in row_runs(start, value.shape[0]):
+        terms[half, row : row + size] = value[done : done + size]
+
+
+def middle_kernel(lower, pairs, w1, gh, cpad, gp_out, terms, even, odd, hid, ups):
     h2, w = 16, pairs.shape[2]
     cells = h2 * PAD
     clear(even)
@@ -155,9 +176,9 @@
     for kd in range(3):
         for kr in range(3):
             term = dot(window(kd, kr), ups[...], TN)
-            first[kd, kr, 0] = term[64:128, 128:256]
-            first[kd, kr, 1] = term[0:64, 0:128]
-            first[kd, kr, 2] = term[64:128, 0:128]
+            base = (kd * 3 + kr) * 192
+            put_rows(terms, base, term[64:128, 128:256])
+            put_rows(terms, base + 64, term[:, 0:128])
     lane_group = lax.broadcasted_iota(jnp.int32, (GROUPS, 16, 256), 2) // 32
     own = lane_group == lax.broadcasted_iota(jnp.int32, (GROUPS, 16, 256), 0)
     for kd in range(3):
@@ -165,7 +186,10 @@
             x = cpad[2 - kd, 2 - kr : 2 - kr + h2].reshape(cells, 256)
             term = dot(hid[...], x, TN).reshape(3, GROUPS, 16, 256)
             for kc in range(3):
-                second[kd, kr, kc] = jnp.sum(jnp.where(own, term[kc], 0.0), axis=0)
+                part = jnp.sum(jnp.where(own, term[kc], 0.0), axis=0)
+                base = 1728 + ((kd * 3 + kr) * 3 + kc) * 16
+                put_rows(terms, base, part[:, 0:128])
+                put_rows(terms, base + 432, part[:, 128:256])
 
 
 def middle(lower, pairs, w1, gh, cpad):
@@ -173,11 +197,10 @@
         middle_kernel,
         out_shape=(
             jax.ShapeDtypeStruct((16, 24, 128), BF16),
-            jax.ShapeDtypeStruct((3, 3, 3, 64, 128), F32),
-            jax.ShapeDtypeStruct((3, 3, 3, 16, 256), F32),
+            jax.ShapeDtypeStruct((2, HALF_PADDED, 128), F32),
         ),
         in_specs=vmem(5),
-        out_specs=tuple(vmem(3)),
+        out_specs=tuple(vmem(2)),
         scratch_shapes=[
             pltpu.VMEM((3, 16, PAD, 128), BF16),
             pltpu.VMEM((3, 17, PAD, 128), BF16),
@@ -196,7 +219,6 @@
     pad[0, 0:h2, 0:w] = gp[...]
     pad[1, 0:h2, 0:w] = upper[...]
     zeros = jnp.zeros((64, 128), BF16)
-    low = lax.broadcasted_iota(jnp.int32, (cells, 128), 1) < 64
     for par in range(2):
         depth = ((0, 1),) if par == 0 else ((0, 2), (1, 0))
         for row_par in range(2):
@@ -235,6 +257,51 @@
     )(gp, upper, w1)
 
 
+def unpack_kernel(summed, first, second):
+    for tap in range(27):
+        for half, row, done, size in row_runs(tap * 64, 64):
+            first[tap, done : done + size] = summed[half, row : row + size]
+        for side in range(2):
+            for half, row, done, size in row_runs(1728 + side * 432 + tap * 16, 16):
+                second[tap, done : done + size, side * 128 : side * 128 + 128] = summed[
+                    half, row : row + size
+                ]
+
+
+def unpack(summed):
+    return pl.pallas_call(
+        unpack_kernel,
+        out_shape=(
+            jax.ShapeDtypeStruct((27, 64, 128), F32),
+            jax.ShapeDtypeStruct((27, 16, 256), F32),
+        ),
+        in_specs=vmem(1),
+        out_specs=tuple(vmem(2)),
+        name="unpack",
+        cost_estimate=pl.CostEstimate(flops=0, bytes_accessed=3 << 20, transcendentals=0),
+    )(summed)
+
+
+def exchange(blocks, axes):
+    return lax.all_to_all(blocks, axes, split_axis=0, concat_axis=0, tiled=True)
+
+
+def spread(block, axes):
+    count = lax.axis_size(axes)
+    return exchange(jnp.broadcast_to(block[None], (count,) + block.shape), axes)
+
+
+def sum_everywhere(terms, scale):
+    plane = ("z", "x")
+    line = ("yl", "yh")
+    half = jnp.sum(exchange(terms, "core"), axis=0)
+    count = lax.axis_size(plane)
+    mine = jnp.sum(exchange(half.reshape(count, HALF_PADDED // count, 128), plane), axis=0)
+    mine = jnp.sum(spread(mine, line), axis=0) * scale
+    half = spread(mine, plane).reshape(HALF_PADDED, 128)
+    return spread(half, "core")
+
+
 def on_device(volume, cotangent, w_first, w_second):
     cot = cotangent[0, 0]
     cot_lo = shifted(cot, 1)
@@ -242,21 +309,22 @@
     pairs = pair_columns(volume[0])
     lower = shifted(pairs[1], 1)
     gh, cpad = group_backward(cot_lo, cot, cot_hi, w_second.reshape(27, 16, 256))
-    gp, first, second = middle(lower, pairs, w_first, gh, cpad)
+    gp, terms = middle(lower, pairs, w_first, gh, cpad)
     upper = shifted(gp, -1)
     grad_input = input_backward(gp, upper, w_first)
-    sum_first, sum_second = lax.psum((first, second), ("dp", "space"))
-    count = lax.axis_size("dp") * lax.axis_size("space") * 16 * 24
+    count = lax.axis_size(SAMPLE_AXES) * lax.axis_size(DEPTH_AXES) * 16 * 24
     scale = float(count) ** (-0.5)
-    return (grad_input[None], sum_first * scale, sum_second * scale)
+    first, second = unpack(sum_everywhere(terms, scale))
+    return (grad_input[None], first.reshape(3, 3, 3, 64, 128), second.reshape(3, 3, 3, 16, 256))
 
 
 def solution(mesh):
-    placed = (P("dp", "space", None, None, None), P("dp", "space", None, None, None), P(), P())
+    fine = Mesh(mesh.devices.reshape(2, 2, 8, 4, 4), SAMPLE_AXES + DEPTH_AXES)
+    split = P(SAMPLE_AXES, DEPTH_AXES, None, None, None)
     return jax.shard_map(
         on_device,
-        mesh=mesh,
-        in_specs=placed,
-        out_specs=(P("dp", "space", None, None, None), P(), P()),
+        mesh=fine,
+        in_specs=(split, split, P(), P()),
+        out_specs=(split, P(), P()),
         check_vma=False,
     )

time: 336 us -> 130 us (0.39)
  waiting for transfers between devices: 286 us -> 18.9 us
  blocking collectives: 0 us -> 68.3 us
  between operations: 14.1 us -> 0.75 us
  starting transfers between devices: 13.8 us -> 19.7 us
    psum x1 -> x0, waiting for transfers between devices: 275 us -> none  [on_device(): sum_first, sum_second = lax.psum((first, second), ('dp', 'space'))]
    all_to_all x0 -> x4, blocking collectives: none -> 68.3 us  [exchange(): return lax.all_to_all(blocks, axes, split_axis=0, concat_axis=0, tiled=True)]
    all_to_all x0 -> x1, waiting for transfers between devices: none -> 9.56 us  [exchange(): return lax.all_to_all(blocks, axes, split_axis=0, concat_axis=0, tiled=True)]
    all_to_all x0 -> x1, starting transfers between devices: none -> 5.93 us  [exchange(): return lax.all_to_all(blocks, axes, split_axis=0, concat_axis=0, tiled=True)]
  transfers between devices with their start and end apart: 5 -> 5, of which waited for: 3 -> 3; matrix products, arithmetic and copies ran while one was open for 0% -> 1% of each run, Pallas kernels for 3% -> 7%
where the time goes in v2:
time: 130 us
  blocking collectives  68.3 us (53%)
  starting transfers between devices  19.7 us (15%)
  waiting for transfers between devices  18.9 us (15%)
  Pallas kernels  17.8 us (14%)
  local copies, waits for them, and re-layouts  4.03 us (3%)
    all_to_all x4, blocking collectives, exchange(): return lax.all_to_all(blocks, axes, split_axis=0, concat_axis=0, tiled=True)  68.3 us
    ppermute x4, starting transfers between devices, shifted(): return lax.ppermute(array, DEPTH_AXES, pairs)  13.7 us
    all_to_all x1, waiting for transfers between devices, exchange(): return lax.all_to_all(blocks, axes, split_axis=0, concat_axis=0, tiled=True)  9.56 us
    ppermute x4, waiting for transfers between devices, shifted(): return lax.ppermute(array, DEPTH_AXES, pairs)  9.31 us
    pallas_call x1, Pallas kernels, middle(): pl.pallas_call(middle_kernel, out_shape=(jax.ShapeDtypeStruct((16, 24, 12...  6.26 us
    all_to_all x1, starting transfers between devices, exchange(): return lax.all_to_all(blocks, axes, split_axis=0, concat_axis=0, tiled=True)  5.93 us
    pallas_call x1, Pallas kernels, group_backward(): pl.pallas_call(group_kernel, out_shape=(jax.ShapeDtypeStruct((16 * PAD, 1...  3.31 us
    pallas_call x1, Pallas kernels, input_backward(): pl.pallas_call(input_kernel, out_shape=jax.ShapeDtypeStruct((2, 32, 48, 6...  3.06 us
  transfers between devices with their start and end apart: 5, of which 3 were waited for; matrix products, arithmetic and copies ran while one was open for 1% of the time, Pallas kernels for 7%

profile of v2, /device:TPU:1, one launch (start us, length us, event | category | flops | bytes accessed | tf_op | source)
XLA Modules:
  0.0 129.7 jit_solution(15395798326013974803)
XLA Ops:
  0.6 1.3 collective-permute-start.2
  1.9 5.7 %collective-permute-start.1 = (bf16[16,24,256]{2,1,0:T(8,128)(2,1)}, bf16[16,24,256]{2,1,0:T(8,128)(2,1)S(1)}, u32[]{:S(2)}, u32[]{:S(2)}) collective-permute-start(bf16[16,24,256]{2,1,0:T(8,128)(2,1)} %bitcast.17), channel_id=1, source_target_pairs={{0,1},{1,2},{2,3},{3,4},{4,5},{5,6},{6,7},{7,8},{8,9},{9,10},{10,1... | collective-permute-start | bytes 589832 | tf_op jit(solution)/shard_map/ppermute | solution.py:34
  7.6 2.7 %pair_columns.1.pairs = bf16[2,32,24,128]{3,2,1,0:T(8,128)(2,1)} custom-call(bf16[2,32,48,64]{3,2,1,0:T(8,128)(2,1)} %bitcast.12), custom_call_target="tpu_custom_call" | custom-call | bytes 2097152 | tf_op jit(solution)/shard_map/pair_columns/pallas_call | solution.py:56
  10.3 0.9 slice_bitcast_fusion
  11.2 5.5 %collective-permute-start = (bf16[32,24,128]{2,1,0:T(8,128)(2,1)S(1)}, bf16[32,24,128]{2,1,0:T(8,128)(2,1)S(1)}, u32[]{:S(2)}, u32[]{:S(2)}) collective-permute-start(bf16[32,24,128]{2,1,0:T(8,128)(2,1)S(1)} %slice_bitcast_fusion), channel_id=1, source_target_pairs={{0,1},{1,2},{2,3},{3,4},{4,5},{5,6},{6,7},{7,8},{8,9},{9,10},{10,1... | collective-permute-start | bytes 589832 | tf_op jit(solution)/shard_map/ppermute | solution.py:34
  16.7 0.0 collective-permute-done.2.cot_hi
  16.7 0.0 copy-start.1
  16.7 0.0 collective-permute-done.1.cot_lo
  16.7 0.0 copy-start.2
  16.8 0.6 copy-done.1
  17.4 0.1 copy-done.2
  17.5 3.3 %group_backward.1 = (bf16[512,128]{1,0:T(8,128)(2,1)}, bf16[3,18,32,256]{3,2,1,0:T(8,128)(2,1)}) custom-call(bf16[16,24,256]{2,1,0:T(8,128)(2,1)} %copy-done.2, bf16[16,24,256]{2,1,0:T(8,128)(2,1)} %bitcast.18, bf16[16,24,256]{2,1,0:T(8,128)(2,1)} %copy-done.1, bf16[27,16,256]{2,1,0:T(8,128)(2,1)} %bitcast.15), custom_call_target="tpu_custom_call" | custom-call | flops 2147483648 | bytes 2097152 | tf_op jit(solution)/shard_map/group_backward/pallas_call | solution.py:103
  20.8 4.3 %collective-permute-done.lower = bf16[32,24,128]{2,1,0:T(8,128)(2,1)S(1)} collective-permute-done((bf16[32,24,128]{2,1,0:T(8,128)(2,1)S(1)}, bf16[32,24,128]{2,1,0:T(8,128)(2,1)S(1)}, u32[]{:S(2)}, u32[]{:S(2)}) %collective-permute-start) | collective-permute-done | bytes 196640 | tf_op jit(solution)/shard_map/ppermute | solution.py:34
  25.1 0.0 copy-start
  25.1 0.7 copy-done
  25.8 6.3 %middle.1 = (bf16[16,24,128]{2,1,0:T(8,128)(2,1)}, f32[2,1536,128]{2,1,0:T(8,128)}) custom-call(bf16[32,24,128]{2,1,0:T(8,128)(2,1)} %copy-done, bf16[2,32,24,128]{3,2,1,0:T(8,128)(2,1)} %pair_columns.1.pairs, bf16[3,3,3,64,128]{4,3,2,1,0:T(8,128)(2,1)} %w1.3, bf16[512,128]{1,0:T(8,128)(2,1)} %get-tuple-element.9.gh, ...), custom_call_target="tpu_custom_call" | custom-call | flops 3221225472 | bytes 4194304 | tf_op jit(solution)/shard_map/middle/pallas_call | solution.py:196
  32.1 7.8 %all_to_all.25 = f32[2,1536,128]{2,1,0:T(8,128)S(1)} all-to-all(f32[2,1536,128]{2,1,0:T(8,128)} %get-tuple-element.12), channel_id=1, replica_groups=mesh['yl'=2,'core'=2,'z'=8,'x'=4,'yh'=4] {'core'}, dimensions={0} | all-to-all | bytes 3145728 | tf_op jit(solution)/shard_map/all_to_all | solution.py:286
  39.9 0.2 reduce_sum.27
  40.0 40.3 %all_to_all.26 = f32[32,48,128]{2,1,0:T(8,128)S(1)} all-to-all(f32[32,48,128]{2,1,0:T(8,128)S(1)} %bitcast.10), channel_id=1, replica_groups=mesh['yl'=2,'core'=2,'z'=8,'x'=4,'yh'=4] {'z','x'}, dimensions={0} | all-to-all | bytes 1572864 | tf_op jit(solution)/shard_map/all_to_all | solution.py:286
  80.3 0.1 reduce_sum.28
  80.4 0.0 copy-start.3
  80.4 10.1 %all_to_all.27 = f32[8,48,128]{2,1,0:T(8,128)S(1)} all-to-all(f32[8,48,128]{2,1,0:T(8,128)S(1)} %broadcast_in_dim.11), channel_id=1, replica_groups=mesh['yl'=2,'core'=2,'z'=8,'x'=4,'yh'=4] {'yl','yh'}, dimensions={0} | all-to-all | bytes 393216 | tf_op jit(solution)/shard_map/all_to_all | solution.py:286
  90.5 0.9 broadcast_in_dim.24
  91.4 5.9 %all-to-all-start.3 = ((f32[32,48,128]{2,1,0:T(8,128)}), f32[32,48,128]{2,1,0:T(8,128)S(1)}, u32[]{:S(2)}, u32[]{:S(2)}) async-start(f32[32,48,128]{2,1,0:T(8,128)} %broadcast_in_dim.24), calls=%async_computation.3 | async-start | bytes 1572864 | tf_op jit(solution)/shard_map/all_to_all | solution.py:286
  97.3 0.0 copy-done.3
  97.3 1.3 collective-permute-start.3
  98.6 5.0 %collective-permute-done.3.upper = bf16[16,24,128]{2,1,0:T(8,128)(2,1)S(1)} collective-permute-done((bf16[16,24,128]{2,1,0:T(8,128)(2,1)S(1)}, bf16[16,24,128]{2,1,0:T(8,128)(2,1)S(1)}, u32[]{:S(2)}, u32[]{:S(2)}) %collective-permute-start.3) | collective-permute-done | bytes 98336 | tf_op jit(solution)/shard_map/ppermute | solution.py:34
  103.6 0.0 copy-start.4
  103.6 0.6 copy-done.4
  104.2 3.1 %input_backward.1 = bf16[2,32,48,64]{3,2,1,0:T(8,128)(2,1)} custom-call(bf16[16,24,128]{2,1,0:T(8,128)(2,1)} %get-tuple-element.11.gp, bf16[16,24,128]{2,1,0:T(8,128)(2,1)} %copy-done.4, bf16[3,3,3,64,128]{4,3,2,1,0:T(8,128)(2,1)} %w1.3), custom_call_target="tpu_custom_call" | custom-call | flops 1073741824 | bytes 2097152 | tf_op jit(solution)/shard_map/input_backward/pallas_call | solution.py:246
  107.3 9.6 %all-to-all-done.3 = f32[32,48,128]{2,1,0:T(8,128)S(1)} async-done(((f32[32,48,128]{2,1,0:T(8,128)}), f32[32,48,128]{2,1,0:T(8,128)S(1)}, u32[]{:S(2)}, u32[]{:S(2)}) %all-to-all-start.3) | async-done | bytes 786464 | tf_op jit(solution)/shard_map/all_to_all | solution.py:286
  116.9 0.1 broadcast_in_dim.26
  117.0 10.2 %all_to_all.28.summed = f32[2,1536,128]{2,1,0:T(8,128)} all-to-all(f32[2,1536,128]{2,1,0:T(8,128)S(1)} %broadcast_in_dim.26), channel_id=1, replica_groups=mesh['yl'=2,'core'=2,'z'=8,'x'=4,'yh'=4] {'core'}, dimensions={0} | all-to-all | bytes 3145728 | tf_op jit(solution)/shard_map/all_to_all | solution.py:286
  127.2 2.5 %unpack.1 = (f32[27,64,128]{2,1,0:T(8,128)}, f32[27,16,256]{2,1,0:T(8,128)}) custom-call(f32[2,1536,128]{2,1,0:T(8,128)} %all_to_all.28.summed), custom_call_target="tpu_custom_call" | custom-call | bytes 3145728 | tf_op jit(solution)/shard_map/unpack/pallas_call | solution.py:272
  (3 shorter events, 0.0 us)
Async XLA Ops:
  0.6 16.1 %collective-permute-start.2 = (bf16[16,24,256]{2,1,0:T(8,128)(2,1)}, bf16[16,24,256]{2,1,0:T(8,128)(2,1)S(1)}, u32[]{:S(2)}, u32[]{:S(2)}) collective-permute-start(bf16[16,24,256]{2,1,0:T(8,128)(2,1)} %bitcast.16), channel_id=1, source_target_pairs={{1,0},{2,1},{3,2},{4,3},{5,4},{6,5},{7,6},{8,7},{9,8},{10,9},{11,1... | collective-permute-start | bytes 589832 | tf_op jit(solution)/shard_map/ppermute | solution.py:34
  1.9 14.8 %collective-permute-start.1 = (bf16[16,24,256]{2,1,0:T(8,128)(2,1)}, bf16[16,24,256]{2,1,0:T(8,128)(2,1)S(1)}, u32[]{:S(2)}, u32[]{:S(2)}) collective-permute-start(bf16[16,24,256]{2,1,0:T(8,128)(2,1)} %bitcast.17), channel_id=1, source_target_pairs={{0,1},{1,2},{2,3},{3,4},{4,5},{5,6},{6,7},{7,8},{8,9},{9,10},{10,1... | collective-permute-start | bytes 589832 | tf_op jit(solution)/shard_map/ppermute | solution.py:34
  11.2 13.9 %collective-permute-start = (bf16[32,24,128]{2,1,0:T(8,128)(2,1)S(1)}, bf16[32,24,128]{2,1,0:T(8,128)(2,1)S(1)}, u32[]{:S(2)}, u32[]{:S(2)}) collective-permute-start(bf16[32,24,128]{2,1,0:T(8,128)(2,1)S(1)} %slice_bitcast_fusion), channel_id=1, source_target_pairs={{0,1},{1,2},{2,3},{3,4},{4,5},{5,6},{6,7},{7,8},{8,9},{9,10},{10,1... | collective-permute-start | bytes 589832 | tf_op jit(solution)/shard_map/ppermute | solution.py:34
  16.7 0.7 copy-start.1
  16.7 0.7 copy-start.2
  25.1 0.7 copy-start
  80.4 17.0 %copy-start.3 = (bf16[16,24,128]{2,1,0:T(8,128)(2,1)S(1)}, bf16[16,24,128]{2,1,0:T(8,128)(2,1)}, u32[]{:S(2)}) copy-start(bf16[16,24,128]{2,1,0:T(8,128)(2,1)} %get-tuple-element.11.gp) | copy-start | bytes 294916
  91.4 25.5 %all-to-all-start.3 = ((f32[32,48,128]{2,1,0:T(8,128)}), f32[32,48,128]{2,1,0:T(8,128)S(1)}, u32[]{:S(2)}, u32[]{:S(2)}) async-start(f32[32,48,128]{2,1,0:T(8,128)} %broadcast_in_dim.24), calls=%async_computation.3 | async-start | bytes 1572864 | tf_op jit(solution)/shard_map/all_to_all | solution.py:286
  97.3 6.3 %collective-permute-start.3 = (bf16[16,24,128]{2,1,0:T(8,128)(2,1)S(1)}, bf16[16,24,128]{2,1,0:T(8,128)(2,1)S(1)}, u32[]{:S(2)}, u32[]{:S(2)}) collective-permute-start(bf16[16,24,128]{2,1,0:T(8,128)(2,1)S(1)} %copy-done.3), channel_id=1, source_target_pairs={{1,0},{2,1},{3,2},{4,3},{5,4},{6,5},{7,6},{8,7},{9,8},{10,9},{11,1... | collective-permute-start | bytes 294920 | tf_op jit(solution)/shard_map/ppermute | solution.py:34
  103.6 0.6 copy-start.4

commit v3 on v2

--- a/solution.py
+++ b/solution.py
@@ -130,7 +130,7 @@
 
 def put_rows(terms, start, value):
     for half, row, done, size in row_runs(start, value.shape[0]):
-        terms[half, row : row + size] = value[done : done + size]
+        terms[half, row : row + size] = value[done : done + size].astype(BF16)
 
 
 def middle_kernel(lower, pairs, w1, gh, cpad, gp_out, terms, even, odd, hid, ups):
@@ -197,7 +197,7 @@
         middle_kernel,
         out_shape=(
             jax.ShapeDtypeStruct((16, 24, 128), BF16),
-            jax.ShapeDtypeStruct((2, HALF_PADDED, 128), F32),
+            jax.ShapeDtypeStruct((2, HALF_PADDED, 128), BF16),
         ),
         in_specs=vmem(5),
         out_specs=tuple(vmem(2)),
@@ -260,12 +260,12 @@
 def unpack_kernel(summed, first, second):
     for tap in range(27):
         for half, row, done, size in row_runs(tap * 64, 64):
-            first[tap, done : done + size] = summed[half, row : row + size]
+            first[tap, done : done + size] = summed[half, row : row + size].astype(F32)
         for side in range(2):
             for half, row, done, size in row_runs(1728 + side * 432 + tap * 16, 16):
                 second[tap, done : done + size, side * 128 : side * 128 + 128] = summed[
                     half, row : row + size
-                ]
+                ].astype(F32)
 
 
 def unpack(summed):
@@ -291,13 +291,17 @@
     return exchange(jnp.broadcast_to(block[None], (count,) + block.shape), axes)
 
 
+def added(blocks):
+    return jnp.sum(blocks.astype(F32), axis=0)
+
+
 def sum_everywhere(terms, scale):
     plane = ("z", "x")
     line = ("yl", "yh")
-    half = jnp.sum(exchange(terms, "core"), axis=0)
     count = lax.axis_size(plane)
-    mine = jnp.sum(exchange(half.reshape(count, HALF_PADDED // count, 128), plane), axis=0)
-    mine = jnp.sum(spread(mine, line), axis=0) * scale
+    half = added(exchange(terms, "core")).astype(BF16)
+    mine = added(exchange(half.reshape(count, HALF_PADDED // count, 128), plane))
+    mine = (added(spread(mine, line)) * scale).astype(BF16)
     half = spread(mine, plane).reshape(HALF_PADDED, 128)
     return spread(half, "core")
 

time: 130 us -> 113 us (0.87)
  blocking collectives: 68.3 us -> 60 us
  waiting for transfers between devices: 18.9 us -> 10.8 us
    all_to_all x4, blocking collectives: 68.3 us -> 60 us  [exchange(): return lax.all_to_all(blocks, axes, split_axis=0, concat_axis=0, tiled=True)]
    all_to_all x1, waiting for transfers between devices: 9.56 us -> 1.48 us  [exchange(): return lax.all_to_all(blocks, axes, split_axis=0, concat_axis=0, tiled=True)]
  transfers between devices with their start and end apart: 5 -> 5, of which waited for: 3 -> 3; matrix products, arithmetic and copies ran while one was open for 1% -> 1% of each run, Pallas kernels for 7% -> 8%
where the time goes in v3:
time: 113 us; the launch traced here: 112 us
  blocking collectives  60 us (53%)
  starting transfers between devices  18.9 us (17%)
  Pallas kernels  17.3 us (15%)
  waiting for transfers between devices  10.8 us (10%)
  local copies, waits for them, and re-layouts  3.84 us (3%)
    all_to_all x4, blocking collectives, exchange(): return lax.all_to_all(blocks, axes, split_axis=0, concat_axis=0, tiled=True)  60 us
    ppermute x4, starting transfers between devices, shifted(): return lax.ppermute(array, DEPTH_AXES, pairs)  13.7 us
    ppermute x4, waiting for transfers between devices, shifted(): return lax.ppermute(array, DEPTH_AXES, pairs)  9.31 us
    pallas_call x1, Pallas kernels, middle(): pl.pallas_call(middle_kernel, out_shape=(jax.ShapeDtypeStruct((16, 24, 12...  5.98 us
    all_to_all x1, starting transfers between devices, exchange(): return lax.all_to_all(blocks, axes, split_axis=0, concat_axis=0, tiled=True)  5.13 us
    pallas_call x1, Pallas kernels, group_backward(): pl.pallas_call(group_kernel, out_shape=(jax.ShapeDtypeStruct((16 * PAD, 1...  3.32 us
    pallas_call x1, Pallas kernels, input_backward(): pl.pallas_call(input_kernel, out_shape=jax.ShapeDtypeStruct((2, 32, 48, 6...  3.06 us
    pallas_call x1, Pallas kernels, pair_columns(): pl.pallas_call(pair_kernel, out_shape=jax.ShapeDtypeStruct((planes, rows,...  2.67 us
  transfers between devices with their start and end apart: 5, of which 3 were waited for; matrix products, arithmetic and copies ran while one was open for 1% of the time, Pallas kernels for 8%

profile of v3, /device:TPU:1, one launch (start us, length us, event | category | flops | bytes accessed | tf_op | source)
XLA Modules:
  0.0 112.0 jit_solution(15109634098842066631)
XLA Ops:
  0.6 1.3 %collective-permute-start.2 = (bf16[16,24,256]{2,1,0:T(8,128)(2,1)}, bf16[16,24,256]{2,1,0:T(8,128)(2,1)S(1)}, u32[]{:S(2)}, u32[]{:S(2)}) collective-permute-start(bf16[16,24,256]{2,1,0:T(8,128)(2,1)} %bitcast.16), channel_id=1, source_target_pairs={{1,0},{2,1},{3,2},{4,3},{5,4},{6,5},{7,6},{8,7},{9,8},{10,9},{11,1... | collective-permute-start | bytes 589832 | tf_op jit(solution)/shard_map/ppermute | solution.py:34
  1.9 5.7 %collective-permute-start.1 = (bf16[16,24,256]{2,1,0:T(8,128)(2,1)}, bf16[16,24,256]{2,1,0:T(8,128)(2,1)S(1)}, u32[]{:S(2)}, u32[]{:S(2)}) collective-permute-start(bf16[16,24,256]{2,1,0:T(8,128)(2,1)} %bitcast.17), channel_id=1, source_target_pairs={{0,1},{1,2},{2,3},{3,4},{4,5},{5,6},{6,7},{7,8},{8,9},{9,10},{10,1... | collective-permute-start | bytes 589832 | tf_op jit(solution)/shard_map/ppermute | solution.py:34
  7.6 2.7 %pair_columns.1.pairs = bf16[2,32,24,128]{3,2,1,0:T(8,128)(2,1)} custom-call(bf16[2,32,48,64]{3,2,1,0:T(8,128)(2,1)} %bitcast.12), custom_call_target="tpu_custom_call" | custom-call | bytes 2097152 | tf_op jit(solution)/shard_map/pair_columns/pallas_call | solution.py:56
  10.3 0.9 slice_bitcast_fusion
  11.2 5.5 %collective-permute-start = (bf16[32,24,128]{2,1,0:T(8,128)(2,1)S(1)}, bf16[32,24,128]{2,1,0:T(8,128)(2,1)S(1)}, u32[]{:S(2)}, u32[]{:S(2)}) collective-permute-start(bf16[32,24,128]{2,1,0:T(8,128)(2,1)S(1)} %slice_bitcast_fusion), channel_id=1, source_target_pairs={{0,1},{1,2},{2,3},{3,4},{4,5},{5,6},{6,7},{7,8},{8,9},{9,10},{10,1... | collective-permute-start | bytes 589832 | tf_op jit(solution)/shard_map/ppermute | solution.py:34
  16.7 0.0 collective-permute-done.2.cot_hi
  16.7 0.0 copy-start.1
  16.7 0.0 collective-permute-done.1.cot_lo
  16.7 0.0 copy-start.2
  16.8 0.6 copy-done.1
  17.4 0.1 copy-done.2
  17.5 3.3 %group_backward.1 = (bf16[512,128]{1,0:T(8,128)(2,1)}, bf16[3,18,32,256]{3,2,1,0:T(8,128)(2,1)}) custom-call(bf16[16,24,256]{2,1,0:T(8,128)(2,1)} %copy-done.2, bf16[16,24,256]{2,1,0:T(8,128)(2,1)} %bitcast.18, bf16[16,24,256]{2,1,0:T(8,128)(2,1)} %copy-done.1, bf16[27,16,256]{2,1,0:T(8,128)(2,1)} %bitcast.15), custom_call_target="tpu_custom_call" | custom-call | flops 2147483648 | bytes 2097152 | tf_op jit(solution)/shard_map/group_backward/pallas_call | solution.py:103
  20.8 4.3 %collective-permute-done.lower = bf16[32,24,128]{2,1,0:T(8,128)(2,1)S(1)} collective-permute-done((bf16[32,24,128]{2,1,0:T(8,128)(2,1)S(1)}, bf16[32,24,128]{2,1,0:T(8,128)(2,1)S(1)}, u32[]{:S(2)}, u32[]{:S(2)}) %collective-permute-start) | collective-permute-done | bytes 196640 | tf_op jit(solution)/shard_map/ppermute | solution.py:34
  25.1 0.0 copy-start
  25.1 0.7 copy-done
  25.8 6.0 %middle.1 = (bf16[16,24,128]{2,1,0:T(8,128)(2,1)}, bf16[2,1536,128]{2,1,0:T(8,128)(2,1)}) custom-call(bf16[32,24,128]{2,1,0:T(8,128)(2,1)} %copy-done, bf16[2,32,24,128]{3,2,1,0:T(8,128)(2,1)} %pair_columns.1.pairs, bf16[3,3,3,64,128]{4,3,2,1,0:T(8,128)(2,1)} %w1.3, bf16[512,128]{1,0:T(8,128)(2,1)} %get-tuple-element.9.gh, ...), custom_call_target="tpu_custom_call" | custom-call | flops 3221225472 | bytes 4194304 | tf_op jit(solution)/shard_map/middle/pallas_call | solution.py:196
  31.8 7.1 %all_to_all.25 = bf16[2,1536,128]{2,1,0:T(8,128)(2,1)S(1)} all-to-all(bf16[2,1536,128]{2,1,0:T(8,128)(2,1)} %get-tuple-element.12), channel_id=1, replica_groups=mesh['yl'=2,'core'=2,'z'=8,'x'=4,'yh'=4] {'core'}, dimensions={0} | all-to-all | bytes 1572864 | tf_op jit(solution)/shard_map/all_to_all | solution.py:286
  38.9 0.4 reduce_sum.30
  39.2 32.8 %all_to_all.26 = bf16[32,48,128]{2,1,0:T(8,128)(2,1)S(1)} all-to-all(bf16[32,48,128]{2,1,0:T(8,128)(2,1)S(1)} %bitcast.11), channel_id=1, replica_groups=mesh['yl'=2,'core'=2,'z'=8,'x'=4,'yh'=4] {'z','x'}, dimensions={0} | all-to-all | bytes 786432 | tf_op jit(solution)/shard_map/all_to_all | solution.py:286
  72.1 0.1 convert_reduce_fusion
  72.2 10.0 %all_to_all.27 = f32[8,48,128]{2,1,0:T(8,128)S(1)} all-to-all(f32[8,48,128]{2,1,0:T(8,128)S(1)} %broadcast_in_dim.11), channel_id=1, replica_groups=mesh['yl'=2,'core'=2,'z'=8,'x'=4,'yh'=4] {'yl','yh'}, dimensions={0} | all-to-all | bytes 393216 | tf_op jit(solution)/shard_map/all_to_all | solution.py:286
  82.2 0.8 broadcast_in_dim.24
  83.0 0.0 copy-start.3
  83.0 5.1 %all-to-all-start.3 = ((bf16[32,48,128]{2,1,0:T(8,128)(2,1)}), bf16[32,48,128]{2,1,0:T(8,128)(2,1)S(1)}, u32[]{:S(2)}, u32[]{:S(2)}) async-start(bf16[32,48,128]{2,1,0:T(8,128)(2,1)} %broadcast_in_dim.24), calls=%async_computation.3 | async-start | bytes 786432 | tf_op jit(solution)/shard_map/all_to_all | solution.py:286
  88.2 0.0 copy-done.3
  88.2 1.3 %collective-permute-start.3 = (bf16[16,24,128]{2,1,0:T(8,128)(2,1)S(1)}, bf16[16,24,128]{2,1,0:T(8,128)(2,1)S(1)}, u32[]{:S(2)}, u32[]{:S(2)}) collective-permute-start(bf16[16,24,128]{2,1,0:T(8,128)(2,1)S(1)} %copy-done.3), channel_id=1, source_target_pairs={{1,0},{2,1},{3,2},{4,3},{5,4},{6,5},{7,6},{8,7},{9,8},{10,9},{11,1... | collective-permute-start | bytes 294920 | tf_op jit(solution)/shard_map/ppermute | solution.py:34
  89.5 5.0 %collective-permute-done.3.upper = bf16[16,24,128]{2,1,0:T(8,128)(2,1)S(1)} collective-permute-done((bf16[16,24,128]{2,1,0:T(8,128)(2,1)S(1)}, bf16[16,24,128]{2,1,0:T(8,128)(2,1)S(1)}, u32[]{:S(2)}, u32[]{:S(2)}) %collective-permute-start.3) | collective-permute-done | bytes 98336 | tf_op jit(solution)/shard_map/ppermute | solution.py:34
  94.4 0.0 copy-start.4
  94.4 0.6 copy-done.4
  95.1 3.1 %input_backward.1 = bf16[2,32,48,64]{3,2,1,0:T(8,128)(2,1)} custom-call(bf16[16,24,128]{2,1,0:T(8,128)(2,1)} %get-tuple-element.11.gp, bf16[16,24,128]{2,1,0:T(8,128)(2,1)} %copy-done.4, bf16[3,3,3,64,128]{4,3,2,1,0:T(8,128)(2,1)} %w1.3), custom_call_target="tpu_custom_call" | custom-call | flops 1073741824 | bytes 2097152 | tf_op jit(solution)/shard_map/input_backward/pallas_call | solution.py:246
  98.1 1.5 %all-to-all-done.3 = bf16[32,48,128]{2,1,0:T(8,128)(2,1)S(1)} async-done(((bf16[32,48,128]{2,1,0:T(8,128)(2,1)}), bf16[32,48,128]{2,1,0:T(8,128)(2,1)S(1)}, u32[]{:S(2)}, u32[]{:S(2)}) %all-to-all-start.3) | async-done | bytes 393248 | tf_op jit(solution)/shard_map/all_to_all | solution.py:286
  99.6 0.1 broadcast_in_dim.26
  99.7 10.0 %all_to_all.28.summed = bf16[2,1536,128]{2,1,0:T(8,128)(2,1)} all-to-all(bf16[2,1536,128]{2,1,0:T(8,128)(2,1)S(1)} %broadcast_in_dim.26), channel_id=1, replica_groups=mesh['yl'=2,'core'=2,'z'=8,'x'=4,'yh'=4] {'core'}, dimensions={0} | all-to-all | bytes 1572864 | tf_op jit(solution)/shard_map/all_to_all | solution.py:286
  109.7 2.3 %unpack.1 = (f32[27,64,128]{2,1,0:T(8,128)}, f32[27,16,256]{2,1,0:T(8,128)}) custom-call(bf16[2,1536,128]{2,1,0:T(8,128)(2,1)} %all_to_all.28.summed), custom_call_target="tpu_custom_call" | custom-call | bytes 3145728 | tf_op jit(solution)/shard_map/unpack/pallas_call | solution.py:272
  (3 shorter events, 0.0 us)
Async XLA Ops:
  0.6 16.1 %collective-permute-start.2 = (bf16[16,24,256]{2,1,0:T(8,128)(2,1)}, bf16[16,24,256]{2,1,0:T(8,128)(2,1)S(1)}, u32[]{:S(2)}, u32[]{:S(2)}) collective-permute-start(bf16[16,24,256]{2,1,0:T(8,128)(2,1)} %bitcast.16), channel_id=1, source_target_pairs={{1,0},{2,1},{3,2},{4,3},{5,4},{6,5},{7,6},{8,7},{9,8},{10,9},{11,1... | collective-permute-start | bytes 589832 | tf_op jit(solution)/shard_map/ppermute | solution.py:34
  1.9 14.8 %collective-permute-start.1 = (bf16[16,24,256]{2,1,0:T(8,128)(2,1)}, bf16[16,24,256]{2,1,0:T(8,128)(2,1)S(1)}, u32[]{:S(2)}, u32[]{:S(2)}) collective-permute-start(bf16[16,24,256]{2,1,0:T(8,128)(2,1)} %bitcast.17), channel_id=1, source_target_pairs={{0,1},{1,2},{2,3},{3,4},{4,5},{5,6},{6,7},{7,8},{8,9},{9,10},{10,1... | collective-permute-start | bytes 589832 | tf_op jit(solution)/shard_map/ppermute | solution.py:34
  11.2 13.9 %collective-permute-start = (bf16[32,24,128]{2,1,0:T(8,128)(2,1)S(1)}, bf16[32,24,128]{2,1,0:T(8,128)(2,1)S(1)}, u32[]{:S(2)}, u32[]{:S(2)}) collective-permute-start(bf16[32,24,128]{2,1,0:T(8,128)(2,1)S(1)} %slice_bitcast_fusion), channel_id=1, source_target_pairs={{0,1},{1,2},{2,3},{3,4},{4,5},{5,6},{6,7},{7,8},{8,9},{9,10},{10,1... | collective-permute-start | bytes 589832 | tf_op jit(solution)/shard_map/ppermute | solution.py:34
  16.7 0.7 copy-start.1
  16.7 0.7 copy-start.2
  25.1 0.7 copy-start
  83.0 5.1 %copy-start.3 = (bf16[16,24,128]{2,1,0:T(8,128)(2,1)S(1)}, bf16[16,24,128]{2,1,0:T(8,128)(2,1)}, u32[]{:S(2)}) copy-start(bf16[16,24,128]{2,1,0:T(8,128)(2,1)} %get-tuple-element.11.gp) | copy-start | bytes 294916
  83.0 16.6 %all-to-all-start.3 = ((bf16[32,48,128]{2,1,0:T(8,128)(2,1)}), bf16[32,48,128]{2,1,0:T(8,128)(2,1)S(1)}, u32[]{:S(2)}, u32[]{:S(2)}) async-start(bf16[32,48,128]{2,1,0:T(8,128)(2,1)} %broadcast_in_dim.24), calls=%async_computation.3 | async-start | bytes 786432 | tf_op jit(solution)/shard_map/all_to_all | solution.py:286
  88.2 6.3 %collective-permute-start.3 = (bf16[16,24,128]{2,1,0:T(8,128)(2,1)S(1)}, bf16[16,24,128]{2,1,0:T(8,128)(2,1)S(1)}, u32[]{:S(2)}, u32[]{:S(2)}) collective-permute-start(bf16[16,24,128]{2,1,0:T(8,128)(2,1)S(1)} %copy-done.3), channel_id=1, source_target_pairs={{1,0},{2,1},{3,2},{4,3},{5,4},{6,5},{7,6},{8,7},{9,8},{10,9},{11,1... | collective-permute-start | bytes 294920 | tf_op jit(solution)/shard_map/ppermute | solution.py:34
  94.4 0.6 copy-start.4

commit v4 on v1

v4 whole, which is shorter than its diff:
```python
import functools

import jax
import jax.numpy as jnp
from jax import lax
from jax.experimental import pallas as pl
from jax.experimental.pallas import tpu as pltpu
from jax.sharding import Mesh
from jax.sharding import PartitionSpec as P

GROUPS = 8
SAMPLE_AXES = ("yl", "core")
DEPTH_AXES = ("z", "x", "yh")
TAPS = 27
CHUNK = 48
PAD = 32
F32 = jnp.float32
BF16 = jnp.bfloat16

NT = (((1,), (1,)), ((), ()))
NN = (((1,), (0,)), ((), ()))
TN = (((0,), (0,)), ((), ()))


def dot(a, b, dims):
    return lax.dot_general(a, b, dims, preferred_element_type=F32)


def vmem(n):
    return [pl.BlockSpec(memory_space=pltpu.VMEM)] * n


def shifted(array, by):
    size = lax.axis_size(DEPTH_AXES)
    pairs = [(i, i + by) for i in range(size) if 0 <= i + by < size]
    return lax.ppermute(array, DEPTH_AXES, pairs)


def clear(ref):
    ref[...] = jnp.zeros_like(ref)


def roll_rows(x, by):
    return pltpu.roll(x, by % x.shape[0], 0)


def half_turn(x):
    return pltpu.roll(x, 64, x.ndim - 1)


def low_lanes(shape):
    return lax.broadcasted_iota(jnp.int32, shape, len(shape) - 1) < 64


def pair_rows(plane, out, tmp):
    step = tmp.shape[0]
    low = low_lanes((step, 24, 128))

    def body(i, carry):
        r = i * step
        tmp[:, :, 0:64] = plane[pl.ds(r, step)].astype(F32)
        even = tmp[:, pl.ds(0, 24, 2), :]
        odd = half_turn(tmp[:, pl.ds(1, 24, 2), :])
        out[pl.ds(r, step)] = jnp.where(low, even, odd).astype(BF16)
        return carry

    lax.fori_loop(0, plane.shape[0] // step, body, 0)


def pack_kernel(vol, cot, out, tmp):
    pair_rows(vol.at[0, 0], out.at[0:32], tmp)
    out[32:48] = cot[:, :, 0:128]
    out[48:64] = cot[:, :, 128:256]


def pack(volume, cot):
    return pl.pallas_call(
        pack_kernel,
        grid=(1,),
        out_shape=jax.ShapeDtypeStruct((64, 24, 128), BF16),
        in_specs=[
            pl.BlockSpec((1, 1, 32, 48, 64), lambda i: (0, 1, 0, 0, 0)),
            pl.BlockSpec((16, 24, 256), lambda i: (0, 0, 0)),
        ],
        out_specs=pl.BlockSpec((64, 24, 128), lambda i: (0, 0, 0)),
        scratch_shapes=[pltpu.VMEM((8, 48, 128), F32)],
        name="pack",
        cost_estimate=pl.CostEstimate(flops=0, bytes_accessed=2 << 20, transcendentals=0),
    )(volume, cot)


def split_rows(pairs, even, odd):
    for r in range(16):
        even[r, 0:24] = pairs[2 * r]
        odd[r + 1, 0:24] = pairs[2 * r + 1]


def window(even, odd, kr):
    rows = even[...] if kr == 1 else odd[kr // 2 : kr // 2 + 16]
    return rows.reshape(16 * PAD, 128)


def strided_terms(windows, w1):
    zeros = jnp.zeros((64, 128), BF16)

    def weights(kd, kr):
        left = jnp.concatenate([w1[kd, kr, 1], w1[kd, kr, 2]], axis=0)
        right = jnp.concatenate([zeros, w1[kd, kr, 0]], axis=0)
        return jnp.concatenate([left, right], axis=1)

    total = None
    for i in range(0, len(windows), 2):
        pair = windows[i : i + 2]
        x = jnp.concatenate([p[2] for p in pair], axis=1) if len(pair) == 2 else pair[0][2]
        w = jnp.concatenate([weights(p[0], p[1]) for p in pair], axis=0)
        term = dot(x, w, NN)
        total = term if total is None else total + term
    return total[:, 0:128] + roll_rows(total[:, 128:256], 1)


def own_group():
    lane_group = lax.broadcasted_iota(jnp.int32, (128, 256), 1) // 32
    return lane_group == lax.broadcasted_iota(jnp.int32, (128, 256), 0) // 16


def put_weights(w2, kd, wd):
    own = own_group()
    for kr in range(3):
        for kc in range(3):
            spread = jnp.concatenate([w2[kd * 9 + kr * 3 + kc]] * GROUPS, axis=0)
            wd[kr, kc * 128 : kc * 128 + 128] = jnp.where(own, spread, 0.0).astype(BF16)


def cot_window(cpad, kr):
    return cpad[2 - kr : 18 - kr].reshape(16 * PAD, 256)


def grouped_terms(cpad, wd):
    total = None
    for kr in range(3):
        term = dot(cot_window(cpad, kr), wd[kr], NT)
        total = term if total is None else total + term
    return total


def join_columns(total):
    return roll_rows(total[:, 0:128], -1) + total[:, 128:256] + roll_rows(total[:, 256:384], 1)


def early_kernel(vol, packed, cot, w1, w2, pre, gh, even, odd, tmp, pairs, cpad, wd):
    clear(even)
    clear(odd)
    clear(cpad)
    pair_rows(vol.at[0, 0], pairs, tmp)
    split_rows(pairs, even.at[0], odd.at[0])
    split_rows(packed, even.at[1], odd.at[1])
    cpad[1:17, 0:24] = cot[...]
    windows = []
    for kd in (1, 2):
        for kr in range(3):
            windows.append((kd, kr, window(even.at[kd - 1], odd.at[kd - 1], kr)))
    pre[...] = strided_terms(windows, w1)
    put_weights(w2, 1, wd)
    gh[...] = join_columns(grouped_terms(cpad, wd))


def early(volume, packed, cot, w1, w2):
    whole = lambda *shape: pl.BlockSpec(shape, lambda i: (0,) * len(shape))
    return pl.pallas_call(
        early_kernel,
        grid=(1,),
        out_shape=(
            jax.ShapeDtypeStruct((16 * PAD, 128), F32),
            jax.ShapeDtypeStruct((16 * PAD, 128), F32),
            jax.ShapeDtypeStruct((2, 16, PAD, 128), BF16),
            jax.ShapeDtypeStruct((2, 17, PAD, 128), BF16),
        ),
        in_specs=[
            whole(1, 1, 32, 48, 64),
            whole(64, 24, 128),
            whole(16, 24, 256),
            whole(3, 3, 3, 64, 128),
            whole(27, 16, 256),
        ],
        out_specs=(
            whole(16 * PAD, 128),
            whole(16 * PAD, 128),
            whole(2, 16, PAD, 128),
            whole(2, 17, PAD, 128),
        ),
        scratch_shapes=[
            pltpu.VMEM((8, 48, 128), F32),
            pltpu.VMEM((32, 24, 128), BF16),
            pltpu.VMEM((18, PAD, 256), BF16),
            pltpu.VMEM((3, 384, 256), BF16),
        ],
        name="early",
        cost_estimate=pl.CostEstimate(flops=1 << 30, bytes_accessed=2 << 20, transcendentals=0),
    )(volume, packed, cot, w1, w2)


def middle_kernel(
    core, got, cot, cot_hi, pre_part, gh_part, even12, odd12, w1, w2,
    gp_out, keep_out, send_out,
    even0, odd0, cpad, wd, hid, ups, hid_t, ups_t,
):
    cells = 16 * PAD
    clear(even0)
    clear(odd0)
    clear(cpad)
    split_rows(got, even0, odd0)
    cpad[0, 1:17, 0:24, 0:128] = got[32:48]
    cpad[0, 1:17, 0:24, 128:256] = got[48:64]
    cpad[1, 1:17, 0:24] = cot[...]
    cpad[2, 1:17, 0:24] = cot_hi[...]
    put_weights(w2, 0, wd.at[0])
    put_weights(w2, 2, wd.at[1])
    total = grouped_terms(cpad.at[2], wd.at[0]) + grouped_terms(cpad.at[0], wd.at[1])
    gh = (join_columns(total) + gh_part[...]).astype(BF16).astype(F32)
    windows = [[window(even0, odd0, kr) for kr in range(3)]]
    for p in range(2):
        windows.append([window(even12.at[p], odd12.at[p], kr) for kr in range(3)])
    pre = strided_terms([(0, kr, windows[0][kr]) for kr in range(3)], w1) + pre_part[...]
    inside = (lax.broadcasted_iota(jnp.int32, (cells, 128), 0) & (PAD - 1)) < 24
    pre = jnp.where(inside, pre, 0.0)
    s = jax.nn.sigmoid(pre)
    hidden = (pre * s).astype(BF16).astype(F32)
    grad = gh * s * (1.0 + pre * (1.0 - s))
    grad = jnp.where(inside, grad, 0.0).astype(BF16).astype(F32)
    ups[:, 0:128] = grad.astype(BF16)
    ups[:, 128:256] = roll_rows(grad, -1).astype(BF16)
    hid[:, 0:128] = roll_rows(hidden, 1).astype(BF16)
    hid[:, 128:256] = hidden.astype(BF16)
    hid[:, 256:384] = roll_rows(hidden, -1).astype(BF16)
    gp_out[...] = ups[:, 0:128].reshape(16, PAD, 128)[:, 0:24]
    ups_t[...] = ups[...].T
    hid_t[...] = hid[...].T
    first_core = core[0] == 0

    def put(tap, row, half0, half1):
        size = half0.shape[0]
        keep_out[tap, row : row + size] = jnp.where(first_core, half0, half1)
        send_out[tap, row : row + size] = jnp.where(first_core, half1, half0).astype(BF16)

    low = low_lanes((32, 128))
    flat = [windows[kd][kr] for kd in range(3) for kr in range(3)]
    for i in range(0, 9, 2):
        pair = flat[i : i + 2]
        x = jnp.concatenate(pair, axis=1) if len(pair) == 2 else pair[0]
        term = dot(ups_t[...], x, NN)
        for j in range(len(pair)):
            part = term[:, j * 128 : j * 128 + 128]
            tap = (i + j) * 3
            centre, side = [], []
            right = []
            for half in range(2):
                p = part[half * 64 : half * 64 + 32]
                q = part[half * 64 + 32 : half * 64 + 64]
                p1 = part[128 + half * 64 : 128 + half * 64 + 32]
                q1 = part[128 + half * 64 + 32 : 128 + half * 64 + 64]
                centre.append(jnp.where(low, p, half_turn(q)))
                right.append(jnp.where(low, half_turn(p), q))
                side.append(jnp.where(low, half_turn(p1), q1))
            put(tap, 0, *side)
            put(tap + 1, 0, *centre)
            put(tap + 2, 0, *right)
    own = own_group()
    for kd in range(3):
        for kr in range(3):
            term = dot(hid_t[...], cot_window(cpad.at[2 - kd], kr), NN)
            for kc in range(3):
                part = jnp.where(own, term[kc * 128 : kc * 128 + 128], 0.0)
                part = jnp.sum(part.reshape(GROUPS, 16, 256), axis=0)
                put((kd * 3 + kr) * 3 + kc, 32, part[:, 0:128], part[:, 128:256])
    keep_out[TAPS:32] = jnp.zeros((32 - TAPS, CHUNK, 128), F32)
    send_out[TAPS:32] = jnp.zeros((32 - TAPS, CHUNK, 128), BF16)


def middle(core, got, cot, cot_hi, pre, gh, even, odd, w1, w2):
    return pl.pallas_call(
        middle_kernel,
        out_shape=(
            jax.ShapeDtypeStruct((16, 24, 128), BF16),
            jax.ShapeDtypeStruct((32, CHUNK, 128), F32),
            jax.ShapeDtypeStruct((32, CHUNK, 128), BF16),
        ),
        in_specs=[pl.BlockSpec(memory_space=pltpu.SMEM)] + vmem(9),
        out_specs=tuple(vmem(3)),
        scratch_shapes=[
            pltpu.VMEM((16, PAD, 128), BF16),
            pltpu.VMEM((17, PAD, 128), BF16),
            pltpu.VMEM((3, 18, PAD, 256), BF16),
            pltpu.VMEM((2, 3, 384, 256), BF16),
            pltpu.VMEM((16 * PAD, 384), BF16),
            pltpu.VMEM((16 * PAD, 256), BF16),
            pltpu.VMEM((384, 16 * PAD), BF16),
            pltpu.VMEM((256, 16 * PAD), BF16),
        ],
        name="middle",
        cost_estimate=pl.CostEstimate(flops=3 << 30, bytes_accessed=4 << 20, transcendentals=1 << 16),
    )(core, got, cot, cot_hi, pre, gh, even, odd, w1, w2)


def input_kernel(gp, upper, w1, out, pad, tmp):
    h2, w = gp.shape[0], gp.shape[1]
    cells = h2 * PAD
    clear(pad)
    pad[0, 0:h2, 0:w] = gp[...]
    pad[1, 0:h2, 0:w] = upper[...]
    zeros = jnp.zeros((64, 128), BF16)
    for par in range(2):
        depth = ((0, 1),) if par == 0 else ((0, 2), (1, 0))
        for row_par in range(2):
            rows = ((0, 1),) if row_par == 0 else ((0, 2), (1, 0))
            total = None
            for plane, kd in depth:
                for start, kr in rows:
                    x = pad[plane, start : start + h2].reshape(cells, 128)
                    weights = jnp.concatenate(
                        [w1[kd, kr, 1], w1[kd, kr, 2], zeros, w1[kd, kr, 0]], axis=0
                    )
                    term = dot(x, weights, NT)
                    total = term if total is None else total + term
            both = total[:, 0:128] + roll_rows(total[:, 128:256], -1)
            turned = pltpu.roll(both, 64, 1)
            both = both.reshape(h2, PAD, 128)
            turned = turned.reshape(h2, PAD, 128)
            for r in range(h2):
                tmp[r % 2, pl.ds(0, w, 2), :] = both[r, 0:w]
                tmp[r % 2, pl.ds(1, w, 2), :] = turned[r, 0:w]
                out[par, 2 * r + row_par] = tmp[r % 2, :, 0:64].astype(BF16)


def input_backward(gp, upper, w1):
    return pl.pallas_call(
        input_kernel,
        out_shape=jax.ShapeDtypeStruct((2, 32, 48, 64), BF16),
        in_specs=vmem(3),
        out_specs=pl.BlockSpec(memory_space=pltpu.VMEM),
        scratch_shapes=[
            pltpu.VMEM((2, 17, PAD, 128), BF16),
            pltpu.VMEM((2, 48, 128), F32),
        ],
        name="input_backward",
        cost_estimate=pl.CostEstimate(flops=1 << 30, bytes_accessed=2 << 20, transcendentals=0),
    )(gp, upper, w1)


def finish_kernel(scale, blocks, out):
    total = jnp.sum(blocks[...], axis=0) * scale
    packed = total[0:32]
    flipped = packed.T
    turned = jnp.concatenate([flipped[0:64], flipped[64:128]], axis=1)
    top = jnp.concatenate([turned[0:32], turned[32:64]], axis=1)
    mine = jnp.concatenate([top, total[32:48]], axis=0).astype(BF16)
    out[...] = jnp.broadcast_to(mine[None], out.shape)


def finish(blocks, count, scale):
    return pl.pallas_call(
        functools.partial(finish_kernel, scale),
        out_shape=jax.ShapeDtypeStruct((count, CHUNK, 128), BF16),
        in_specs=vmem(1),
        out_specs=pl.BlockSpec(memory_space=pltpu.VMEM),
        name="finish",
        cost_estimate=pl.CostEstimate(flops=1 << 16, bytes_accessed=1 << 20, transcendentals=0),
    )(blocks)


def unpack_kernel(core, mine, other, first, second):
    first_core = core[0] == 0
    low = low_lanes((32, 128))
    for tap in range(TAPS):
        a = mine[tap].astype(F32)
        b = other[tap].astype(F32)
        half0 = jnp.where(first_core, a, b)
        half1 = jnp.where(first_core, b, a)
        top, bottom = half0[0:32], half1[0:32]
        first[tap, 0:32] = jnp.where(low, top, half_turn(bottom))
        first[tap, 32:64] = jnp.where(low, half_turn(top), bottom)
        second[tap, :, 0:128] = half0[32:48]
        second[tap, :, 128:256] = half1[32:48]


def unpack(core, mine, other):
    return pl.pallas_call(
        unpack_kernel,
        out_shape=(
            jax.ShapeDtypeStruct((TAPS, 64, 128), F32),
            jax.ShapeDtypeStruct((TAPS, 16, 256), F32),
        ),
        in_specs=[pl.BlockSpec(memory_space=pltpu.SMEM)] + vmem(2),
        out_specs=tuple(vmem(2)),
        name="unpack",
        cost_estimate=pl.CostEstimate(flops=0, bytes_accessed=3 << 20, transcendentals=0),
    )(core, mine, other)


def exchange(blocks, axes):
    return lax.all_to_all(blocks, axes, split_axis=0, concat_axis=0, tiled=True)


def swap_cores(array):
    return lax.ppermute(array, "core", [(0, 1), (1, 0)])


def on_device(volume, cotangent, w_first, w_second):
    plane = ("z", "x")
    line = ("yl", "yh")
    core = lax.axis_index("core").astype(jnp.int32).reshape(1)
    cot = cotangent[0, 0]
    w2 = w_second.reshape(TAPS, 16, 256)
    packed = pack(volume, cot)
    got = shifted(packed, 1)
    cot_after, _ = lax.optimization_barrier((cot, packed))
    cot_hi = shifted(cot_after, -1)
    pre, gh, even, odd = early(volume, packed, cot, w_first, w2)
    gp, keep, send = middle(core, got, cot, cot_hi, pre, gh, even, odd, w_first, w2)
    upper = shifted(gp, -1)
    half = (keep + swap_cores(send).astype(F32)).astype(BF16)
    parts = exchange(half, plane)
    parts, upper = lax.optimization_barrier((parts, upper))
    mine = jnp.sum(parts.astype(F32), axis=0)
    lines = lax.axis_size(line)
    blocks = exchange(jnp.broadcast_to(mine[None], (lines,) + mine.shape), line)
    count = lax.axis_size(SAMPLE_AXES) * lax.axis_size(DEPTH_AXES) * 16 * 24
    scale = float(count) ** (-0.5)
    own_half = exchange(finish(blocks, lax.axis_size(plane), scale), plane)
    grad_input = input_backward(gp, upper, w_first)
    first, second = unpack(core, own_half, swap_cores(own_half))
    return (grad_input[None], first.reshape(3, 3, 3, 64, 128), second.reshape(3, 3, 3, 16, 256))


def solution(mesh):
    fine = Mesh(mesh.devices.reshape(2, 2, 8, 4, 4), SAMPLE_AXES + DEPTH_AXES)
    split = P(SAMPLE_AXES, DEPTH_AXES, None, None, None)
    return jax.shard_map(
        on_device,
        mesh=fine,
        in_specs=(split, split, P(), P()),
        out_specs=(split, P(), P()),
        check_vma=False,
    )
```

time: 336 us -> 113 us (0.34)
  waiting for transfers between devices: 286 us -> 24.2 us
  blocking collectives: 0 us -> 29.8 us
  starting transfers between devices: 13.8 us -> 35.1 us
  between operations: 14.1 us -> 0.73 us
  Pallas kernels: 14.9 us -> 18.6 us
    psum x1 -> x0, waiting for transfers between devices: 275 us -> none  [on_device(): sum_first, sum_second = lax.psum((first, second), ('dp', 'space'))]
    all_to_all x0 -> x2, blocking collectives: none -> 29.8 us  [exchange(): return lax.all_to_all(blocks, axes, split_axis=0, concat_axis=0, tiled=True)]
    all_to_all x0 -> x1, starting transfers between devices: none -> 18.3 us  [exchange(): return lax.all_to_all(blocks, axes, split_axis=0, concat_axis=0, tiled=True)]
    all_to_all x0 -> x1, waiting for transfers between devices: none -> 7.31 us  [exchange(): return lax.all_to_all(blocks, axes, split_axis=0, concat_axis=0, tiled=True)]
    ppermute x4 -> x5, waiting for transfers between devices: 10.2 us -> 16.9 us  [the longest x3 15.4 us: shifted(): return lax.ppermute(array, DEPTH_AXES, pairs)]
    pallas_call x2 -> x4, Pallas kernels: 5.99 us -> 9.96 us  [the longest x1 3.43 us: early(): pl.pallas_call(early_kernel, grid=(1,), out_shape=(jax.ShapeDtypeStruct((...]
    ppermute x4 -> x5, starting transfers between devices: 13.7 us -> 16.7 us  [the longest x2 9.09 us: swap_cores(): return lax.ppermute(array, 'core', [(0, 1), (1, 0)])]
  transfers between devices with their start and end apart: 5 -> 6, of which waited for: 3 -> 4; matrix products, arithmetic and copies ran while one was open for 0% -> 0% of each run, Pallas kernels for 3% -> 6%
where the time goes in v4:
time: 113 us; the launch traced here: 112 us
  starting transfers between devices  35.1 us (31%)
  blocking collectives  29.8 us (26%)
  waiting for transfers between devices  24.2 us (21%)
  Pallas kernels  18.6 us (16%)
  other arithmetic  2.02 us (2%)
  local copies, waits for them, and re-layouts  1.6 us (1%)
    all_to_all x2, blocking collectives, exchange(): return lax.all_to_all(blocks, axes, split_axis=0, concat_axis=0, tiled=True)  29.8 us
    all_to_all x1, starting transfers between devices, exchange(): return lax.all_to_all(blocks, axes, split_axis=0, concat_axis=0, tiled=True)  18.3 us
    ppermute x3, waiting for transfers between devices, shifted(): return lax.ppermute(array, DEPTH_AXES, pairs)  15.4 us
    ppermute x2, starting transfers between devices, swap_cores(): return lax.ppermute(array, 'core', [(0, 1), (1, 0)])  9.09 us
    ppermute x3, starting transfers between devices, shifted(): return lax.ppermute(array, DEPTH_AXES, pairs)  7.63 us
    all_to_all x1, waiting for transfers between devices, exchange(): return lax.all_to_all(blocks, axes, split_axis=0, concat_axis=0, tiled=True)  7.31 us
    pallas_call x1, Pallas kernels, middle(): pl.pallas_call(middle_kernel, out_shape=(jax.ShapeDtypeStruct((16, 24, 12...  5.54 us
    pallas_call x1, Pallas kernels, early(): pl.pallas_call(early_kernel, grid=(1,), out_shape=(jax.ShapeDtypeStruct((...  3.43 us
  transfers between devices with their start and end apart: 6, of which 4 were waited for; matrix products, arithmetic and copies ran while one was open for 0% of the time, Pallas kernels for 6%

profile of v4, /device:TPU:1, one launch (start us, length us, event | category | flops | bytes accessed | tf_op | source)
XLA Modules:
  0.0 112.0 jit_solution(6271134636730085845)
XLA Ops:
  0.6 0.0 copy-start.2
  0.6 2.2 %pack.1.packed = bf16[64,24,128]{2,1,0:T(8,128)(2,1)} custom-call(bf16[1,2,32,48,64]{4,3,2,1,0:T(8,128)(2,1)} %vol.3, bf16[16,24,256]{2,1,0:T(8,128)(2,1)} %bitcast.6), custom_call_target="tpu_custom_call" | custom-call | bytes 2097152 | tf_op jit(solution)/shard_map/pack/pallas_call | solution.py:77
  2.9 5.0 %collective-permute-start = (bf16[64,24,128]{2,1,0:T(8,128)(2,1)}, bf16[64,24,128]{2,1,0:T(8,128)(2,1)S(1)}, u32[]{:S(2)}, u32[]{:S(2)}) collective-permute-start(bf16[64,24,128]{2,1,0:T(8,128)(2,1)} %pack.1.packed), channel_id=1, source_target_pairs={{0,1},{1,2},{2,3},{3,4},{4,5},{5,6},{6,7},{7,8},{8,9},{9,10},{10,1... | collective-permute-start | bytes 1179656 | tf_op jit(solution)/shard_map/ppermute | solution.py:36
  7.9 0.0 copy-done.2
  7.9 1.3 %collective-permute-start.1 = (bf16[16,24,256]{2,1,0:T(8,128)(2,1)S(1)}, bf16[16,24,256]{2,1,0:T(8,128)(2,1)S(1)}, u32[]{:S(2)}, u32[]{:S(2)}) collective-permute-start(bf16[16,24,256]{2,1,0:T(8,128)(2,1)S(1)} %bitcast.9), channel_id=1, source_target_pairs={{1,0},{2,1},{3,2},{4,3},{5,4},{6,5},{7,6},{8,7},{9,8},{10,9},{11,1... | collective-permute-start | bytes 589832 | tf_op jit(solution)/shard_map/ppermute | solution.py:36
  9.3 3.4 %early.1 = (f32[512,128]{1,0:T(8,128)}, f32[512,128]{1,0:T(8,128)}, bf16[2,16,32,128]{3,2,1,0:T(8,128)(2,1)}, bf16[2,17,32,128]{3,2,1,0:T(8,128)(2,1)}) custom-call(bf16[1,2,32,48,64]{4,3,2,1,0:T(8,128)(2,1)} %vol.3, bf16[64,24,128]{2,1,0:T(8,128)(2,1)} %pack.1.packed, bf16[16,24,256]{2,1,0:T(8,128)(2,1)} %bitcast.7, bf16[3,3,3,64,128]{4,3,2,1,0:T(8,128)(2,1)} %w1.5, ...), custom_call_target="tpu_custom_call" | custom-call | flops 1073741824 | bytes 2097152 | tf_op jit(solution)/shard_map/early/pallas_call | solution.py:169
  12.7 10.1 %collective-permute-done.1.cot_hi = bf16[16,24,256]{2,1,0:T(8,128)(2,1)S(1)} collective-permute-done((bf16[16,24,256]{2,1,0:T(8,128)(2,1)S(1)}, bf16[16,24,256]{2,1,0:T(8,128)(2,1)S(1)}, u32[]{:S(2)}, u32[]{:S(2)}) %collective-permute-start.1) | collective-permute-done | bytes 196640 | tf_op jit(solution)/shard_map/ppermute | solution.py:36
  22.8 0.0 copy-start.4
  22.8 0.0 collective-permute-done.got
  22.8 0.0 copy-start.3
  22.8 0.7 copy-done.4
  23.5 0.1 copy-done.3
  23.6 5.5 %middle.1 = (bf16[16,24,128]{2,1,0:T(8,128)(2,1)}, f32[32,48,128]{2,1,0:T(8,128)}, bf16[32,48,128]{2,1,0:T(8,128)(2,1)}) custom-call(s32[1]{0:T(128)} %bitcast.core, bf16[64,24,128]{2,1,0:T(8,128)(2,1)} %copy-done.3, bf16[16,24,256]{2,1,0:T(8,128)(2,1)} %bitcast.8, bf16[16,24,256]{2,1,0:T(8,128)(2,1)} %copy-done.4, f32[512,128]{1,0:T(8,128)} %get-tuple-element.16.pre_part, ...), custom_call_target="tpu_custom_call" | custom-call | flops 3221225472 | bytes 4194304 | tf_op jit(solution)/shard_map/middle/pallas_call | solution.py:280
  29.2 2.5 %collective-permute-start.2 = (bf16[32,48,128]{2,1,0:T(8,128)(2,1)}, bf16[32,48,128]{2,1,0:T(8,128)(2,1)S(1)}, u32[]{:S(2)}, u32[]{:S(2)}) collective-permute-start(bf16[32,48,128]{2,1,0:T(8,128)(2,1)} %get-tuple-element.22), channel_id=1, source_target_pairs={{0,128},{128,0},{1,129},{129,1},{2,130},{130,2},{3,131},{131,3},{4... | collective-permute-start | bytes 1179656 | tf_op jit(solution)/shard_map/ppermute | solution.py:404
  31.7 1.5 %collective-permute-done.2 = bf16[32,48,128]{2,1,0:T(8,128)(2,1)S(1)} collective-permute-done((bf16[32,48,128]{2,1,0:T(8,128)(2,1)}, bf16[32,48,128]{2,1,0:T(8,128)(2,1)S(1)}, u32[]{:S(2)}, u32[]{:S(2)}) %collective-permute-start.2) | collective-permute-done | bytes 393248 | tf_op jit(solution)/shard_map/ppermute | solution.py:404
  33.2 2.0 %add_convert_fusion = bf16[32,48,128]{2,1,0:T(8,128)(2,1)} fusion(f32[32,48,128]{2,1,0:T(8,128)} %get-tuple-element.21, bf16[32,48,128]{2,1,0:T(8,128)(2,1)S(1)} %collective-permute-done.2), kind=kLoop, calls=%fused_computation.1 | loop fusion | flops 589824 | bytes 1572864 | tf_op jit(solution)/shard_map/convert_element_type | solution.py:420
  35.2 0.0 copy-start.5
  35.2 18.3 %all-to-all-start = ((bf16[32,48,128]{2,1,0:T(8,128)(2,1)}), bf16[32,48,128]{2,1,0:T(8,128)(2,1)S(1)}, u32[]{:S(2)}, u32[]{:S(2)}) async-start(bf16[32,48,128]{2,1,0:T(8,128)(2,1)} %add_convert_fusion), calls=%async_computation | async-start | bytes 786432 | tf_op jit(solution)/shard_map/all_to_all | solution.py:400
  53.5 0.0 copy-done.5
  53.5 1.3 %collective-permute-start.3 = (bf16[16,24,128]{2,1,0:T(8,128)(2,1)S(1)}, bf16[16,24,128]{2,1,0:T(8,128)(2,1)S(1)}, u32[]{:S(2)}, u32[]{:S(2)}) collective-permute-start(bf16[16,24,128]{2,1,0:T(8,128)(2,1)S(1)} %copy-done.5), channel_id=1, source_target_pairs={{1,0},{2,1},{3,2},{4,3},{5,4},{6,5},{7,6},{8,7},{9,8},{10,9},{11,1... | collective-permute-start | bytes 294920 | tf_op jit(solution)/shard_map/ppermute | solution.py:36
  54.8 5.3 %collective-permute-done.3.upper = bf16[16,24,128]{2,1,0:T(8,128)(2,1)S(1)} collective-permute-done((bf16[16,24,128]{2,1,0:T(8,128)(2,1)S(1)}, bf16[16,24,128]{2,1,0:T(8,128)(2,1)S(1)}, u32[]{:S(2)}, u32[]{:S(2)}) %collective-permute-start.3) | collective-permute-done | bytes 98336 | tf_op jit(solution)/shard_map/ppermute | solution.py:36
  60.1 0.0 copy-start.6
  60.1 7.3 %all-to-all-done = bf16[32,48,128]{2,1,0:T(8,128)(2,1)S(1)} async-done(((bf16[32,48,128]{2,1,0:T(8,128)(2,1)}), bf16[32,48,128]{2,1,0:T(8,128)(2,1)S(1)}, u32[]{:S(2)}, u32[]{:S(2)}) %all-to-all-start) | async-done | bytes 393248 | tf_op jit(solution)/shard_map/all_to_all | solution.py:400
  67.4 0.1 convert_reduce_fusion
  67.5 0.0 copy-done.6
  67.5 13.1 %all_to_all.15.blocks = f32[8,48,128]{2,1,0:T(8,128)} all-to-all(f32[8,48,128]{2,1,0:T(8,128)S(1)} %broadcast_in_dim.10), channel_id=1, replica_groups=mesh['yl'=2,'core'=2,'z'=8,'x'=4,'yh'=4] {'yl','yh'}, dimensions={0} | all-to-all | bytes 393216 | tf_op jit(solution)/shard_map/all_to_all | solution.py:400
  80.6 1.9 %finish.1 = bf16[32,48,128]{2,1,0:T(8,128)(2,1)} custom-call(f32[8,48,128]{2,1,0:T(8,128)} %all_to_all.15.blocks), custom_call_target="tpu_custom_call" | custom-call | flops 65536 | bytes 1048576 | tf_op jit(solution)/shard_map/finish/pallas_call | solution.py:360
  82.6 16.6 %all_to_all.16.mine = bf16[32,48,128]{2,1,0:T(8,128)(2,1)S(1)} all-to-all(bf16[32,48,128]{2,1,0:T(8,128)(2,1)} %finish.1), channel_id=1, replica_groups=mesh['yl'=2,'core'=2,'z'=8,'x'=4,'yh'=4] {'z','x'}, dimensions={0} | all-to-all | bytes 786432 | tf_op jit(solution)/shard_map/all_to_all | solution.py:400
  99.2 0.0 copy-start
  99.2 6.6 %collective-permute-start.4 = (bf16[32,48,128]{2,1,0:T(8,128)(2,1)S(1)}, bf16[32,48,128]{2,1,0:T(8,128)(2,1)S(1)}, u32[]{:S(2)}, u32[]{:S(2)}) collective-permute-start(bf16[32,48,128]{2,1,0:T(8,128)(2,1)S(1)} %all_to_all.16.mine), channel_id=1, source_target_pairs={{0,128},{128,0},{1,129},{129,1},{2,130},{130,2},{3,131},{131,3},{4... | collective-permute-start | bytes 1179656 | tf_op jit(solution)/shard_map/ppermute | solution.py:404
  105.8 3.1 %input_backward.1 = bf16[2,32,48,64]{3,2,1,0:T(8,128)(2,1)} custom-call(bf16[16,24,128]{2,1,0:T(8,128)(2,1)} %get-tuple-element.20.gp, bf16[16,24,128]{2,1,0:T(8,128)(2,1)} %copy-done.6, bf16[3,3,3,64,128]{4,3,2,1,0:T(8,128)(2,1)} %w1.5), custom_call_target="tpu_custom_call" | custom-call | flops 1073741824 | bytes 2097152 | tf_op jit(solution)/shard_map/input_backward/pallas_call | solution.py:335
  108.9 0.0 copy-done
  108.9 0.0 collective-permute-done.4.other
  108.9 0.0 copy-start.1
  108.9 0.8 copy-done.1
  109.6 2.4 %unpack.1 = (f32[27,64,128]{2,1,0:T(8,128)}, f32[27,16,256]{2,1,0:T(8,128)}) custom-call(s32[1]{0:T(128)} %bitcast.core, bf16[32,48,128]{2,1,0:T(8,128)(2,1)} %copy-done, bf16[32,48,128]{2,1,0:T(8,128)(2,1)} %copy-done.1), custom_call_target="tpu_custom_call" | custom-call | bytes 3145728 | tf_op jit(solution)/shard_map/unpack/pallas_call | solution.py:386
  (1 shorter events, 0.0 us)
Async XLA Ops:
  0.6 7.3 %copy-start.2 = (bf16[1,1,16,24,256]{4,3,2,1,0:T(8,128)(2,1)S(1)}, bf16[1,1,16,24,256]{4,3,2,1,0:T(8,128)(2,1)}, u32[]{:S(2)}) copy-start(bf16[1,1,16,24,256]{4,3,2,1,0:T(8,128)(2,1)} %param.5) | copy-start | bytes 589828
  2.9 19.9 %collective-permute-start = (bf16[64,24,128]{2,1,0:T(8,128)(2,1)}, bf16[64,24,128]{2,1,0:T(8,128)(2,1)S(1)}, u32[]{:S(2)}, u32[]{:S(2)}) collective-permute-start(bf16[64,24,128]{2,1,0:T(8,128)(2,1)} %pack.1.packed), channel_id=1, source_target_pairs={{0,1},{1,2},{2,3},{3,4},{4,5},{5,6},{6,7},{7,8},{8,9},{9,10},{10,1... | collective-permute-start | bytes 1179656 | tf_op jit(solution)/shard_map/ppermute | solution.py:36
  7.9 14.9 %collective-permute-start.1 = (bf16[16,24,256]{2,1,0:T(8,128)(2,1)S(1)}, bf16[16,24,256]{2,1,0:T(8,128)(2,1)S(1)}, u32[]{:S(2)}, u32[]{:S(2)}) collective-permute-start(bf16[16,24,256]{2,1,0:T(8,128)(2,1)S(1)} %bitcast.9), channel_id=1, source_target_pairs={{1,0},{2,1},{3,2},{4,3},{5,4},{6,5},{7,6},{8,7},{9,8},{10,9},{11,1... | collective-permute-start | bytes 589832 | tf_op jit(solution)/shard_map/ppermute | solution.py:36
  22.8 0.7 copy-start.4
  22.8 0.8 copy-start.3
  29.2 4.0 %collective-permute-start.2 = (bf16[32,48,128]{2,1,0:T(8,128)(2,1)}, bf16[32,48,128]{2,1,0:T(8,128)(2,1)S(1)}, u32[]{:S(2)}, u32[]{:S(2)}) collective-permute-start(bf16[32,48,128]{2,1,0:T(8,128)(2,1)} %get-tuple-element.22), channel_id=1, source_target_pairs={{0,128},{128,0},{1,129},{129,1},{2,130},{130,2},{3,131},{131,3},{4... | collective-permute-start | bytes 1179656 | tf_op jit(solution)/shard_map/ppermute | solution.py:404
  35.2 18.4 %copy-start.5 = (bf16[16,24,128]{2,1,0:T(8,128)(2,1)S(1)}, bf16[16,24,128]{2,1,0:T(8,128)(2,1)}, u32[]{:S(2)}) copy-start(bf16[16,24,128]{2,1,0:T(8,128)(2,1)} %get-tuple-element.20.gp) | copy-start | bytes 294916
  35.2 32.2 %all-to-all-start = ((bf16[32,48,128]{2,1,0:T(8,128)(2,1)}), bf16[32,48,128]{2,1,0:T(8,128)(2,1)S(1)}, u32[]{:S(2)}, u32[]{:S(2)}) async-start(bf16[32,48,128]{2,1,0:T(8,128)(2,1)} %add_convert_fusion), calls=%async_computation | async-start | bytes 786432 | tf_op jit(solution)/shard_map/all_to_all | solution.py:400
  53.5 6.6 %collective-permute-start.3 = (bf16[16,24,128]{2,1,0:T(8,128)(2,1)S(1)}, bf16[16,24,128]{2,1,0:T(8,128)(2,1)S(1)}, u32[]{:S(2)}, u32[]{:S(2)}) collective-permute-start(bf16[16,24,128]{2,1,0:T(8,128)(2,1)S(1)} %copy-done.5), channel_id=1, source_target_pairs={{1,0},{2,1},{3,2},{4,3},{5,4},{6,5},{7,6},{8,7},{9,8},{10,9},{11,1... | collective-permute-start | bytes 294920 | tf_op jit(solution)/shard_map/ppermute | solution.py:36
  60.1 7.4 %copy-start.6 = (bf16[16,24,128]{2,1,0:T(8,128)(2,1)}, bf16[16,24,128]{2,1,0:T(8,128)(2,1)S(1)}, u32[]{:S(2)}) copy-start(bf16[16,24,128]{2,1,0:T(8,128)(2,1)S(1)} %collective-permute-done.3.upper) | copy-start | bytes 294916
  99.2 9.7 %copy-start = (bf16[32,48,128]{2,1,0:T(8,128)(2,1)}, bf16[32,48,128]{2,1,0:T(8,128)(2,1)S(1)}, u32[]{:S(2)}) copy-start(bf16[32,48,128]{2,1,0:T(8,128)(2,1)S(1)} %all_to_all.16.mine) | copy-start | bytes 1179652
  99.2 9.7 %collective-permute-start.4 = (bf16[32,48,128]{2,1,0:T(8,128)(2,1)S(1)}, bf16[32,48,128]{2,1,0:T(8,128)(2,1)S(1)}, u32[]{:S(2)}, u32[]{:S(2)}) collective-permute-start(bf16[32,48,128]{2,1,0:T(8,128)(2,1)S(1)} %all_to_all.16.mine), channel_id=1, source_target_pairs={{0,128},{128,0},{1,129},{129,1},{2,130},{130,2},{3,131},{131,3},{4... | collective-permute-start | bytes 1179656 | tf_op jit(solution)/shard_map/ppermute | solution.py:404
  108.9 0.8 copy-start.1

commit v5 on v4

--- a/solution.py
+++ b/solution.py
@@ -1,5 +1,3 @@
-import functools
-
 import jax
 import jax.numpy as jnp
 from jax import lax
@@ -68,31 +66,32 @@
 
 
 def pack_kernel(vol, cot, out, tmp):
-    pair_rows(vol.at[0, 0], out.at[0:32], tmp)
-    out[32:48] = cot[:, :, 0:128]
-    out[48:64] = cot[:, :, 128:256]
+    pair_rows(vol.at[0, 0], out.at[0, 0:8], tmp)
+    out[0, 8:12] = cot[:, :, 0:128]
+    out[0, 12:16] = cot[:, :, 128:256]
 
 
 def pack(volume, cot):
     return pl.pallas_call(
         pack_kernel,
-        grid=(1,),
-        out_shape=jax.ShapeDtypeStruct((64, 24, 128), BF16),
+        grid=(4,),
+        out_shape=jax.ShapeDtypeStruct((4, 16, 24, 128), BF16),
         in_specs=[
-            pl.BlockSpec((1, 1, 32, 48, 64), lambda i: (0, 1, 0, 0, 0)),
-            pl.BlockSpec((16, 24, 256), lambda i: (0, 0, 0)),
+            pl.BlockSpec((1, 1, 8, 48, 64), lambda i: (0, 1, i, 0, 0)),
+            pl.BlockSpec((4, 24, 256), lambda i: (i, 0, 0)),
         ],
-        out_specs=pl.BlockSpec((64, 24, 128), lambda i: (0, 0, 0)),
+        out_specs=pl.BlockSpec((1, 16, 24, 128), lambda i: (i, 0, 0, 0)),
         scratch_shapes=[pltpu.VMEM((8, 48, 128), F32)],
         name="pack",
+        compiler_params=pltpu.CompilerParams(vmem_limit_bytes=4 << 20),
         cost_estimate=pl.CostEstimate(flops=0, bytes_accessed=2 << 20, transcendentals=0),
     )(volume, cot)
 
 
-def split_rows(pairs, even, odd):
+def split_rows(packed, even, odd):
     for r in range(16):
-        even[r, 0:24] = pairs[2 * r]
-        odd[r + 1, 0:24] = pairs[2 * r + 1]
+        even[r, 0:24] = packed[r // 4, 2 * (r % 4)]
+        odd[r + 1, 0:24] = packed[r // 4, 2 * (r % 4) + 1]
 
 
 def window(even, odd, kr):
@@ -151,7 +150,8 @@
     clear(even)
     clear(odd)
     clear(cpad)
-    pair_rows(vol.at[0, 0], pairs, tmp)
+    for g in range(4):
+        pair_rows(vol.at[0, 0, 8 * g : 8 * g + 8], pairs.at[g], tmp)
     split_rows(pairs, even.at[0], odd.at[0])
     split_rows(packed, even.at[1], odd.at[1])
     cpad[1:17, 0:24] = cot[...]
@@ -177,7 +177,7 @@
         ),
         in_specs=[
             whole(1, 1, 32, 48, 64),
-            whole(64, 24, 128),
+            whole(4, 16, 24, 128),
             whole(16, 24, 256),
             whole(3, 3, 3, 64, 128),
             whole(27, 16, 256),
@@ -190,17 +190,18 @@
         ),
         scratch_shapes=[
             pltpu.VMEM((8, 48, 128), F32),
-            pltpu.VMEM((32, 24, 128), BF16),
+            pltpu.VMEM((4, 8, 24, 128), BF16),
             pltpu.VMEM((18, PAD, 256), BF16),
             pltpu.VMEM((3, 384, 256), BF16),
         ],
         name="early",
+        compiler_params=pltpu.CompilerParams(vmem_limit_bytes=12 << 20),
         cost_estimate=pl.CostEstimate(flops=1 << 30, bytes_accessed=2 << 20, transcendentals=0),
     )(volume, packed, cot, w1, w2)
 
 
 def middle_kernel(
-    core, got, cot, cot_hi, pre_part, gh_part, even12, odd12, w1, w2,
+    core, got, cot_hi, cot, pre_part, gh_part, even12, odd12, w1, w2,
     gp_out, keep_out, send_out,
     even0, odd0, cpad, wd, hid, ups, hid_t, ups_t,
 ):
@@ -208,13 +209,14 @@
     clear(even0)
     clear(odd0)
     clear(cpad)
-    split_rows(got, even0, odd0)
-    cpad[0, 1:17, 0:24, 0:128] = got[32:48]
-    cpad[0, 1:17, 0:24, 128:256] = got[48:64]
     cpad[1, 1:17, 0:24] = cot[...]
-    cpad[2, 1:17, 0:24] = cot_hi[...]
     put_weights(w2, 0, wd.at[0])
     put_weights(w2, 2, wd.at[1])
+    split_rows(got, even0, odd0)
+    for g in range(4):
+        cpad[0, 1 + 4 * g : 5 + 4 * g, 0:24, 0:128] = got[g, 8:12]
+        cpad[0, 1 + 4 * g : 5 + 4 * g, 0:24, 128:256] = got[g, 12:16]
+    cpad[2, 1:17, 0:24] = cot_hi[...]
     total = grouped_terms(cpad.at[2], wd.at[0]) + grouped_terms(cpad.at[0], wd.at[1])
     gh = (join_columns(total) + gh_part[...]).astype(BF16).astype(F32)
     windows = [[window(even0, odd0, kr) for kr in range(3)]]
@@ -239,7 +241,7 @@
 
     def put(tap, row, half0, half1):
         size = half0.shape[0]
-        keep_out[tap, row : row + size] = jnp.where(first_core, half0, half1)
+        keep_out[tap, row : row + size] = jnp.where(first_core, half0, half1).astype(BF16)
         send_out[tap, row : row + size] = jnp.where(first_core, half1, half0).astype(BF16)
 
     low = low_lanes((32, 128))
@@ -272,19 +274,20 @@
                 part = jnp.where(own, term[kc * 128 : kc * 128 + 128], 0.0)
                 part = jnp.sum(part.reshape(GROUPS, 16, 256), axis=0)
                 put((kd * 3 + kr) * 3 + kc, 32, part[:, 0:128], part[:, 128:256])
-    keep_out[TAPS:32] = jnp.zeros((32 - TAPS, CHUNK, 128), F32)
+    keep_out[TAPS:32] = jnp.zeros((32 - TAPS, CHUNK, 128), BF16)
     send_out[TAPS:32] = jnp.zeros((32 - TAPS, CHUNK, 128), BF16)
 
 
-def middle(core, got, cot, cot_hi, pre, gh, even, odd, w1, w2):
+def middle(core, got, cot_hi, cot, pre, gh, even, odd, w1, w2):
     return pl.pallas_call(
         middle_kernel,
         out_shape=(
             jax.ShapeDtypeStruct((16, 24, 128), BF16),
-            jax.ShapeDtypeStruct((32, CHUNK, 128), F32),
+            jax.ShapeDtypeStruct((32, CHUNK, 128), BF16),
             jax.ShapeDtypeStruct((32, CHUNK, 128), BF16),
         ),
-        in_specs=[pl.BlockSpec(memory_space=pltpu.SMEM)] + vmem(9),
+        in_specs=[pl.BlockSpec(memory_space=pltpu.SMEM)]
+        + vmem(9),
         out_specs=tuple(vmem(3)),
         scratch_shapes=[
             pltpu.VMEM((16, PAD, 128), BF16),
@@ -297,8 +300,9 @@
             pltpu.VMEM((256, 16 * PAD), BF16),
         ],
         name="middle",
+        compiler_params=pltpu.CompilerParams(vmem_limit_bytes=20 << 20),
         cost_estimate=pl.CostEstimate(flops=3 << 30, bytes_accessed=4 << 20, transcendentals=1 << 16),
-    )(core, got, cot, cot_hi, pre, gh, even, odd, w1, w2)
+    )(core, got, cot_hi, cot, pre, gh, even, odd, w1, w2)
 
 
 def input_kernel(gp, upper, w1, out, pad, tmp):
@@ -342,62 +346,71 @@
             pltpu.VMEM((2, 48, 128), F32),
         ],
         name="input_backward",
+        compiler_params=pltpu.CompilerParams(vmem_limit_bytes=10 << 20),
         cost_estimate=pl.CostEstimate(flops=1 << 30, bytes_accessed=2 << 20, transcendentals=0),
     )(gp, upper, w1)
-
-
-def finish_kernel(scale, blocks, out):
-    total = jnp.sum(blocks[...], axis=0) * scale
-    packed = total[0:32]
-    flipped = packed.T
-    turned = jnp.concatenate([flipped[0:64], flipped[64:128]], axis=1)
-    top = jnp.concatenate([turned[0:32], turned[32:64]], axis=1)
-    mine = jnp.concatenate([top, total[32:48]], axis=0).astype(BF16)
-    out[...] = jnp.broadcast_to(mine[None], out.shape)
-
-
-def finish(blocks, count, scale):
-    return pl.pallas_call(
-        functools.partial(finish_kernel, scale),
-        out_shape=jax.ShapeDtypeStruct((count, CHUNK, 128), BF16),
-        in_specs=vmem(1),
-        out_specs=pl.BlockSpec(memory_space=pltpu.VMEM),
-        name="finish",
-        cost_estimate=pl.CostEstimate(flops=1 << 16, bytes_accessed=1 << 20, transcendentals=0),
-    )(blocks)
 
 
 def unpack_kernel(core, mine, other, first, second):
     first_core = core[0] == 0
     low = low_lanes((32, 128))
-    for tap in range(TAPS):
+    halves = []
+    for tap in range(mine.shape[0]):
         a = mine[tap].astype(F32)
         b = other[tap].astype(F32)
         half0 = jnp.where(first_core, a, b)
         half1 = jnp.where(first_core, b, a)
-        top, bottom = half0[0:32], half1[0:32]
-        first[tap, 0:32] = jnp.where(low, top, half_turn(bottom))
-        first[tap, 32:64] = jnp.where(low, half_turn(top), bottom)
         second[tap, :, 0:128] = half0[32:48]
         second[tap, :, 128:256] = half1[32:48]
+        halves.append((half0[0:32], half1[0:32]))
+    for tap in range(0, mine.shape[0], 2):
+        last = min(tap + 1, mine.shape[0] - 1)
+        rows = []
+        for half in range(2):
+            a, b = halves[tap][half], halves[last][half]
+            rows.append(jnp.where(low, a, half_turn(b)))
+            rows.append(jnp.where(low, half_turn(a), b))
+        turned = jnp.concatenate(rows, axis=0).T
+        first[tap] = turned[0:64]
+        if last > tap:
+            first[last] = turned[64:128]
 
 
 def unpack(core, mine, other):
+    step = 9
+    halves = pl.BlockSpec((step, CHUNK, 128), lambda i: (i, 0, 0))
     return pl.pallas_call(
         unpack_kernel,
+        grid=(TAPS // step,),
         out_shape=(
             jax.ShapeDtypeStruct((TAPS, 64, 128), F32),
             jax.ShapeDtypeStruct((TAPS, 16, 256), F32),
         ),
-        in_specs=[pl.BlockSpec(memory_space=pltpu.SMEM)] + vmem(2),
-        out_specs=tuple(vmem(2)),
+        in_specs=[pl.BlockSpec(memory_space=pltpu.SMEM), halves, halves],
+        out_specs=(
+            pl.BlockSpec((step, 64, 128), lambda i: (i, 0, 0)),
+            pl.BlockSpec((step, 16, 256), lambda i: (i, 0, 0)),
+        ),
         name="unpack",
+        compiler_params=pltpu.CompilerParams(vmem_limit_bytes=8 << 20),
         cost_estimate=pl.CostEstimate(flops=0, bytes_accessed=3 << 20, transcendentals=0),
     )(core, mine, other)
 
 
 def exchange(blocks, axes):
     return lax.all_to_all(blocks, axes, split_axis=0, concat_axis=0, tiled=True)
+
+
+def repeated(block, axes):
+    return jnp.broadcast_to(block[None], (lax.axis_size(axes),) + block.shape)
+
+
+def added(a, b):
+    return (a.astype(F32) + b.astype(F32)).astype(BF16)
+
+
+def total(blocks):
+    return jnp.sum(blocks.astype(F32), axis=0)
 
 
 def swap_cores(array):
@@ -410,22 +423,21 @@
     core = lax.axis_index("core").astype(jnp.int32).reshape(1)
     cot = cotangent[0, 0]
     w2 = w_second.reshape(TAPS, 16, 256)
-    packed = pack(volume, cot)
+    packed = pack(pltpu.with_memory_space_constraint(volume, pltpu.HBM), cot)
     got = shifted(packed, 1)
     cot_after, _ = lax.optimization_barrier((cot, packed))
     cot_hi = shifted(cot_after, -1)
     pre, gh, even, odd = early(volume, packed, cot, w_first, w2)
-    gp, keep, send = middle(core, got, cot, cot_hi, pre, gh, even, odd, w_first, w2)
+    gp, keep, send = middle(core, got, cot_hi, cot, pre, gh, even, odd, w_first, w2)
     upper = shifted(gp, -1)
-    half = (keep + swap_cores(send).astype(F32)).astype(BF16)
-    parts = exchange(half, plane)
-    parts, upper = lax.optimization_barrier((parts, upper))
-    mine = jnp.sum(parts.astype(F32), axis=0)
-    lines = lax.axis_size(line)
-    blocks = exchange(jnp.broadcast_to(mine[None], (lines,) + mine.shape), line)
+    half = added(keep, swap_cores(send))
+    mine = total(exchange(half, plane)).astype(BF16)
+    blocks = exchange(repeated(mine, line), line)
     count = lax.axis_size(SAMPLE_AXES) * lax.axis_size(DEPTH_AXES) * 16 * 24
     scale = float(count) ** (-0.5)
-    own_half = exchange(finish(blocks, lax.axis_size(plane), scale), plane)
+    mine = (total(blocks) * scale).astype(BF16)
+    own_half = exchange(repeated(mine, plane), plane)
+    own_half, upper = lax.optimization_barrier((own_half, upper))
     grad_input = input_backward(gp, upper, w_first)
     first, second = unpack(core, own_half, swap_cores(own_half))
     return (grad_input[None], first.reshape(3, 3, 3, 64, 128), second.reshape(3, 3, 3, 16, 256))

time: 113 us -> 104 us (0.920)
  blocking collectives: 29.8 us -> 44.1 us
  starting transfers between devices: 35.1 us -> 22.3 us
  Pallas kernels: 18.6 us -> 11.8 us
  other arithmetic: 2.02 us -> 0.2 us
  waiting for transfers between devices: 24.2 us -> 22.4 us
    all_to_all x2, blocking collectives: 29.8 us -> 44.1 us  [exchange(): return lax.all_to_all(blocks, axes, split_axis=0, concat_axis=0, tiled=True)]
    all_to_all x1, starting transfers between devices: 18.3 us -> 4.98 us  [exchange(): return lax.all_to_all(blocks, axes, split_axis=0, concat_axis=0, tiled=True)]
    pallas_call x3 -> x2, Pallas kernels: 6.53 us -> 4.13 us  [the longest x1 2.24 us: pack(): pl.pallas_call(pack_kernel, grid=(4,), out_shape=jax.ShapeDtypeStruct((4,...]
    all_to_all x1, waiting for transfers between devices: 7.31 us -> 5.19 us  [exchange(): return lax.all_to_all(blocks, axes, split_axis=0, concat_axis=0, tiled=True)]
    convert_element_type x1 -> x2, other arithmetic: 1.96 us -> 0.11 us  [the longest x1 0.11 us: added(): return (a.astype(F32) + b.astype(F32)).astype(BF16)]
    pallas_call x1, Pallas kernels: 5.54 us -> 3.81 us  [middle(): pl.pallas_call(middle_kernel, out_shape=(jax.ShapeDtypeStruct((16, 24, 12...]
    pallas_call x1, Pallas kernels: 3.43 us -> 1.91 us  [early(): pl.pallas_call(early_kernel, grid=(1,), out_shape=(jax.ShapeDtypeStruct((...]
  transfers between devices with their start and end apart: 6 -> 6, of which waited for: 4 -> 4; matrix products, arithmetic and copies ran while one was open for 0% -> 0% of each run, Pallas kernels for 6% -> 4%
where the time goes in v5:
time: 104 us; the launch traced here: 103 us
  blocking collectives  44.1 us (42%)
  waiting for transfers between devices  22.4 us (22%)
  starting transfers between devices  22.3 us (21%)
  Pallas kernels  11.8 us (11%)
  local copies, waits for them, and re-layouts  1.76 us (2%)
    all_to_all x2, blocking collectives, exchange(): return lax.all_to_all(blocks, axes, split_axis=0, concat_axis=0, tiled=True)  44.1 us
    ppermute x3, waiting for transfers between devices, shifted(): return lax.ppermute(array, DEPTH_AXES, pairs)  15.9 us
    ppermute x2, starting transfers between devices, swap_cores(): return lax.ppermute(array, 'core', [(0, 1), (1, 0)])  9.72 us
    ppermute x3, starting transfers between devices, shifted(): return lax.ppermute(array, DEPTH_AXES, pairs)  7.64 us
    all_to_all x1, waiting for transfers between devices, exchange(): return lax.all_to_all(blocks, axes, split_axis=0, concat_axis=0, tiled=True)  5.19 us
    all_to_all x1, starting transfers between devices, exchange(): return lax.all_to_all(blocks, axes, split_axis=0, concat_axis=0, tiled=True)  4.98 us
    pallas_call x1, Pallas kernels, middle(): pl.pallas_call(middle_kernel, out_shape=(jax.ShapeDtypeStruct((16, 24, 12...  3.81 us
    pallas_call x1, Pallas kernels, pack(): pl.pallas_call(pack_kernel, grid=(4,), out_shape=jax.ShapeDtypeStruct((4,...  2.24 us
  transfers between devices with their start and end apart: 6, of which 4 were waited for; matrix products, arithmetic and copies ran while one was open for 0% of the time, Pallas kernels for 4%

profile of v5, /device:TPU:1, one launch (start us, length us, event | category | flops | bytes accessed | tf_op | source)
XLA Modules:
  0.0 103.3 jit_solution(10637007996694103098)
XLA Ops:
  0.6 0.0 copy-start
  0.6 0.0 copy-start.1
  0.6 2.2 %pack.1.packed = bf16[4,16,24,128]{3,2,1,0:T(8,128)(2,1)S(1)} custom-call(bf16[1,2,32,48,64]{4,3,2,1,0:T(8,128)(2,1)} %vol.3, bf16[16,24,256]{2,1,0:T(8,128)(2,1)} %bitcast.1.cot), custom_call_target="tpu_custom_call" | custom-call | bytes 2097152 | tf_op jit(solution)/shard_map/pack/pallas_call | solution.py:75
  2.9 5.1 %collective-permute-start = (bf16[4,16,24,128]{3,2,1,0:T(8,128)(2,1)S(1)}, bf16[4,16,24,128]{3,2,1,0:T(8,128)(2,1)S(1)}, u32[]{:S(2)}, u32[]{:S(2)}) collective-permute-start(bf16[4,16,24,128]{3,2,1,0:T(8,128)(2,1)S(1)} %pack.1.packed), channel_id=1, source_target_pairs={{0,1},{1,2},{2,3},{3,4},{4,5},{5,6},{6,7},{7,8},{8,9},{9,10},{10,1... | collective-permute-start | bytes 1179656 | tf_op jit(solution)/shard_map/ppermute | solution.py:34
  8.0 1.3 %collective-permute-start.1 = (bf16[16,24,256]{2,1,0:T(8,128)(2,1)}, bf16[16,24,256]{2,1,0:T(8,128)(2,1)S(1)}, u32[]{:S(2)}, u32[]{:S(2)}) collective-permute-start(bf16[16,24,256]{2,1,0:T(8,128)(2,1)} %bitcast.1.cot), channel_id=1, source_target_pairs={{1,0},{2,1},{3,2},{4,3},{5,4},{6,5},{7,6},{8,7},{9,8},{10,9},{11,1... | collective-permute-start | bytes 589832 | tf_op jit(solution)/shard_map/ppermute | solution.py:34
  9.3 0.0 copy-done
  9.3 0.0 copy-done.1
  9.3 0.0 copy-start.2
  9.3 0.9 copy-done.2
  10.2 0.0 copy-start.3
  10.2 1.9 %early.1 = (f32[512,128]{1,0:T(8,128)S(1)}, f32[512,128]{1,0:T(8,128)S(1)}, bf16[2,16,32,128]{3,2,1,0:T(8,128)(2,1)S(1)}, bf16[2,17,32,128]{3,2,1,0:T(8,128)(2,1)S(1)}) custom-call(bf16[1,2,32,48,64]{4,3,2,1,0:T(8,128)(2,1)S(1)} %copy-done, bf16[4,16,24,128]{3,2,1,0:T(8,128)(2,1)S(1)} %pack.1.packed, bf16[16,24,256]{2,1,0:T(8,128)(2,1)} %bitcast.1.cot, ...), custom_call_target="tpu_custom_call" | custom-call | flops 1073741824 | bytes 2097152 | tf_op jit(solution)/shard_map/early/pallas_call | solution.py:169
  12.1 10.9 %collective-permute-done.1.cot_hi = bf16[16,24,256]{2,1,0:T(8,128)(2,1)S(1)} collective-permute-done((bf16[16,24,256]{2,1,0:T(8,128)(2,1)}, bf16[16,24,256]{2,1,0:T(8,128)(2,1)S(1)}, u32[]{:S(2)}, u32[]{:S(2)}) %collective-permute-start.1) | collective-permute-done | bytes 196640 | tf_op jit(solution)/shard_map/ppermute | solution.py:34
  23.0 0.0 collective-permute-done.got
  23.0 0.0 copy-done.3
  23.0 3.8 %middle.1 = (bf16[16,24,128]{2,1,0:T(8,128)(2,1)S(1)}, bf16[32,48,128]{2,1,0:T(8,128)(2,1)S(1)}, bf16[32,48,128]{2,1,0:T(8,128)(2,1)S(1)}) custom-call(s32[1]{0:T(128)} %bitcast.core, bf16[4,16,24,128]{3,2,1,0:T(8,128)(2,1)S(1)} %collective-permute-done.got, bf16[16,24,256]{2,1,0:T(8,128)(2,1)S(1)} %collective-permute-done.1.cot_hi, ...), custom_call_target="tpu_custom_call" | custom-call | flops 3221225472 | bytes 4194304 | tf_op jit(solution)/shard_map/middle/pallas_call | solution.py:282
  26.9 2.5 %collective-permute-start.2 = (bf16[32,48,128]{2,1,0:T(8,128)(2,1)S(1)}, bf16[32,48,128]{2,1,0:T(8,128)(2,1)S(1)}, u32[]{:S(2)}, u32[]{:S(2)}) collective-permute-start(bf16[32,48,128]{2,1,0:T(8,128)(2,1)S(1)} %get-tuple-element.22), channel_id=1, source_target_pairs={{0,128},{128,0},{1,129},{129,1},{2,130},{130,2},{3,131},{131,3},{4... | collective-permute-start | bytes 1179656 | tf_op jit(solution)/shard_map/ppermute | solution.py:417
  29.4 1.3 %collective-permute-done.2 = bf16[32,48,128]{2,1,0:T(8,128)(2,1)S(1)} collective-permute-done((bf16[32,48,128]{2,1,0:T(8,128)(2,1)S(1)}, bf16[32,48,128]{2,1,0:T(8,128)(2,1)S(1)}, u32[]{:S(2)}, u32[]{:S(2)}) %collective-permute-start.2) | collective-permute-done | bytes 393248 | tf_op jit(solution)/shard_map/ppermute | solution.py:417
  30.7 0.1 add_convert_fusion
  30.8 31.5 %all_to_all.15 = bf16[32,48,128]{2,1,0:T(8,128)(2,1)S(1)} all-to-all(bf16[32,48,128]{2,1,0:T(8,128)(2,1)S(1)} %add_convert_fusion), channel_id=1, replica_groups=mesh['yl'=2,'core'=2,'z'=8,'x'=4,'yh'=4] {'z','x'}, dimensions={0} | all-to-all | bytes 786432 | tf_op jit(solution)/shard_map/all_to_all | solution.py:401
  62.4 0.1 reduce_sum.21
  62.4 12.5 %all_to_all.16 = bf16[8,48,128]{2,1,0:T(8,128)(2,1)S(1)} all-to-all(bf16[8,48,128]{2,1,0:T(8,128)(2,1)S(1)} %broadcast_in_dim.6), channel_id=1, replica_groups=mesh['yl'=2,'core'=2,'z'=8,'x'=4,'yh'=4] {'yl','yh'}, dimensions={0} | all-to-all | bytes 196608 | tf_op jit(solution)/shard_map/all_to_all | solution.py:401
  75.0 0.8 broadcast_in_dim.7
  75.8 5.0 %all-to-all-start.2 = ((bf16[32,48,128]{2,1,0:T(8,128)(2,1)}), bf16[32,48,128]{2,1,0:T(8,128)(2,1)S(1)}, u32[]{:S(2)}, u32[]{:S(2)}) async-start(bf16[32,48,128]{2,1,0:T(8,128)(2,1)} %broadcast_in_dim.7), calls=%async_computation.2 | async-start | bytes 786432 | tf_op jit(solution)/shard_map/all_to_all | solution.py:401
  80.8 1.3 %collective-permute-start.3 = (bf16[16,24,128]{2,1,0:T(8,128)(2,1)S(1)}, bf16[16,24,128]{2,1,0:T(8,128)(2,1)S(1)}, u32[]{:S(2)}, u32[]{:S(2)}) collective-permute-start(bf16[16,24,128]{2,1,0:T(8,128)(2,1)S(1)} %get-tuple-element.20.gp), channel_id=1, source_target_pairs={{1,0},{2,1},{3,2},{4,3},{5,4},{6,5},{7,6},{8,7},{9,8},{10,9},{11,1... | collective-permute-start | bytes 294920 | tf_op jit(solution)/shard_map/ppermute | solution.py:34
  82.1 5.0 %collective-permute-done.3.upper = bf16[16,24,128]{2,1,0:T(8,128)(2,1)S(1)} collective-permute-done((bf16[16,24,128]{2,1,0:T(8,128)(2,1)S(1)}, bf16[16,24,128]{2,1,0:T(8,128)(2,1)S(1)}, u32[]{:S(2)}, u32[]{:S(2)}) %collective-permute-start.3) | collective-permute-done | bytes 98336 | tf_op jit(solution)/shard_map/ppermute | solution.py:34
  87.1 5.2 %all-to-all-done.2.mine = bf16[32,48,128]{2,1,0:T(8,128)(2,1)S(1)} async-done(((bf16[32,48,128]{2,1,0:T(8,128)(2,1)}), bf16[32,48,128]{2,1,0:T(8,128)(2,1)S(1)}, u32[]{:S(2)}, u32[]{:S(2)}) %all-to-all-start.2) | async-done | bytes 393248 | tf_op jit(solution)/shard_map/all_to_all | solution.py:401
  92.3 7.2 %collective-permute-start.4 = (bf16[32,48,128]{2,1,0:T(8,128)(2,1)S(1)}, bf16[32,48,128]{2,1,0:T(8,128)(2,1)S(1)}, u32[]{:S(2)}, u32[]{:S(2)}) collective-permute-start(bf16[32,48,128]{2,1,0:T(8,128)(2,1)S(1)} %all-to-all-done.2.mine), channel_id=1, source_target_pairs={{0,128},{128,0},{1,129},{129,1},{2,130},{130,2},{3,131},{131,3},{4... | collective-permute-start | bytes 1179656 | tf_op jit(solution)/shard_map/ppermute | solution.py:417
  99.5 1.9 %input_backward.1 = bf16[2,32,48,64]{3,2,1,0:T(8,128)(2,1)} custom-call(bf16[16,24,128]{2,1,0:T(8,128)(2,1)S(1)} %get-tuple-element.20.gp, bf16[16,24,128]{2,1,0:T(8,128)(2,1)S(1)} %collective-permute-done.3.upper, bf16[3,3,3,64,128]{4,3,2,1,0:T(8,128)(2,1)S(1)} %copy-done.1), custom_call_target="tpu_custom_call" | custom-call | flops 1073741824 | bytes 2097152 | tf_op jit(solution)/shard_map/input_backward/pallas_call | solution.py:339
  101.4 0.0 collective-permute-done.4.other
  101.4 1.9 %unpack.1 = (f32[27,64,128]{2,1,0:T(8,128)}, f32[27,16,256]{2,1,0:T(8,128)}) custom-call(s32[1]{0:T(128)} %bitcast.core, bf16[32,48,128]{2,1,0:T(8,128)(2,1)S(1)} %all-to-all-done.2.mine, bf16[32,48,128]{2,1,0:T(8,128)(2,1)S(1)} %collective-permute-done.4.other), custom_call_target="tpu_custom_call" | custom-call | bytes 3145728 | tf_op jit(solution)/shard_map/unpack/pallas_call | solution.py:382
  (3 shorter events, 0.0 us)
Async XLA Ops:
  0.6 8.6 %copy-start = (bf16[1,2,32,48,64]{4,3,2,1,0:T(8,128)(2,1)S(1)}, bf16[1,2,32,48,64]{4,3,2,1,0:T(8,128)(2,1)}, u32[]{:S(2)}) copy-start(bf16[1,2,32,48,64]{4,3,2,1,0:T(8,128)(2,1)} %vol.3) | copy-start | bytes 1179652
  0.6 8.6 %copy-start.1 = (bf16[3,3,3,64,128]{4,3,2,1,0:T(8,128)(2,1)S(1)}, bf16[3,3,3,64,128]{4,3,2,1,0:T(8,128)(2,1)}, u32[]{:S(2)}) copy-start(bf16[3,3,3,64,128]{4,3,2,1,0:T(8,128)(2,1)} %w1.5) | copy-start | bytes 1327108
  2.9 20.1 %collective-permute-start = (bf16[4,16,24,128]{3,2,1,0:T(8,128)(2,1)S(1)}, bf16[4,16,24,128]{3,2,1,0:T(8,128)(2,1)S(1)}, u32[]{:S(2)}, u32[]{:S(2)}) collective-permute-start(bf16[4,16,24,128]{3,2,1,0:T(8,128)(2,1)S(1)} %pack.1.packed), channel_id=1, source_target_pairs={{0,1},{1,2},{2,3},{3,4},{4,5},{5,6},{6,7},{7,8},{8,9},{9,10},{10,1... | collective-permute-start | bytes 1179656 | tf_op jit(solution)/shard_map/ppermute | solution.py:34
  8.0 15.1 %collective-permute-start.1 = (bf16[16,24,256]{2,1,0:T(8,128)(2,1)}, bf16[16,24,256]{2,1,0:T(8,128)(2,1)S(1)}, u32[]{:S(2)}, u32[]{:S(2)}) collective-permute-start(bf16[16,24,256]{2,1,0:T(8,128)(2,1)} %bitcast.1.cot), channel_id=1, source_target_pairs={{1,0},{2,1},{3,2},{4,3},{5,4},{6,5},{7,6},{8,7},{9,8},{10,9},{11,1... | collective-permute-start | bytes 589832 | tf_op jit(solution)/shard_map/ppermute | solution.py:34
  9.3 0.9 copy-start.2
  10.2 12.8 %copy-start.3 = (bf16[3,3,3,16,256]{4,3,2,1,0:T(8,128)(2,1)S(1)}, bf16[3,3,3,16,256]{4,3,2,1,0:T(8,128)(2,1)}, u32[]{:S(2)}) copy-start(bf16[3,3,3,16,256]{4,3,2,1,0:T(8,128)(2,1)} %param.7) | copy-start | bytes 663556
  26.9 3.9 %collective-permute-start.2 = (bf16[32,48,128]{2,1,0:T(8,128)(2,1)S(1)}, bf16[32,48,128]{2,1,0:T(8,128)(2,1)S(1)}, u32[]{:S(2)}, u32[]{:S(2)}) collective-permute-start(bf16[32,48,128]{2,1,0:T(8,128)(2,1)S(1)} %get-tuple-element.22), channel_id=1, source_target_pairs={{0,128},{128,0},{1,129},{129,1},{2,130},{130,2},{3,131},{131,3},{4... | collective-permute-start | bytes 1179656 | tf_op jit(solution)/shard_map/ppermute | solution.py:417
  75.8 16.4 %all-to-all-start.2 = ((bf16[32,48,128]{2,1,0:T(8,128)(2,1)}), bf16[32,48,128]{2,1,0:T(8,128)(2,1)S(1)}, u32[]{:S(2)}, u32[]{:S(2)}) async-start(bf16[32,48,128]{2,1,0:T(8,128)(2,1)} %broadcast_in_dim.7), calls=%async_computation.2 | async-start | bytes 786432 | tf_op jit(solution)/shard_map/all_to_all | solution.py:401
  80.8 6.3 %collective-permute-start.3 = (bf16[16,24,128]{2,1,0:T(8,128)(2,1)S(1)}, bf16[16,24,128]{2,1,0:T(8,128)(2,1)S(1)}, u32[]{:S(2)}, u32[]{:S(2)}) collective-permute-start(bf16[16,24,128]{2,1,0:T(8,128)(2,1)S(1)} %get-tuple-element.20.gp), channel_id=1, source_target_pairs={{1,0},{2,1},{3,2},{4,3},{5,4},{6,5},{7,6},{8,7},{9,8},{10,9},{11,1... | collective-permute-start | bytes 294920 | tf_op jit(solution)/shard_map/ppermute | solution.py:34
  92.3 9.1 %collective-permute-start.4 = (bf16[32,48,128]{2,1,0:T(8,128)(2,1)S(1)}, bf16[32,48,128]{2,1,0:T(8,128)(2,1)S(1)}, u32[]{:S(2)}, u32[]{:S(2)}) collective-permute-start(bf16[32,48,128]{2,1,0:T(8,128)(2,1)S(1)} %all-to-all-done.2.mine), channel_id=1, source_target_pairs={{0,128},{128,0},{1,129},{129,1},{2,130},{130,2},{3,131},{131,3},{4... | collective-permute-start | bytes 1179656 | tf_op jit(solution)/shard_map/ppermute | solution.py:417

commit v6 on v5

--- a/solution.py
+++ b/solution.py
@@ -1,3 +1,5 @@
+import functools
+
 import jax
 import jax.numpy as jnp
 from jax import lax
@@ -146,7 +148,7 @@
     return roll_rows(total[:, 0:128], -1) + total[:, 128:256] + roll_rows(total[:, 256:384], 1)
 
 
-def early_kernel(vol, packed, cot, w1, w2, pre, gh, even, odd, tmp, pairs, cpad, wd):
+def early_kernel(vol, packed, cot, w1, w2, pre, gh, even, odd, wd02, tmp, pairs, cpad, wd):
     clear(even)
     clear(odd)
     clear(cpad)
@@ -162,6 +164,8 @@
     pre[...] = strided_terms(windows, w1)
     put_weights(w2, 1, wd)
     gh[...] = join_columns(grouped_terms(cpad, wd))
+    put_weights(w2, 0, wd02.at[0])
+    put_weights(w2, 2, wd02.at[1])
 
 
 def early(volume, packed, cot, w1, w2):
@@ -174,6 +178,7 @@
             jax.ShapeDtypeStruct((16 * PAD, 128), F32),
             jax.ShapeDtypeStruct((2, 16, PAD, 128), BF16),
             jax.ShapeDtypeStruct((2, 17, PAD, 128), BF16),
+            jax.ShapeDtypeStruct((2, 3, 384, 256), BF16),
         ),
         in_specs=[
             whole(1, 1, 32, 48, 64),
@@ -187,6 +192,7 @@
             whole(16 * PAD, 128),
             whole(2, 16, PAD, 128),
             whole(2, 17, PAD, 128),
+            whole(2, 3, 384, 256),
         ),
         scratch_shapes=[
             pltpu.VMEM((8, 48, 128), F32),
@@ -200,24 +206,43 @@
     )(volume, packed, cot, w1, w2)
 
 
+def upper_kernel(cot_hi, gh_part, wd, gh, cpad):
+    clear(cpad)
+    cpad[1:17, 0:24] = cot_hi[...]
+    gh[...] = gh_part[...] + join_columns(grouped_terms(cpad, wd.at[0]))
+
+
+def upper_share(cot_hi, gh, wd):
+    return pl.pallas_call(
+        upper_kernel,
+        out_shape=(
+            jax.ShapeDtypeStruct((16 * PAD, 128), F32),
+            jax.ShapeDtypeStruct((18, PAD, 256), BF16),
+        ),
+        in_specs=vmem(3),
+        out_specs=tuple(vmem(2)),
+        name="upper_share",
+        compiler_params=pltpu.CompilerParams(vmem_limit_bytes=8 << 20),
+        cost_estimate=pl.CostEstimate(flops=1 << 29, bytes_accessed=2 << 20, transcendentals=0),
+    )(cot_hi, gh, wd)
+
+
 def middle_kernel(
-    core, got, cot_hi, cot, pre_part, gh_part, even12, odd12, w1, w2,
+    core, got, cpad_hi, cot, pre_part, gh_part, even12, odd12, w1, wd,
     gp_out, keep_out, send_out,
-    even0, odd0, cpad, wd, hid, ups, hid_t, ups_t,
+    even0, odd0, cpad, hid, ups, hid_t, ups_t,
 ):
     cells = 16 * PAD
     clear(even0)
     clear(odd0)
     clear(cpad)
     cpad[1, 1:17, 0:24] = cot[...]
-    put_weights(w2, 0, wd.at[0])
-    put_weights(w2, 2, wd.at[1])
     split_rows(got, even0, odd0)
     for g in range(4):
         cpad[0, 1 + 4 * g : 5 + 4 * g, 0:24, 0:128] = got[g, 8:12]
         cpad[0, 1 + 4 * g : 5 + 4 * g, 0:24, 128:256] = got[g, 12:16]
-    cpad[2, 1:17, 0:24] = cot_hi[...]
-    total = grouped_terms(cpad.at[2], wd.at[0]) + grouped_terms(cpad.at[0], wd.at[1])
+    total = grouped_terms(cpad.at[0], wd.at[1])
+    planes = (cpad_hi, cpad.at[1], cpad.at[0])
     gh = (join_columns(total) + gh_part[...]).astype(BF16).astype(F32)
     windows = [[window(even0, odd0, kr) for kr in range(3)]]
     for p in range(2):
@@ -269,7 +294,7 @@
     own = own_group()
     for kd in range(3):
         for kr in range(3):
-            term = dot(hid_t[...], cot_window(cpad.at[2 - kd], kr), NN)
+            term = dot(hid_t[...], cot_window(planes[kd], kr), NN)
             for kc in range(3):
                 part = jnp.where(own, term[kc * 128 : kc * 128 + 128], 0.0)
                 part = jnp.sum(part.reshape(GROUPS, 16, 256), axis=0)
@@ -278,7 +303,7 @@
     send_out[TAPS:32] = jnp.zeros((32 - TAPS, CHUNK, 128), BF16)
 
 
-def middle(core, got, cot_hi, cot, pre, gh, even, odd, w1, w2):
+def middle(core, got, cpad_hi, cot, pre, gh, even, odd, w1, wd):
     return pl.pallas_call(
         middle_kernel,
         out_shape=(
@@ -292,8 +317,7 @@
         scratch_shapes=[
             pltpu.VMEM((16, PAD, 128), BF16),
             pltpu.VMEM((17, PAD, 128), BF16),
-            pltpu.VMEM((3, 18, PAD, 256), BF16),
-            pltpu.VMEM((2, 3, 384, 256), BF16),
+            pltpu.VMEM((2, 18, PAD, 256), BF16),
             pltpu.VMEM((16 * PAD, 384), BF16),
             pltpu.VMEM((16 * PAD, 256), BF16),
             pltpu.VMEM((384, 16 * PAD), BF16),
@@ -302,7 +326,7 @@
         name="middle",
         compiler_params=pltpu.CompilerParams(vmem_limit_bytes=20 << 20),
         cost_estimate=pl.CostEstimate(flops=3 << 30, bytes_accessed=4 << 20, transcendentals=1 << 16),
-    )(core, got, cot_hi, cot, pre, gh, even, odd, w1, w2)
+    )(core, got, cpad_hi, cot, pre, gh, even, odd, w1, wd)
 
 
 def input_kernel(gp, upper, w1, out, pad, tmp):
@@ -351,29 +375,41 @@
     )(gp, upper, w1)
 
 
+def finish_kernel(scale, blocks, out):
+    total = jnp.sum(blocks[...].astype(F32), axis=0) * scale
+    packed = total[0:32]
+    flipped = packed.T
+    turned = jnp.concatenate([flipped[0:64], flipped[64:128]], axis=1)
+    top = jnp.concatenate([turned[0:32], turned[32:64]], axis=1)
+    mine = jnp.concatenate([top, total[32:48]], axis=0).astype(BF16)
+    out[...] = jnp.broadcast_to(mine[None], out.shape)
+
+
+def finish(blocks, count, scale):
+    return pl.pallas_call(
+        functools.partial(finish_kernel, scale),
+        out_shape=jax.ShapeDtypeStruct((count, CHUNK, 128), BF16),
+        in_specs=vmem(1),
+        out_specs=pl.BlockSpec(memory_space=pltpu.VMEM),
+        name="finish",
+        compiler_params=pltpu.CompilerParams(vmem_limit_bytes=4 << 20),
+        cost_estimate=pl.CostEstimate(flops=1 << 16, bytes_accessed=1 << 20, transcendentals=0),
+    )(blocks)
+
+
 def unpack_kernel(core, mine, other, first, second):
     first_core = core[0] == 0
     low = low_lanes((32, 128))
-    halves = []
     for tap in range(mine.shape[0]):
         a = mine[tap].astype(F32)
         b = other[tap].astype(F32)
         half0 = jnp.where(first_core, a, b)
         half1 = jnp.where(first_core, b, a)
+        top, bottom = half0[0:32], half1[0:32]
+        first[tap, 0:32] = jnp.where(low, top, half_turn(bottom))
+        first[tap, 32:64] = jnp.where(low, half_turn(top), bottom)
         second[tap, :, 0:128] = half0[32:48]
         second[tap, :, 128:256] = half1[32:48]
-        halves.append((half0[0:32], half1[0:32]))
-    for tap in range(0, mine.shape[0], 2):
-        last = min(tap + 1, mine.shape[0] - 1)
-        rows = []
-        for half in range(2):
-            a, b = halves[tap][half], halves[last][half]
-            rows.append(jnp.where(low, a, half_turn(b)))
-            rows.append(jnp.where(low, half_turn(a), b))
-        turned = jnp.concatenate(rows, axis=0).T
-        first[tap] = turned[0:64]
-        if last > tap:
-            first[last] = turned[64:128]
 
 
 def unpack(core, mine, other):
@@ -427,16 +463,16 @@
     got = shifted(packed, 1)
     cot_after, _ = lax.optimization_barrier((cot, packed))
     cot_hi = shifted(cot_after, -1)
-    pre, gh, even, odd = early(volume, packed, cot, w_first, w2)
-    gp, keep, send = middle(core, got, cot_hi, cot, pre, gh, even, odd, w_first, w2)
+    pre, gh, even, odd, wd = early(volume, packed, cot, w_first, w2)
+    gh, cpad_hi = upper_share(cot_hi, gh, wd)
+    gp, keep, send = middle(core, got, cpad_hi, cot, pre, gh, even, odd, w_first, wd)
     upper = shifted(gp, -1)
     half = added(keep, swap_cores(send))
     mine = total(exchange(half, plane)).astype(BF16)
     blocks = exchange(repeated(mine, line), line)
     count = lax.axis_size(SAMPLE_AXES) * lax.axis_size(DEPTH_AXES) * 16 * 24
     scale = float(count) ** (-0.5)
-    mine = (total(blocks) * scale).astype(BF16)
-    own_half = exchange(repeated(mine, plane), plane)
+    own_half = exchange(finish(blocks, lax.axis_size(plane), scale), plane)
     own_half, upper = lax.optimization_barrier((own_half, upper))
     grad_input = input_backward(gp, upper, w_first)
     first, second = unpack(core, own_half, swap_cores(own_half))

time: 104 us -> 103 us (level)
    pallas_call x0 -> x2, Pallas kernels: none -> 1.61 us  [the longest x1 1.01 us: finish(): pl.pallas_call(functools.partial(finish_kernel, scale), out_shape=jax.Sha...]
where the time goes in v6:
time: 103 us
  blocking collectives  43.4 us (42%)
  starting transfers between devices  22.3 us (22%)
  waiting for transfers between devices  22.3 us (22%)
  Pallas kernels  12.8 us (12%)
    all_to_all x2, blocking collectives, exchange(): return lax.all_to_all(blocks, axes, split_axis=0, concat_axis=0, tiled=True)  43.4 us
    ppermute x3, waiting for transfers between devices, shifted(): return lax.ppermute(array, DEPTH_AXES, pairs)  15.8 us
    ppermute x2, starting transfers between devices, swap_cores(): return lax.ppermute(array, 'core', [(0, 1), (1, 0)])  9.7 us
    ppermute x3, starting transfers between devices, shifted(): return lax.ppermute(array, DEPTH_AXES, pairs)  7.64 us
    all_to_all x1, waiting for transfers between devices, exchange(): return lax.all_to_all(blocks, axes, split_axis=0, concat_axis=0, tiled=True)  5.19 us
    all_to_all x1, starting transfers between devices, exchange(): return lax.all_to_all(blocks, axes, split_axis=0, concat_axis=0, tiled=True)  4.98 us
    pallas_call x1, Pallas kernels, middle(): pl.pallas_call(middle_kernel, out_shape=(jax.ShapeDtypeStruct((16, 24, 12...  3.38 us
    pallas_call x1, Pallas kernels, pack(): pl.pallas_call(pack_kernel, grid=(4,), out_shape=jax.ShapeDtypeStruct((4,...  2.24 us
  transfers between devices with their start and end apart: 6, of which 4 were waited for; matrix products, arithmetic and copies ran while one was open for 0% of the time, Pallas kernels for 4%

profile of v6, /device:TPU:1, one launch (start us, length us, event | category | flops | bytes accessed | tf_op | source)
XLA Modules:
  0.0 102.8 jit_solution(17518692783315101196)
XLA Ops:
  0.6 0.0 copy-start
  0.6 0.0 copy-start.1
  0.6 2.2 %pack.1.packed = bf16[4,16,24,128]{3,2,1,0:T(8,128)(2,1)S(1)} custom-call(bf16[1,2,32,48,64]{4,3,2,1,0:T(8,128)(2,1)} %vol.3, bf16[16,24,256]{2,1,0:T(8,128)(2,1)} %bitcast.1.cot), custom_call_target="tpu_custom_call" | custom-call | bytes 2097152 | tf_op jit(solution)/shard_map/pack/pallas_call | solution.py:77
  2.9 5.1 %collective-permute-start = (bf16[4,16,24,128]{3,2,1,0:T(8,128)(2,1)S(1)}, bf16[4,16,24,128]{3,2,1,0:T(8,128)(2,1)S(1)}, u32[]{:S(2)}, u32[]{:S(2)}) collective-permute-start(bf16[4,16,24,128]{3,2,1,0:T(8,128)(2,1)S(1)} %pack.1.packed), channel_id=1, source_target_pairs={{0,1},{1,2},{2,3},{3,4},{4,5},{5,6},{6,7},{7,8},{8,9},{9,10},{10,1... | collective-permute-start | bytes 1179656 | tf_op jit(solution)/shard_map/ppermute | solution.py:36
  8.0 1.3 %collective-permute-start.1 = (bf16[16,24,256]{2,1,0:T(8,128)(2,1)}, bf16[16,24,256]{2,1,0:T(8,128)(2,1)S(1)}, u32[]{:S(2)}, u32[]{:S(2)}) collective-permute-start(bf16[16,24,256]{2,1,0:T(8,128)(2,1)} %bitcast.1.cot), channel_id=1, source_target_pairs={{1,0},{2,1},{3,2},{4,3},{5,4},{6,5},{7,6},{8,7},{9,8},{10,9},{11,1... | collective-permute-start | bytes 589832 | tf_op jit(solution)/shard_map/ppermute | solution.py:36
  9.3 0.0 copy-done
  9.3 0.0 copy-done.1
  9.3 0.0 copy-start.2
  9.3 0.9 copy-done.2
  10.2 2.0 %early.1 = (f32[512,128]{1,0:T(8,128)S(1)}, f32[512,128]{1,0:T(8,128)S(1)}, bf16[2,16,32,128]{3,2,1,0:T(8,128)(2,1)S(1)}, bf16[2,17,32,128]{3,2,1,0:T(8,128)(2,1)S(1)}, bf16[2,3,384,256]{3,2,1,0:T(8,128)(2,1)S(1)}) custom-call(bf16[1,2,32,48,64]{4,3,2,1,0:T(8,128)(2,1)S(1)} %copy-done, bf16[4,16,24,128]{3,2,1,0:T(8,128)(2,1)S(1)} %pack.1.packed, ...), custom_call_target="tpu_custom_call" | custom-call | flops 1073741824 | bytes 2097152 | tf_op jit(solution)/shard_map/early/pallas_call | solution.py:173
  12.2 10.8 %collective-permute-done.1.cot_hi = bf16[16,24,256]{2,1,0:T(8,128)(2,1)S(1)} collective-permute-done((bf16[16,24,256]{2,1,0:T(8,128)(2,1)}, bf16[16,24,256]{2,1,0:T(8,128)(2,1)S(1)}, u32[]{:S(2)}, u32[]{:S(2)}) %collective-permute-start.1) | collective-permute-done | bytes 196640 | tf_op jit(solution)/shard_map/ppermute | solution.py:36
  23.0 0.6 upper_share.1
  23.6 0.0 collective-permute-done.got
  23.7 3.4 %middle.1 = (bf16[16,24,128]{2,1,0:T(8,128)(2,1)S(1)}, bf16[32,48,128]{2,1,0:T(8,128)(2,1)S(1)}, bf16[32,48,128]{2,1,0:T(8,128)(2,1)S(1)}) custom-call(s32[1]{0:T(128)} %bitcast.core, bf16[4,16,24,128]{3,2,1,0:T(8,128)(2,1)S(1)} %collective-permute-done.got, bf16[18,32,256]{2,1,0:T(8,128)(2,1)S(1)} %get-tuple-element.21.cpad_hi, ...), custom_call_target="tpu_custom_call" | custom-call | flops 3221225472 | bytes 4194304 | tf_op jit(solution)/shard_map/middle/pallas_call | solution.py:307
  27.0 2.5 %collective-permute-start.2 = (bf16[32,48,128]{2,1,0:T(8,128)(2,1)S(1)}, bf16[32,48,128]{2,1,0:T(8,128)(2,1)S(1)}, u32[]{:S(2)}, u32[]{:S(2)}) collective-permute-start(bf16[32,48,128]{2,1,0:T(8,128)(2,1)S(1)} %get-tuple-element.28), channel_id=1, source_target_pairs={{0,128},{128,0},{1,129},{129,1},{2,130},{130,2},{3,131},{131,3},{4... | collective-permute-start | bytes 1179656 | tf_op jit(solution)/shard_map/ppermute | solution.py:453
  29.6 1.3 %collective-permute-done.2 = bf16[32,48,128]{2,1,0:T(8,128)(2,1)S(1)} collective-permute-done((bf16[32,48,128]{2,1,0:T(8,128)(2,1)S(1)}, bf16[32,48,128]{2,1,0:T(8,128)(2,1)S(1)}, u32[]{:S(2)}, u32[]{:S(2)}) %collective-permute-start.2) | collective-permute-done | bytes 393248 | tf_op jit(solution)/shard_map/ppermute | solution.py:453
  30.9 0.1 add_convert_fusion
  31.0 30.9 %all_to_all.15 = bf16[32,48,128]{2,1,0:T(8,128)(2,1)S(1)} all-to-all(bf16[32,48,128]{2,1,0:T(8,128)(2,1)S(1)} %add_convert_fusion), channel_id=1, replica_groups=mesh['yl'=2,'core'=2,'z'=8,'x'=4,'yh'=4] {'z','x'}, dimensions={0} | all-to-all | bytes 786432 | tf_op jit(solution)/shard_map/all_to_all | solution.py:437
  61.9 0.1 reduce_sum.12
  62.0 12.5 %all_to_all.16.blocks = bf16[8,48,128]{2,1,0:T(8,128)(2,1)S(1)} all-to-all(bf16[8,48,128]{2,1,0:T(8,128)(2,1)S(1)} %broadcast_in_dim.4), channel_id=1, replica_groups=mesh['yl'=2,'core'=2,'z'=8,'x'=4,'yh'=4] {'yl','yh'}, dimensions={0} | all-to-all | bytes 196608 | tf_op jit(solution)/shard_map/all_to_all | solution.py:437
  74.5 1.0 finish.1
  75.5 5.0 %all-to-all-start.2 = ((bf16[32,48,128]{2,1,0:T(8,128)(2,1)}), bf16[32,48,128]{2,1,0:T(8,128)(2,1)S(1)}, u32[]{:S(2)}, u32[]{:S(2)}) async-start(bf16[32,48,128]{2,1,0:T(8,128)(2,1)} %finish.1), calls=%async_computation.2 | async-start | bytes 786432 | tf_op jit(solution)/shard_map/all_to_all | solution.py:437
  80.5 1.3 %collective-permute-start.3 = (bf16[16,24,128]{2,1,0:T(8,128)(2,1)S(1)}, bf16[16,24,128]{2,1,0:T(8,128)(2,1)S(1)}, u32[]{:S(2)}, u32[]{:S(2)}) collective-permute-start(bf16[16,24,128]{2,1,0:T(8,128)(2,1)S(1)} %get-tuple-element.26.gp), channel_id=1, source_target_pairs={{1,0},{2,1},{3,2},{4,3},{5,4},{6,5},{7,6},{8,7},{9,8},{10,9},{11,1... | collective-permute-start | bytes 294920 | tf_op jit(solution)/shard_map/ppermute | solution.py:36
  81.8 5.0 %collective-permute-done.3.upper = bf16[16,24,128]{2,1,0:T(8,128)(2,1)S(1)} collective-permute-done((bf16[16,24,128]{2,1,0:T(8,128)(2,1)S(1)}, bf16[16,24,128]{2,1,0:T(8,128)(2,1)S(1)}, u32[]{:S(2)}, u32[]{:S(2)}) %collective-permute-start.3) | collective-permute-done | bytes 98336 | tf_op jit(solution)/shard_map/ppermute | solution.py:36
  86.8 5.2 %all-to-all-done.2.mine = bf16[32,48,128]{2,1,0:T(8,128)(2,1)S(1)} async-done(((bf16[32,48,128]{2,1,0:T(8,128)(2,1)}), bf16[32,48,128]{2,1,0:T(8,128)(2,1)S(1)}, u32[]{:S(2)}, u32[]{:S(2)}) %all-to-all-start.2) | async-done | bytes 393248 | tf_op jit(solution)/shard_map/all_to_all | solution.py:437
  92.0 7.2 %collective-permute-start.4 = (bf16[32,48,128]{2,1,0:T(8,128)(2,1)S(1)}, bf16[32,48,128]{2,1,0:T(8,128)(2,1)S(1)}, u32[]{:S(2)}, u32[]{:S(2)}) collective-permute-start(bf16[32,48,128]{2,1,0:T(8,128)(2,1)S(1)} %all-to-all-done.2.mine), channel_id=1, source_target_pairs={{0,128},{128,0},{1,129},{129,1},{2,130},{130,2},{3,131},{131,3},{4... | collective-permute-start | bytes 1179656 | tf_op jit(solution)/shard_map/ppermute | solution.py:453
  99.2 2.0 %input_backward.1 = bf16[2,32,48,64]{3,2,1,0:T(8,128)(2,1)} custom-call(bf16[16,24,128]{2,1,0:T(8,128)(2,1)S(1)} %get-tuple-element.26.gp, bf16[16,24,128]{2,1,0:T(8,128)(2,1)S(1)} %collective-permute-done.3.upper, bf16[3,3,3,64,128]{4,3,2,1,0:T(8,128)(2,1)S(1)} %copy-done.1), custom_call_target="tpu_custom_call" | custom-call | flops 1073741824 | bytes 2097152 | tf_op jit(solution)/shard_map/input_backward/pallas_call | solution.py:363
  101.1 0.0 collective-permute-done.4.other
  101.1 1.7 %unpack.1 = (f32[27,64,128]{2,1,0:T(8,128)}, f32[27,16,256]{2,1,0:T(8,128)}) custom-call(s32[1]{0:T(128)} %bitcast.core, bf16[32,48,128]{2,1,0:T(8,128)(2,1)S(1)} %all-to-all-done.2.mine, bf16[32,48,128]{2,1,0:T(8,128)(2,1)S(1)} %collective-permute-done.4.other), custom_call_target="tpu_custom_call" | custom-call | bytes 3145728 | tf_op jit(solution)/shard_map/unpack/pallas_call | solution.py:418
  (1 shorter events, 0.0 us)
Async XLA Ops:
  0.6 8.6 %copy-start = (bf16[1,2,32,48,64]{4,3,2,1,0:T(8,128)(2,1)S(1)}, bf16[1,2,32,48,64]{4,3,2,1,0:T(8,128)(2,1)}, u32[]{:S(2)}) copy-start(bf16[1,2,32,48,64]{4,3,2,1,0:T(8,128)(2,1)} %vol.3) | copy-start | bytes 1179652
  0.6 8.6 %copy-start.1 = (bf16[3,3,3,64,128]{4,3,2,1,0:T(8,128)(2,1)S(1)}, bf16[3,3,3,64,128]{4,3,2,1,0:T(8,128)(2,1)}, u32[]{:S(2)}) copy-start(bf16[3,3,3,64,128]{4,3,2,1,0:T(8,128)(2,1)} %w1.5) | copy-start | bytes 1327108
  2.9 20.7 %collective-permute-start = (bf16[4,16,24,128]{3,2,1,0:T(8,128)(2,1)S(1)}, bf16[4,16,24,128]{3,2,1,0:T(8,128)(2,1)S(1)}, u32[]{:S(2)}, u32[]{:S(2)}) collective-permute-start(bf16[4,16,24,128]{3,2,1,0:T(8,128)(2,1)S(1)} %pack.1.packed), channel_id=1, source_target_pairs={{0,1},{1,2},{2,3},{3,4},{4,5},{5,6},{6,7},{7,8},{8,9},{9,10},{10,1... | collective-permute-start | bytes 1179656 | tf_op jit(solution)/shard_map/ppermute | solution.py:36
  8.0 15.1 %collective-permute-start.1 = (bf16[16,24,256]{2,1,0:T(8,128)(2,1)}, bf16[16,24,256]{2,1,0:T(8,128)(2,1)S(1)}, u32[]{:S(2)}, u32[]{:S(2)}) collective-permute-start(bf16[16,24,256]{2,1,0:T(8,128)(2,1)} %bitcast.1.cot), channel_id=1, source_target_pairs={{1,0},{2,1},{3,2},{4,3},{5,4},{6,5},{7,6},{8,7},{9,8},{10,9},{11,1... | collective-permute-start | bytes 589832 | tf_op jit(solution)/shard_map/ppermute | solution.py:36
  9.3 0.9 copy-start.2
  27.0 3.9 %collective-permute-start.2 = (bf16[32,48,128]{2,1,0:T(8,128)(2,1)S(1)}, bf16[32,48,128]{2,1,0:T(8,128)(2,1)S(1)}, u32[]{:S(2)}, u32[]{:S(2)}) collective-permute-start(bf16[32,48,128]{2,1,0:T(8,128)(2,1)S(1)} %get-tuple-element.28), channel_id=1, source_target_pairs={{0,128},{128,0},{1,129},{129,1},{2,130},{130,2},{3,131},{131,3},{4... | collective-permute-start | bytes 1179656 | tf_op jit(solution)/shard_map/ppermute | solution.py:453
  75.5 16.4 %all-to-all-start.2 = ((bf16[32,48,128]{2,1,0:T(8,128)(2,1)}), bf16[32,48,128]{2,1,0:T(8,128)(2,1)S(1)}, u32[]{:S(2)}, u32[]{:S(2)}) async-start(bf16[32,48,128]{2,1,0:T(8,128)(2,1)} %finish.1), calls=%async_computation.2 | async-start | bytes 786432 | tf_op jit(solution)/shard_map/all_to_all | solution.py:437
  80.5 6.3 %collective-permute-start.3 = (bf16[16,24,128]{2,1,0:T(8,128)(2,1)S(1)}, bf16[16,24,128]{2,1,0:T(8,128)(2,1)S(1)}, u32[]{:S(2)}, u32[]{:S(2)}) collective-permute-start(bf16[16,24,128]{2,1,0:T(8,128)(2,1)S(1)} %get-tuple-element.26.gp), channel_id=1, source_target_pairs={{1,0},{2,1},{3,2},{4,3},{5,4},{6,5},{7,6},{8,7},{9,8},{10,9},{11,1... | collective-permute-start | bytes 294920 | tf_op jit(solution)/shard_map/ppermute | solution.py:36
  92.0 9.2 %collective-permute-start.4 = (bf16[32,48,128]{2,1,0:T(8,128)(2,1)S(1)}, bf16[32,48,128]{2,1,0:T(8,128)(2,1)S(1)}, u32[]{:S(2)}, u32[]{:S(2)}) collective-permute-start(bf16[32,48,128]{2,1,0:T(8,128)(2,1)S(1)} %all-to-all-done.2.mine), channel_id=1, source_target_pairs={{0,128},{128,0},{1,129},{129,1},{2,130},{130,2},{3,131},{131,3},{4... | collective-permute-start | bytes 1179656 | tf_op jit(solution)/shard_map/ppermute | solution.py:453

commit v7 on v6

--- a/solution.py
+++ b/solution.py
@@ -468,12 +468,12 @@
     gp, keep, send = middle(core, got, cpad_hi, cot, pre, gh, even, odd, w_first, wd)
     upper = shifted(gp, -1)
     half = added(keep, swap_cores(send))
-    mine = total(exchange(half, plane)).astype(BF16)
+    parts, upper = lax.optimization_barrier((exchange(half, plane), upper))
+    mine = total(parts).astype(BF16)
     blocks = exchange(repeated(mine, line), line)
     count = lax.axis_size(SAMPLE_AXES) * lax.axis_size(DEPTH_AXES) * 16 * 24
     scale = float(count) ** (-0.5)
     own_half = exchange(finish(blocks, lax.axis_size(plane), scale), plane)
-    own_half, upper = lax.optimization_barrier((own_half, upper))
     grad_input = input_backward(gp, upper, w_first)
     first, second = unpack(core, own_half, swap_cores(own_half))
     return (grad_input[None], first.reshape(3, 3, 3, 64, 128), second.reshape(3, 3, 3, 16, 256))

time: 103 us -> 103 us (level)
  blocking collectives: 43.4 us -> 28.8 us
  starting transfers between devices: 22.3 us -> 34.6 us
  waiting for transfers between devices: 22.3 us -> 24.7 us
    all_to_all x2, blocking collectives: 43.4 us -> 28.8 us  [exchange(): return lax.all_to_all(blocks, axes, split_axis=0, concat_axis=0, tiled=True)]
    all_to_all x1, starting transfers between devices: 4.98 us -> 17.2 us  [exchange(): return lax.all_to_all(blocks, axes, split_axis=0, concat_axis=0, tiled=True)]
    all_to_all x1, waiting for transfers between devices: 5.19 us -> 7.32 us  [exchange(): return lax.all_to_all(blocks, axes, split_axis=0, concat_axis=0, tiled=True)]
where the time goes in v7:
time: 103 us
  starting transfers between devices  34.6 us (34%)
  blocking collectives  28.8 us (28%)
  waiting for transfers between devices  24.7 us (24%)
  Pallas kernels  12.1 us (12%)
    all_to_all x2, blocking collectives, exchange(): return lax.all_to_all(blocks, axes, split_axis=0, concat_axis=0, tiled=True)  28.8 us
    all_to_all x1, starting transfers between devices, exchange(): return lax.all_to_all(blocks, axes, split_axis=0, concat_axis=0, tiled=True)  17.2 us
    ppermute x3, waiting for transfers between devices, shifted(): return lax.ppermute(array, DEPTH_AXES, pairs)  16.1 us
    ppermute x2, starting transfers between devices, swap_cores(): return lax.ppermute(array, 'core', [(0, 1), (1, 0)])  9.7 us
    ppermute x3, starting transfers between devices, shifted(): return lax.ppermute(array, DEPTH_AXES, pairs)  7.64 us
    all_to_all x1, waiting for transfers between devices, exchange(): return lax.all_to_all(blocks, axes, split_axis=0, concat_axis=0, tiled=True)  7.32 us
    pallas_call x1, Pallas kernels, middle(): pl.pallas_call(middle_kernel, out_shape=(jax.ShapeDtypeStruct((16, 24, 12...  3.38 us
    pallas_call x1, Pallas kernels, pack(): pl.pallas_call(pack_kernel, grid=(4,), out_shape=jax.ShapeDtypeStruct((4,...  2.24 us
  transfers between devices with their start and end apart: 6, of which 4 were waited for; matrix products, arithmetic and copies ran while one was open for 0% of the time, Pallas kernels for 4%

profile of v7, /device:TPU:1, one launch (start us, length us, event | category | flops | bytes accessed | tf_op | source)
XLA Modules:
  0.0 102.8 jit_solution(1048400864625815602)
XLA Ops:
  0.6 0.0 copy-start
  0.6 0.0 copy-start.1
  0.6 2.2 %pack.1.packed = bf16[4,16,24,128]{3,2,1,0:T(8,128)(2,1)S(1)} custom-call(bf16[1,2,32,48,64]{4,3,2,1,0:T(8,128)(2,1)} %vol.3, bf16[16,24,256]{2,1,0:T(8,128)(2,1)} %bitcast.1.cot), custom_call_target="tpu_custom_call" | custom-call | bytes 2097152 | tf_op jit(solution)/shard_map/pack/pallas_call | solution.py:77
  2.9 5.1 %collective-permute-start = (bf16[4,16,24,128]{3,2,1,0:T(8,128)(2,1)S(1)}, bf16[4,16,24,128]{3,2,1,0:T(8,128)(2,1)S(1)}, u32[]{:S(2)}, u32[]{:S(2)}) collective-permute-start(bf16[4,16,24,128]{3,2,1,0:T(8,128)(2,1)S(1)} %pack.1.packed), channel_id=1, source_target_pairs={{0,1},{1,2},{2,3},{3,4},{4,5},{5,6},{6,7},{7,8},{8,9},{9,10},{10,1... | collective-permute-start | bytes 1179656 | tf_op jit(solution)/shard_map/ppermute | solution.py:36
  8.0 1.3 %collective-permute-start.1 = (bf16[16,24,256]{2,1,0:T(8,128)(2,1)}, bf16[16,24,256]{2,1,0:T(8,128)(2,1)S(1)}, u32[]{:S(2)}, u32[]{:S(2)}) collective-permute-start(bf16[16,24,256]{2,1,0:T(8,128)(2,1)} %bitcast.1.cot), channel_id=1, source_target_pairs={{1,0},{2,1},{3,2},{4,3},{5,4},{6,5},{7,6},{8,7},{9,8},{10,9},{11,1... | collective-permute-start | bytes 589832 | tf_op jit(solution)/shard_map/ppermute | solution.py:36
  9.3 0.0 copy-done
  9.3 0.0 copy-done.1
  9.3 0.0 copy-start.2
  9.3 0.9 copy-done.2
  10.2 2.0 %early.1 = (f32[512,128]{1,0:T(8,128)S(1)}, f32[512,128]{1,0:T(8,128)S(1)}, bf16[2,16,32,128]{3,2,1,0:T(8,128)(2,1)S(1)}, bf16[2,17,32,128]{3,2,1,0:T(8,128)(2,1)S(1)}, bf16[2,3,384,256]{3,2,1,0:T(8,128)(2,1)S(1)}) custom-call(bf16[1,2,32,48,64]{4,3,2,1,0:T(8,128)(2,1)S(1)} %copy-done, bf16[4,16,24,128]{3,2,1,0:T(8,128)(2,1)S(1)} %pack.1.packed, ...), custom_call_target="tpu_custom_call" | custom-call | flops 1073741824 | bytes 2097152 | tf_op jit(solution)/shard_map/early/pallas_call | solution.py:173
  12.2 10.8 %collective-permute-done.1.cot_hi = bf16[16,24,256]{2,1,0:T(8,128)(2,1)S(1)} collective-permute-done((bf16[16,24,256]{2,1,0:T(8,128)(2,1)}, bf16[16,24,256]{2,1,0:T(8,128)(2,1)S(1)}, u32[]{:S(2)}, u32[]{:S(2)}) %collective-permute-start.1) | collective-permute-done | bytes 196640 | tf_op jit(solution)/shard_map/ppermute | solution.py:36
  23.0 0.6 upper_share.1
  23.6 0.0 collective-permute-done.got
  23.7 3.4 %middle.1 = (bf16[16,24,128]{2,1,0:T(8,128)(2,1)S(1)}, bf16[32,48,128]{2,1,0:T(8,128)(2,1)S(1)}, bf16[32,48,128]{2,1,0:T(8,128)(2,1)S(1)}) custom-call(s32[1]{0:T(128)} %bitcast.core, bf16[4,16,24,128]{3,2,1,0:T(8,128)(2,1)S(1)} %collective-permute-done.got, bf16[18,32,256]{2,1,0:T(8,128)(2,1)S(1)} %get-tuple-element.21.cpad_hi, ...), custom_call_target="tpu_custom_call" | custom-call | flops 3221225472 | bytes 4194304 | tf_op jit(solution)/shard_map/middle/pallas_call | solution.py:307
  27.0 2.5 %collective-permute-start.2 = (bf16[32,48,128]{2,1,0:T(8,128)(2,1)S(1)}, bf16[32,48,128]{2,1,0:T(8,128)(2,1)S(1)}, u32[]{:S(2)}, u32[]{:S(2)}) collective-permute-start(bf16[32,48,128]{2,1,0:T(8,128)(2,1)S(1)} %get-tuple-element.28), channel_id=1, source_target_pairs={{0,128},{128,0},{1,129},{129,1},{2,130},{130,2},{3,131},{131,3},{4... | collective-permute-start | bytes 1179656 | tf_op jit(solution)/shard_map/ppermute | solution.py:453
  29.6 1.3 %collective-permute-done.2 = bf16[32,48,128]{2,1,0:T(8,128)(2,1)S(1)} collective-permute-done((bf16[32,48,128]{2,1,0:T(8,128)(2,1)S(1)}, bf16[32,48,128]{2,1,0:T(8,128)(2,1)S(1)}, u32[]{:S(2)}, u32[]{:S(2)}) %collective-permute-start.2) | collective-permute-done | bytes 393248 | tf_op jit(solution)/shard_map/ppermute | solution.py:453
  30.9 0.9 add_convert_fusion
  31.8 17.2 %all-to-all-start = ((bf16[32,48,128]{2,1,0:T(8,128)(2,1)}), bf16[32,48,128]{2,1,0:T(8,128)(2,1)S(1)}, u32[]{:S(2)}, u32[]{:S(2)}) async-start(bf16[32,48,128]{2,1,0:T(8,128)(2,1)} %add_convert_fusion), calls=%async_computation | async-start | bytes 786432 | tf_op jit(solution)/shard_map/all_to_all | solution.py:437
  49.0 1.3 %collective-permute-start.3 = (bf16[16,24,128]{2,1,0:T(8,128)(2,1)S(1)}, bf16[16,24,128]{2,1,0:T(8,128)(2,1)S(1)}, u32[]{:S(2)}, u32[]{:S(2)}) collective-permute-start(bf16[16,24,128]{2,1,0:T(8,128)(2,1)S(1)} %get-tuple-element.26.gp), channel_id=1, source_target_pairs={{1,0},{2,1},{3,2},{4,3},{5,4},{6,5},{7,6},{8,7},{9,8},{10,9},{11,1... | collective-permute-start | bytes 294920 | tf_op jit(solution)/shard_map/ppermute | solution.py:36
  50.3 5.3 %collective-permute-done.3.upper = bf16[16,24,128]{2,1,0:T(8,128)(2,1)S(1)} collective-permute-done((bf16[16,24,128]{2,1,0:T(8,128)(2,1)S(1)}, bf16[16,24,128]{2,1,0:T(8,128)(2,1)S(1)}, u32[]{:S(2)}, u32[]{:S(2)}) %collective-permute-start.3) | collective-permute-done | bytes 98336 | tf_op jit(solution)/shard_map/ppermute | solution.py:36
  55.6 7.3 %all-to-all-done = bf16[32,48,128]{2,1,0:T(8,128)(2,1)S(1)} async-done(((bf16[32,48,128]{2,1,0:T(8,128)(2,1)}), bf16[32,48,128]{2,1,0:T(8,128)(2,1)S(1)}, u32[]{:S(2)}, u32[]{:S(2)}) %all-to-all-start) | async-done | bytes 393248 | tf_op jit(solution)/shard_map/all_to_all | solution.py:437
  62.9 0.1 reduce_sum.12
  63.0 12.5 %all_to_all.15.blocks = bf16[8,48,128]{2,1,0:T(8,128)(2,1)S(1)} all-to-all(bf16[8,48,128]{2,1,0:T(8,128)(2,1)S(1)} %broadcast_in_dim.10), channel_id=1, replica_groups=mesh['yl'=2,'core'=2,'z'=8,'x'=4,'yh'=4] {'yl','yh'}, dimensions={0} | all-to-all | bytes 196608 | tf_op jit(solution)/shard_map/all_to_all | solution.py:437
  75.5 0.3 finish.1
  75.8 16.2 %all_to_all.16.mine = bf16[32,48,128]{2,1,0:T(8,128)(2,1)S(1)} all-to-all(bf16[32,48,128]{2,1,0:T(8,128)(2,1)S(1)} %finish.1), channel_id=1, replica_groups=mesh['yl'=2,'core'=2,'z'=8,'x'=4,'yh'=4] {'z','x'}, dimensions={0} | all-to-all | bytes 786432 | tf_op jit(solution)/shard_map/all_to_all | solution.py:437
  92.0 7.2 %collective-permute-start.4 = (bf16[32,48,128]{2,1,0:T(8,128)(2,1)S(1)}, bf16[32,48,128]{2,1,0:T(8,128)(2,1)S(1)}, u32[]{:S(2)}, u32[]{:S(2)}) collective-permute-start(bf16[32,48,128]{2,1,0:T(8,128)(2,1)S(1)} %all_to_all.16.mine), channel_id=1, source_target_pairs={{0,128},{128,0},{1,129},{129,1},{2,130},{130,2},{3,131},{131,3},{4... | collective-permute-start | bytes 1179656 | tf_op jit(solution)/shard_map/ppermute | solution.py:453
  99.2 1.9 %input_backward.1 = bf16[2,32,48,64]{3,2,1,0:T(8,128)(2,1)} custom-call(bf16[16,24,128]{2,1,0:T(8,128)(2,1)S(1)} %get-tuple-element.26.gp, bf16[16,24,128]{2,1,0:T(8,128)(2,1)S(1)} %collective-permute-done.3.upper, bf16[3,3,3,64,128]{4,3,2,1,0:T(8,128)(2,1)S(1)} %copy-done.1), custom_call_target="tpu_custom_call" | custom-call | flops 1073741824 | bytes 2097152 | tf_op jit(solution)/shard_map/input_backward/pallas_call | solution.py:363
  101.2 0.0 collective-permute-done.4.other
  101.2 1.7 %unpack.1 = (f32[27,64,128]{2,1,0:T(8,128)}, f32[27,16,256]{2,1,0:T(8,128)}) custom-call(s32[1]{0:T(128)} %bitcast.core, bf16[32,48,128]{2,1,0:T(8,128)(2,1)S(1)} %all_to_all.16.mine, bf16[32,48,128]{2,1,0:T(8,128)(2,1)S(1)} %collective-permute-done.4.other), custom_call_target="tpu_custom_call" | custom-call | bytes 3145728 | tf_op jit(solution)/shard_map/unpack/pallas_call | solution.py:418
  (1 shorter events, 0.0 us)
Async XLA Ops:
  0.6 8.6 %copy-start = (bf16[1,2,32,48,64]{4,3,2,1,0:T(8,128)(2,1)S(1)}, bf16[1,2,32,48,64]{4,3,2,1,0:T(8,128)(2,1)}, u32[]{:S(2)}) copy-start(bf16[1,2,32,48,64]{4,3,2,1,0:T(8,128)(2,1)} %vol.3) | copy-start | bytes 1179652
  0.6 8.6 %copy-start.1 = (bf16[3,3,3,64,128]{4,3,2,1,0:T(8,128)(2,1)S(1)}, bf16[3,3,3,64,128]{4,3,2,1,0:T(8,128)(2,1)}, u32[]{:S(2)}) copy-start(bf16[3,3,3,64,128]{4,3,2,1,0:T(8,128)(2,1)} %w1.5) | copy-start | bytes 1327108
  2.9 20.7 %collective-permute-start = (bf16[4,16,24,128]{3,2,1,0:T(8,128)(2,1)S(1)}, bf16[4,16,24,128]{3,2,1,0:T(8,128)(2,1)S(1)}, u32[]{:S(2)}, u32[]{:S(2)}) collective-permute-start(bf16[4,16,24,128]{3,2,1,0:T(8,128)(2,1)S(1)} %pack.1.packed), channel_id=1, source_target_pairs={{0,1},{1,2},{2,3},{3,4},{4,5},{5,6},{6,7},{7,8},{8,9},{9,10},{10,1... | collective-permute-start | bytes 1179656 | tf_op jit(solution)/shard_map/ppermute | solution.py:36
  8.0 15.1 %collective-permute-start.1 = (bf16[16,24,256]{2,1,0:T(8,128)(2,1)}, bf16[16,24,256]{2,1,0:T(8,128)(2,1)S(1)}, u32[]{:S(2)}, u32[]{:S(2)}) collective-permute-start(bf16[16,24,256]{2,1,0:T(8,128)(2,1)} %bitcast.1.cot), channel_id=1, source_target_pairs={{1,0},{2,1},{3,2},{4,3},{5,4},{6,5},{7,6},{8,7},{9,8},{10,9},{11,1... | collective-permute-start | bytes 589832 | tf_op jit(solution)/shard_map/ppermute | solution.py:36
  9.3 0.9 copy-start.2
  27.0 3.9 %collective-permute-start.2 = (bf16[32,48,128]{2,1,0:T(8,128)(2,1)S(1)}, bf16[32,48,128]{2,1,0:T(8,128)(2,1)S(1)}, u32[]{:S(2)}, u32[]{:S(2)}) collective-permute-start(bf16[32,48,128]{2,1,0:T(8,128)(2,1)S(1)} %get-tuple-element.28), channel_id=1, source_target_pairs={{0,128},{128,0},{1,129},{129,1},{2,130},{130,2},{3,131},{131,3},{4... | collective-permute-start | bytes 1179656 | tf_op jit(solution)/shard_map/ppermute | solution.py:453
  31.8 31.1 %all-to-all-start = ((bf16[32,48,128]{2,1,0:T(8,128)(2,1)}), bf16[32,48,128]{2,1,0:T(8,128)(2,1)S(1)}, u32[]{:S(2)}, u32[]{:S(2)}) async-start(bf16[32,48,128]{2,1,0:T(8,128)(2,1)} %add_convert_fusion), calls=%async_computation | async-start | bytes 786432 | tf_op jit(solution)/shard_map/all_to_all | solution.py:437
  49.0 6.6 %collective-permute-start.3 = (bf16[16,24,128]{2,1,0:T(8,128)(2,1)S(1)}, bf16[16,24,128]{2,1,0:T(8,128)(2,1)S(1)}, u32[]{:S(2)}, u32[]{:S(2)}) collective-permute-start(bf16[16,24,128]{2,1,0:T(8,128)(2,1)S(1)} %get-tuple-element.26.gp), channel_id=1, source_target_pairs={{1,0},{2,1},{3,2},{4,3},{5,4},{6,5},{7,6},{8,7},{9,8},{10,9},{11,1... | collective-permute-start | bytes 294920 | tf_op jit(solution)/shard_map/ppermute | solution.py:36
  92.0 9.1 %collective-permute-start.4 = (bf16[32,48,128]{2,1,0:T(8,128)(2,1)S(1)}, bf16[32,48,128]{2,1,0:T(8,128)(2,1)S(1)}, u32[]{:S(2)}, u32[]{:S(2)}) collective-permute-start(bf16[32,48,128]{2,1,0:T(8,128)(2,1)S(1)} %all_to_all.16.mine), channel_id=1, source_target_pairs={{0,128},{128,0},{1,129},{129,1},{2,130},{130,2},{3,131},{131,3},{4... | collective-permute-start | bytes 1179656 | tf_op jit(solution)/shard_map/ppermute | solution.py:453

commit v8 on v7

--- a/solution.py
+++ b/solution.py
@@ -299,8 +299,6 @@
                 part = jnp.where(own, term[kc * 128 : kc * 128 + 128], 0.0)
                 part = jnp.sum(part.reshape(GROUPS, 16, 256), axis=0)
                 put((kd * 3 + kr) * 3 + kc, 32, part[:, 0:128], part[:, 128:256])
-    keep_out[TAPS:32] = jnp.zeros((32 - TAPS, CHUNK, 128), BF16)
-    send_out[TAPS:32] = jnp.zeros((32 - TAPS, CHUNK, 128), BF16)
 
 
 def middle(core, got, cpad_hi, cot, pre, gh, even, odd, w1, wd):
@@ -308,8 +306,8 @@
         middle_kernel,
         out_shape=(
             jax.ShapeDtypeStruct((16, 24, 128), BF16),
-            jax.ShapeDtypeStruct((32, CHUNK, 128), BF16),
-            jax.ShapeDtypeStruct((32, CHUNK, 128), BF16),
+            jax.ShapeDtypeStruct((TAPS, CHUNK, 128), BF16),
+            jax.ShapeDtypeStruct((TAPS, CHUNK, 128), BF16),
         ),
         in_specs=[pl.BlockSpec(memory_space=pltpu.SMEM)]
         + vmem(9),
@@ -413,7 +411,7 @@
 
 
 def unpack(core, mine, other):
-    step = 9
+    step = 3
     halves = pl.BlockSpec((step, CHUNK, 128), lambda i: (i, 0, 0))
     return pl.pallas_call(
         unpack_kernel,
@@ -467,7 +465,8 @@
     gh, cpad_hi = upper_share(cot_hi, gh, wd)
     gp, keep, send = middle(core, got, cpad_hi, cot, pre, gh, even, odd, w_first, wd)
     upper = shifted(gp, -1)
-    half = added(keep, swap_cores(send))
+    spare = lax.axis_size(plane) - TAPS
+    half = jnp.pad(added(keep, swap_cores(send)), ((0, spare), (0, 0), (0, 0)))
     parts, upper = lax.optimization_barrier((exchange(half, plane), upper))
     mine = total(parts).astype(BF16)
     blocks = exchange(repeated(mine, line), line)

time: 103 us -> 105 us (1.019)
  Pallas kernels: 12.1 us -> 14 us
    pallas_call x1, Pallas kernels: 1.67 us -> 3.64 us  [unpack(): pl.pallas_call(unpack_kernel, grid=(TAPS // step,), out_shape=(jax.ShapeD...]
where the time goes in v8:
time: 105 us
  starting transfers between devices  34.6 us (33%)
  blocking collectives  28.8 us (27%)
  waiting for transfers between devices  24.7 us (24%)
  Pallas kernels  14 us (13%)
  local copies, waits for them, and re-layouts  1.73 us (2%)
    all_to_all x2, blocking collectives, exchange(): return lax.all_to_all(blocks, axes, split_axis=0, concat_axis=0, tiled=True)  28.8 us
    all_to_all x1, starting transfers between devices, exchange(): return lax.all_to_all(blocks, axes, split_axis=0, concat_axis=0, tiled=True)  17.2 us
    ppermute x3, waiting for transfers between devices, shifted(): return lax.ppermute(array, DEPTH_AXES, pairs)  16.1 us
    ppermute x2, starting transfers between devices, swap_cores(): return lax.ppermute(array, 'core', [(0, 1), (1, 0)])  9.7 us
    ppermute x3, starting transfers between devices, shifted(): return lax.ppermute(array, DEPTH_AXES, pairs)  7.64 us
    all_to_all x1, waiting for transfers between devices, exchange(): return lax.all_to_all(blocks, axes, split_axis=0, concat_axis=0, tiled=True)  7.32 us
    pallas_call x1, Pallas kernels, unpack(): pl.pallas_call(unpack_kernel, grid=(TAPS // step,), out_shape=(jax.ShapeD...  3.64 us
    pallas_call x1, Pallas kernels, middle(): pl.pallas_call(middle_kernel, out_shape=(jax.ShapeDtypeStruct((16, 24, 12...  3.36 us
  transfers between devices with their start and end apart: 6, of which 4 were waited for; matrix products, arithmetic and copies ran while one was open for 0% of the time, Pallas kernels for 4%

profile of v8, /device:TPU:1, one launch (start us, length us, event | category | flops | bytes accessed | tf_op | source)
XLA Modules:
  0.0 104.7 jit_solution(11187824999193310935)
XLA Ops:
  0.6 0.0 copy-start
  0.6 0.0 copy-start.1
  0.6 2.2 %pack.1.packed = bf16[4,16,24,128]{3,2,1,0:T(8,128)(2,1)S(1)} custom-call(bf16[1,2,32,48,64]{4,3,2,1,0:T(8,128)(2,1)} %vol.3, bf16[16,24,256]{2,1,0:T(8,128)(2,1)} %bitcast.1.cot), custom_call_target="tpu_custom_call" | custom-call | bytes 2097152 | tf_op jit(solution)/shard_map/pack/pallas_call | solution.py:77
  2.9 5.1 %collective-permute-start = (bf16[4,16,24,128]{3,2,1,0:T(8,128)(2,1)S(1)}, bf16[4,16,24,128]{3,2,1,0:T(8,128)(2,1)S(1)}, u32[]{:S(2)}, u32[]{:S(2)}) collective-permute-start(bf16[4,16,24,128]{3,2,1,0:T(8,128)(2,1)S(1)} %pack.1.packed), channel_id=1, source_target_pairs={{0,1},{1,2},{2,3},{3,4},{4,5},{5,6},{6,7},{7,8},{8,9},{9,10},{10,1... | collective-permute-start | bytes 1179656 | tf_op jit(solution)/shard_map/ppermute | solution.py:36
  8.0 1.3 %collective-permute-start.1 = (bf16[16,24,256]{2,1,0:T(8,128)(2,1)}, bf16[16,24,256]{2,1,0:T(8,128)(2,1)S(1)}, u32[]{:S(2)}, u32[]{:S(2)}) collective-permute-start(bf16[16,24,256]{2,1,0:T(8,128)(2,1)} %bitcast.1.cot), channel_id=1, source_target_pairs={{1,0},{2,1},{3,2},{4,3},{5,4},{6,5},{7,6},{8,7},{9,8},{10,9},{11,1... | collective-permute-start | bytes 589832 | tf_op jit(solution)/shard_map/ppermute | solution.py:36
  9.3 0.0 copy-done
  9.3 0.0 copy-done.1
  9.3 0.0 copy-start.2
  9.3 0.9 copy-done.2
  10.2 2.0 %early.1 = (f32[512,128]{1,0:T(8,128)S(1)}, f32[512,128]{1,0:T(8,128)S(1)}, bf16[2,16,32,128]{3,2,1,0:T(8,128)(2,1)S(1)}, bf16[2,17,32,128]{3,2,1,0:T(8,128)(2,1)S(1)}, bf16[2,3,384,256]{3,2,1,0:T(8,128)(2,1)S(1)}) custom-call(bf16[1,2,32,48,64]{4,3,2,1,0:T(8,128)(2,1)S(1)} %copy-done, bf16[4,16,24,128]{3,2,1,0:T(8,128)(2,1)S(1)} %pack.1.packed, ...), custom_call_target="tpu_custom_call" | custom-call | flops 1073741824 | bytes 2097152 | tf_op jit(solution)/shard_map/early/pallas_call | solution.py:173
  12.2 10.8 %collective-permute-done.1.cot_hi = bf16[16,24,256]{2,1,0:T(8,128)(2,1)S(1)} collective-permute-done((bf16[16,24,256]{2,1,0:T(8,128)(2,1)}, bf16[16,24,256]{2,1,0:T(8,128)(2,1)S(1)}, u32[]{:S(2)}, u32[]{:S(2)}) %collective-permute-start.1) | collective-permute-done | bytes 196640 | tf_op jit(solution)/shard_map/ppermute | solution.py:36
  23.0 0.6 upper_share.1
  23.6 0.0 collective-permute-done.got
  23.7 3.4 %middle.1 = (bf16[16,24,128]{2,1,0:T(8,128)(2,1)S(1)}, bf16[27,48,128]{2,1,0:T(8,128)(2,1)S(1)}, bf16[27,48,128]{2,1,0:T(8,128)(2,1)S(1)}) custom-call(s32[1]{0:T(128)} %bitcast.core, bf16[4,16,24,128]{3,2,1,0:T(8,128)(2,1)S(1)} %collective-permute-done.got, bf16[18,32,256]{2,1,0:T(8,128)(2,1)S(1)} %get-tuple-element.21.cpad_hi, ...), custom_call_target="tpu_custom_call" | custom-call | flops 3221225472 | bytes 4194304 | tf_op jit(solution)/shard_map/middle/pallas_call | solution.py:305
  27.0 2.5 %collective-permute-start.2 = (bf16[27,48,128]{2,1,0:T(8,128)(2,1)S(1)}, bf16[27,48,128]{2,1,0:T(8,128)(2,1)S(1)}, u32[]{:S(2)}, u32[]{:S(2)}) collective-permute-start(bf16[27,48,128]{2,1,0:T(8,128)(2,1)S(1)} %get-tuple-element.28), channel_id=1, source_target_pairs={{0,128},{128,0},{1,129},{129,1},{2,130},{130,2},{3,131},{131,3},{4... | collective-permute-start | bytes 995336 | tf_op jit(solution)/shard_map/ppermute | solution.py:451
  29.5 1.2 %collective-permute-done.2 = bf16[27,48,128]{2,1,0:T(8,128)(2,1)S(1)} collective-permute-done((bf16[27,48,128]{2,1,0:T(8,128)(2,1)S(1)}, bf16[27,48,128]{2,1,0:T(8,128)(2,1)S(1)}, u32[]{:S(2)}, u32[]{:S(2)}) %collective-permute-start.2) | collective-permute-done | bytes 331808 | tf_op jit(solution)/shard_map/ppermute | solution.py:451
  30.8 0.1 add_convert_fusion
  30.9 0.8 pad.4
  31.7 17.2 %all-to-all-start = ((bf16[32,48,128]{2,1,0:T(8,128)(2,1)}), bf16[32,48,128]{2,1,0:T(8,128)(2,1)S(1)}, u32[]{:S(2)}, u32[]{:S(2)}) async-start(bf16[32,48,128]{2,1,0:T(8,128)(2,1)} %pad.4), calls=%async_computation | async-start | bytes 786432 | tf_op jit(solution)/shard_map/all_to_all | solution.py:435
  48.9 1.3 %collective-permute-start.3 = (bf16[16,24,128]{2,1,0:T(8,128)(2,1)S(1)}, bf16[16,24,128]{2,1,0:T(8,128)(2,1)S(1)}, u32[]{:S(2)}, u32[]{:S(2)}) collective-permute-start(bf16[16,24,128]{2,1,0:T(8,128)(2,1)S(1)} %get-tuple-element.26.gp), channel_id=1, source_target_pairs={{1,0},{2,1},{3,2},{4,3},{5,4},{6,5},{7,6},{8,7},{9,8},{10,9},{11,1... | collective-permute-start | bytes 294920 | tf_op jit(solution)/shard_map/ppermute | solution.py:36
  50.2 5.3 %collective-permute-done.3.upper = bf16[16,24,128]{2,1,0:T(8,128)(2,1)S(1)} collective-permute-done((bf16[16,24,128]{2,1,0:T(8,128)(2,1)S(1)}, bf16[16,24,128]{2,1,0:T(8,128)(2,1)S(1)}, u32[]{:S(2)}, u32[]{:S(2)}) %collective-permute-start.3) | collective-permute-done | bytes 98336 | tf_op jit(solution)/shard_map/ppermute | solution.py:36
  55.5 7.3 %all-to-all-done = bf16[32,48,128]{2,1,0:T(8,128)(2,1)S(1)} async-done(((bf16[32,48,128]{2,1,0:T(8,128)(2,1)}), bf16[32,48,128]{2,1,0:T(8,128)(2,1)S(1)}, u32[]{:S(2)}, u32[]{:S(2)}) %all-to-all-start) | async-done | bytes 393248 | tf_op jit(solution)/shard_map/all_to_all | solution.py:435
  62.8 0.1 reduce_sum.12
  62.9 12.5 %all_to_all.15.blocks = bf16[8,48,128]{2,1,0:T(8,128)(2,1)S(1)} all-to-all(bf16[8,48,128]{2,1,0:T(8,128)(2,1)S(1)} %broadcast_in_dim.10), channel_id=1, replica_groups=mesh['yl'=2,'core'=2,'z'=8,'x'=4,'yh'=4] {'yl','yh'}, dimensions={0} | all-to-all | bytes 196608 | tf_op jit(solution)/shard_map/all_to_all | solution.py:435
  75.4 0.3 finish.1
  75.7 16.2 %all_to_all.16.mine = bf16[32,48,128]{2,1,0:T(8,128)(2,1)S(1)} all-to-all(bf16[32,48,128]{2,1,0:T(8,128)(2,1)S(1)} %finish.1), channel_id=1, replica_groups=mesh['yl'=2,'core'=2,'z'=8,'x'=4,'yh'=4] {'z','x'}, dimensions={0} | all-to-all | bytes 786432 | tf_op jit(solution)/shard_map/all_to_all | solution.py:435
  91.9 7.2 %collective-permute-start.4 = (bf16[32,48,128]{2,1,0:T(8,128)(2,1)S(1)}, bf16[32,48,128]{2,1,0:T(8,128)(2,1)S(1)}, u32[]{:S(2)}, u32[]{:S(2)}) collective-permute-start(bf16[32,48,128]{2,1,0:T(8,128)(2,1)S(1)} %all_to_all.16.mine), channel_id=1, source_target_pairs={{0,128},{128,0},{1,129},{129,1},{2,130},{130,2},{3,131},{131,3},{4... | collective-permute-start | bytes 1179656 | tf_op jit(solution)/shard_map/ppermute | solution.py:451
  99.1 1.9 %input_backward.1 = bf16[2,32,48,64]{3,2,1,0:T(8,128)(2,1)} custom-call(bf16[16,24,128]{2,1,0:T(8,128)(2,1)S(1)} %get-tuple-element.26.gp, bf16[16,24,128]{2,1,0:T(8,128)(2,1)S(1)} %collective-permute-done.3.upper, bf16[3,3,3,64,128]{4,3,2,1,0:T(8,128)(2,1)S(1)} %copy-done.1), custom_call_target="tpu_custom_call" | custom-call | flops 1073741824 | bytes 2097152 | tf_op jit(solution)/shard_map/input_backward/pallas_call | solution.py:361
  101.1 0.0 collective-permute-done.4.other
  101.1 3.6 %unpack.1 = (f32[27,64,128]{2,1,0:T(8,128)}, f32[27,16,256]{2,1,0:T(8,128)}) custom-call(s32[1]{0:T(128)} %bitcast.core, bf16[32,48,128]{2,1,0:T(8,128)(2,1)S(1)} %all_to_all.16.mine, bf16[32,48,128]{2,1,0:T(8,128)(2,1)S(1)} %collective-permute-done.4.other), custom_call_target="tpu_custom_call" | custom-call | bytes 3145728 | tf_op jit(solution)/shard_map/unpack/pallas_call | solution.py:416
  (1 shorter events, 0.0 us)
Async XLA Ops:
  0.6 8.6 %copy-start = (bf16[1,2,32,48,64]{4,3,2,1,0:T(8,128)(2,1)S(1)}, bf16[1,2,32,48,64]{4,3,2,1,0:T(8,128)(2,1)}, u32[]{:S(2)}) copy-start(bf16[1,2,32,48,64]{4,3,2,1,0:T(8,128)(2,1)} %vol.3) | copy-start | bytes 1179652
  0.6 8.6 %copy-start.1 = (bf16[3,3,3,64,128]{4,3,2,1,0:T(8,128)(2,1)S(1)}, bf16[3,3,3,64,128]{4,3,2,1,0:T(8,128)(2,1)}, u32[]{:S(2)}) copy-start(bf16[3,3,3,64,128]{4,3,2,1,0:T(8,128)(2,1)} %w1.5) | copy-start | bytes 1327108
  2.9 20.7 %collective-permute-start = (bf16[4,16,24,128]{3,2,1,0:T(8,128)(2,1)S(1)}, bf16[4,16,24,128]{3,2,1,0:T(8,128)(2,1)S(1)}, u32[]{:S(2)}, u32[]{:S(2)}) collective-permute-start(bf16[4,16,24,128]{3,2,1,0:T(8,128)(2,1)S(1)} %pack.1.packed), channel_id=1, source_target_pairs={{0,1},{1,2},{2,3},{3,4},{4,5},{5,6},{6,7},{7,8},{8,9},{9,10},{10,1... | collective-permute-start | bytes 1179656 | tf_op jit(solution)/shard_map/ppermute | solution.py:36
  8.0 15.1 %collective-permute-start.1 = (bf16[16,24,256]{2,1,0:T(8,128)(2,1)}, bf16[16,24,256]{2,1,0:T(8,128)(2,1)S(1)}, u32[]{:S(2)}, u32[]{:S(2)}) collective-permute-start(bf16[16,24,256]{2,1,0:T(8,128)(2,1)} %bitcast.1.cot), channel_id=1, source_target_pairs={{1,0},{2,1},{3,2},{4,3},{5,4},{6,5},{7,6},{8,7},{9,8},{10,9},{11,1... | collective-permute-start | bytes 589832 | tf_op jit(solution)/shard_map/ppermute | solution.py:36
  9.3 0.9 copy-start.2
  27.0 3.8 %collective-permute-start.2 = (bf16[27,48,128]{2,1,0:T(8,128)(2,1)S(1)}, bf16[27,48,128]{2,1,0:T(8,128)(2,1)S(1)}, u32[]{:S(2)}, u32[]{:S(2)}) collective-permute-start(bf16[27,48,128]{2,1,0:T(8,128)(2,1)S(1)} %get-tuple-element.28), channel_id=1, source_target_pairs={{0,128},{128,0},{1,129},{129,1},{2,130},{130,2},{3,131},{131,3},{4... | collective-permute-start | bytes 995336 | tf_op jit(solution)/shard_map/ppermute | solution.py:451
  31.7 31.1 %all-to-all-start = ((bf16[32,48,128]{2,1,0:T(8,128)(2,1)}), bf16[32,48,128]{2,1,0:T(8,128)(2,1)S(1)}, u32[]{:S(2)}, u32[]{:S(2)}) async-start(bf16[32,48,128]{2,1,0:T(8,128)(2,1)} %pad.4), calls=%async_computation | async-start | bytes 786432 | tf_op jit(solution)/shard_map/all_to_all | solution.py:435
  48.9 6.6 %collective-permute-start.3 = (bf16[16,24,128]{2,1,0:T(8,128)(2,1)S(1)}, bf16[16,24,128]{2,1,0:T(8,128)(2,1)S(1)}, u32[]{:S(2)}, u32[]{:S(2)}) collective-permute-start(bf16[16,24,128]{2,1,0:T(8,128)(2,1)S(1)} %get-tuple-element.26.gp), channel_id=1, source_target_pairs={{1,0},{2,1},{3,2},{4,3},{5,4},{6,5},{7,6},{8,7},{9,8},{10,9},{11,1... | collective-permute-start | bytes 294920 | tf_op jit(solution)/shard_map/ppermute | solution.py:36
  91.9 9.1 %collective-permute-start.4 = (bf16[32,48,128]{2,1,0:T(8,128)(2,1)S(1)}, bf16[32,48,128]{2,1,0:T(8,128)(2,1)S(1)}, u32[]{:S(2)}, u32[]{:S(2)}) collective-permute-start(bf16[32,48,128]{2,1,0:T(8,128)(2,1)S(1)} %all_to_all.16.mine), channel_id=1, source_target_pairs={{0,128},{128,0},{1,129},{129,1},{2,130},{130,2},{3,131},{131,3},{4... | collective-permute-start | bytes 1179656 | tf_op jit(solution)/shard_map/ppermute | solution.py:451
